TPU v7x, 32 devices: a whole 2x2x4 slice. The times are simulated.
32 devices in a mesh: dp: 4 (over y, x), mp: 8 (over z, core).
Axes of the slice: x: 2, y: 2, z: 4, core: 2. Of those that a mesh axis runs over, the one named last changes fastest.
Arguments:
- tokens: bfloat16 [512, 6144], P(('dp', 'mp')), may hold values from -6 to 6
- norm_gain: float32 [6144], replicated, may hold values from 0.5 to 1.5
- up_weight: bfloat16 [6144, 16384], P(None, 'mp'), may hold values from -0.078125 to 0.078125
- down_weight: bfloat16 [16384, 6144], P('mp'), may hold values from -0.046875 to 0.046875
- out_grad: bfloat16 [512, 6144], P(('dp', 'mp')), may hold values from -6 to 6
Outputs:
- input_grad: bfloat16 [512, 6144], P(('dp', 'mp'))
- up_grad: bfloat16 [6144, 16384], P('dp', 'mp')
- down_grad: bfloat16 [16384, 6144], P('mp', 'dp')
- gain_grad: float32 [6144], replicated
All inputs are finite; a program needn't handle non-finite values.
Results may differ from a plain program's by a relative error of at most 0.018.
Values may be sent and summed in bfloat16 or wider, within the bound.
No kernel may reach another device: no remote copies, remote signals or barrier semaphores. Data moves between devices by JAX's collectives and lax.ppermute only.
A program may use at most 192 MiB of HBM per device.

v0:
```python
import math

import jax
import jax.numpy as jnp
from jax import lax
from jax.sharding import PartitionSpec as P


def gelu_value(preact):
    return 0.5 * preact * (1.0 + lax.erf(preact * 0.7071067811865476))


def gelu_slope(preact):
    return (
        0.5 * (1.0 + lax.erf(preact * 0.7071067811865476))
        + preact * jnp.exp(-0.5 * preact * preact) * 0.3989422804014327
    )


def swap_perm(size, mask):
    return [(i, i ^ mask) for i in range(size)]


def ring_perm(size, shift):
    chips = size // 2
    order = list(range(0, chips, 2)) + list(range(1, chips, 2))[::-1]
    moved = {order[k]: order[(k + shift) % chips] for k in range(chips)}
    return [(2 * c + core, 2 * moved[c] + core) for c in range(chips) for core in range(2)]


def contract(a, b, dims):
    return lax.dot_general(a, b, (dims, ((), ())), preferred_element_type=jnp.float32)


def layer(tokens, norm_gain, up_weight, down_weight, out_grad):
    n_dp, n_mp = lax.axis_size("dp"), lax.axis_size("mp")
    chips = n_mp // 2
    rows, width = tokens.shape
    cols = width // n_dp
    me = lax.axis_index("dp")
    factor = 1.0 / math.sqrt(rows * n_mp * n_dp)

    def along_ring(array, shift=1):
        return lax.ppermute(array, "mp", ring_perm(n_mp, shift))

    def across(array):
        return lax.ppermute(array, "mp", swap_perm(n_mp, 1))

    def replica(array, mask):
        return lax.ppermute(array, "dp", swap_perm(n_dp, mask))

    def spread(own):
        pieces = [own]
        for _ in range(1, chips):
            pieces.append(along_ring(pieces[-1]))
        return pieces, [across(p) for p in pieces]

    def replicas(own, low):
        out = [own]
        for k in range(1, n_dp):
            bit = (k & -k) if low else 1 << (k.bit_length() - 1)
            out.append(replica(out[k ^ bit], bit))
        return out

    values = tokens.astype(jnp.float32)
    centered = values - jnp.mean(values, axis=1, keepdims=True)
    inv_std = lax.rsqrt(jnp.mean(centered * centered, axis=1, keepdims=True) + 1e-06)
    x_hat = centered * inv_std
    normed = (x_hat * norm_gain).astype(jnp.bfloat16)

    cotan_mine, cotan_other = spread(out_grad)
    normed_mine, normed_other = spread(normed)
    normed_all = jnp.concatenate(normed_mine + normed_other, axis=0)
    cotan_all = jnp.concatenate(cotan_mine + cotan_other, axis=0)

    def block_of(array, k):
        return lax.dynamic_slice_in_dim(array, (me ^ k) * cols, cols, axis=1)

    def column_shards(k):
        both = jnp.stack([block_of(normed, k), block_of(out_grad, k)])
        return replica(both, k) if k else both

    shard_list = [column_shards(k) for k in range(n_dp)]
    shard = jnp.stack(shard_list)
    shards_mine, shards_other = spread(shard)
    columns = jnp.stack([jnp.stack(shards_mine), jnp.stack(shards_other)])
    columns = columns.transpose(3, 2, 0, 1, 4, 5).reshape(2, -1, cols)

    preact = contract(normed_all, up_weight, ((1,), (0,)))
    hidden = gelu_value(preact).astype(jnp.bfloat16)
    hid_grad = contract(cotan_all, down_weight, ((1,), (1,)))
    pre_grad = (hid_grad * gelu_slope(preact)).astype(jnp.bfloat16)
    partial = contract(pre_grad, up_weight, ((1,), (1,))).astype(jnp.bfloat16)
    x_hat_all = normed_all.astype(jnp.float32) / norm_gain
    gain_grad = jnp.sum(partial.astype(jnp.float32) * x_hat_all, axis=0)

    hidden_all = jnp.concatenate(replicas(hidden, True), axis=0)
    pre_all = jnp.concatenate(replicas(pre_grad, False), axis=0)

    for bit in range((n_dp - 1).bit_length()):
        gain_grad = gain_grad + replica(gain_grad, 1 << bit)
    gain_grad = gain_grad + across(gain_grad)
    shift = 1
    while shift < chips:
        gain_grad = gain_grad + along_ring(gain_grad, shift)
        shift *= 2
    gain_grad = gain_grad * factor

    half = rows * chips
    total = partial[:half].astype(jnp.float32) + across(partial[half:]).astype(jnp.float32)
    parts = total.astype(jnp.bfloat16).reshape(chips, rows, width)
    norm_grad = total[:rows]
    for s in range(1, chips):
        norm_grad = norm_grad + along_ring(parts[s], -s).astype(jnp.float32)
    scaled = norm_gain * norm_grad
    input_grad = (
        scaled
        - jnp.mean(scaled, axis=1, keepdims=True)
        - x_hat * jnp.mean(scaled * x_hat, axis=1, keepdims=True)
    ) * inv_std

    down_grad = (contract(hidden_all, columns[1], ((0,), (0,))) * factor).astype(jnp.bfloat16)
    up_grad = (contract(columns[0], pre_all, ((0,), (0,))) * factor).astype(jnp.bfloat16)
    return (input_grad.astype(jnp.bfloat16), up_grad, down_grad, gain_grad)


def solution(mesh):
    placed = (P(("dp", "mp"), None), P(), P(None, "mp"), P("mp", None), P(("dp", "mp"), None))
    return jax.shard_map(
        layer,
        mesh=mesh,
        in_specs=placed,
        out_specs=(P(("dp", "mp"), None), P("dp", "mp"), P("mp", "dp"), P()),
        check_vma=False,
    )
```

profile of v0, /device:TPU:0, one launch (start us, length us, event | category | flops | bytes accessed | tf_op | source)
XLA Modules:
  0.0 173.4 jit_solution(5056483834424753991)
XLA Ops:
  0.6 0.6 collective-permute-start.3
  1.2 3.6 %collective-permute-start = (bf16[16,6144]{1,0:T(8,128)(2,1)}, bf16[16,6144]{1,0:T(8,128)(2,1)S(1)}, u32[]{:S(2)}, u32[]{:S(2)}) collective-permute-start(bf16[16,6144]{1,0:T(8,128)(2,1)} %param.9), channel_id=1, source_target_pairs={{0,4},{1,5},{2,0},{3,1},{4,6},{5,7},{6,2},{7,3},{8,12},{9,13},{10,... | collective-permute-start | bytes 589832 | tf_op jit(solution)/shard_map/ppermute | solution.py:44
  4.8 1.1 convert_reduce_fusion
  5.9 1.2 fusion.29
  7.1 1.1 constant_dynamic-update-slice_fusion.15
  8.2 0.9 dynamic-slice_bitcast_fusion.6
  9.2 2.5 %collective-permute-start.20 = (bf16[2,16,1536]{2,1,0:T(8,128)(2,1)S(1)}, bf16[2,16,1536]{2,1,0:T(8,128)(2,1)S(1)}, u32[]{:S(2)}, u32[]{:S(2)}) collective-permute-start(bf16[2,16,1536]{2,1,0:T(8,128)(2,1)S(1)} %pad_maximum_fusion.3), channel_id=1, source_target_pairs={{0,24},{8,16},{16,8},{24,0},{1,25},{9,17},{17,9},{25,1},{2,26},{10... | collective-permute-start | bytes 294920 | tf_op jit(solution)/shard_map/ppermute | solution.py:50
  11.7 0.6 collective-permute-start.18
  12.3 0.6 collective-permute-start.19
  12.9 2.9 %collective-permute-done.20 = bf16[2,16,1536]{2,1,0:T(8,128)(2,1)S(1)} collective-permute-done((bf16[2,16,1536]{2,1,0:T(8,128)(2,1)S(1)}, bf16[2,16,1536]{2,1,0:T(8,128)(2,1)S(1)}, u32[]{:S(2)}, u32[]{:S(2)}) %collective-permute-start.20) | collective-permute-done | bytes 98336 | tf_op jit(solution)/shard_map/ppermute | solution.py:50
  15.8 1.4 collective-permute-done.18
  17.1 1.6 collective-permute-start.7
  18.8 0.4 collective-permute-start.21
  19.2 5.7 %collective-permute-done.7 = bf16[16,6144]{1,0:T(8,128)(2,1)S(1)} collective-permute-done((bf16[16,6144]{1,0:T(8,128)(2,1)S(1)}, bf16[16,6144]{1,0:T(8,128)(2,1)S(1)}, u32[]{:S(2)}, u32[]{:S(2)}) %collective-permute-start.7) | collective-permute-done | bytes 196640 | tf_op jit(solution)/shard_map/ppermute | solution.py:44
  24.9 2.5 %collective-permute-start.1 = (bf16[16,6144]{1,0:T(8,128)(2,1)S(1)}, bf16[16,6144]{1,0:T(8,128)(2,1)S(1)}, u32[]{:S(2)}, u32[]{:S(2)}) collective-permute-start(bf16[16,6144]{1,0:T(8,128)(2,1)S(1)} %collective-permute-done), channel_id=1, source_target_pairs={{0,4},{1,5},{2,0},{3,1},{4,6},{5,7},{6,2},{7,3},{8,12},{9,13},{10,... | collective-permute-start | bytes 589832 | tf_op jit(solution)/shard_map/ppermute | solution.py:44
  27.4 8.5 %collective-permute-done.1 = bf16[16,6144]{1,0:T(8,128)(2,1)S(1)} collective-permute-done((bf16[16,6144]{1,0:T(8,128)(2,1)S(1)}, bf16[16,6144]{1,0:T(8,128)(2,1)S(1)}, u32[]{:S(2)}, u32[]{:S(2)}) %collective-permute-start.1) | collective-permute-done | bytes 196640 | tf_op jit(solution)/shard_map/ppermute | solution.py:44
  35.9 2.5 %collective-permute-start.8 = (bf16[16,6144]{1,0:T(8,128)(2,1)S(1)}, bf16[16,6144]{1,0:T(8,128)(2,1)S(1)}, u32[]{:S(2)}, u32[]{:S(2)}) collective-permute-start(bf16[16,6144]{1,0:T(8,128)(2,1)S(1)} %collective-permute-done.7), channel_id=1, source_target_pairs={{0,4},{1,5},{2,0},{3,1},{4,6},{5,7},{6,2},{7,3},{8,12},{9,13},{10,... | collective-permute-start | bytes 589832 | tf_op jit(solution)/shard_map/ppermute | solution.py:44
  38.4 3.2 %collective-permute-done.8 = bf16[16,6144]{1,0:T(8,128)(2,1)S(1)} collective-permute-done((bf16[16,6144]{1,0:T(8,128)(2,1)S(1)}, bf16[16,6144]{1,0:T(8,128)(2,1)S(1)}, u32[]{:S(2)}, u32[]{:S(2)}) %collective-permute-start.8) | collective-permute-done | bytes 196640 | tf_op jit(solution)/shard_map/ppermute | solution.py:44
  41.6 3.4 %collective-permute-start.2 = (bf16[16,6144]{1,0:T(8,128)(2,1)S(1)}, bf16[16,6144]{1,0:T(8,128)(2,1)S(1)}, u32[]{:S(2)}, u32[]{:S(2)}) collective-permute-start(bf16[16,6144]{1,0:T(8,128)(2,1)S(1)} %collective-permute-done.1), channel_id=1, source_target_pairs={{0,4},{1,5},{2,0},{3,1},{4,6},{5,7},{6,2},{7,3},{8,12},{9,13},{10,... | collective-permute-start | bytes 589832 | tf_op jit(solution)/shard_map/ppermute | solution.py:44
  45.0 3.2 %collective-permute-done.2 = bf16[16,6144]{1,0:T(8,128)(2,1)S(1)} collective-permute-done((bf16[16,6144]{1,0:T(8,128)(2,1)S(1)}, bf16[16,6144]{1,0:T(8,128)(2,1)S(1)}, u32[]{:S(2)}, u32[]{:S(2)}) %collective-permute-start.2) | collective-permute-done | bytes 196640 | tf_op jit(solution)/shard_map/ppermute | solution.py:44
  48.2 0.6 collective-permute-start.5
  48.9 3.4 %collective-permute-start.9 = (bf16[16,6144]{1,0:T(8,128)(2,1)S(1)}, bf16[16,6144]{1,0:T(8,128)(2,1)S(1)}, u32[]{:S(2)}, u32[]{:S(2)}) collective-permute-start(bf16[16,6144]{1,0:T(8,128)(2,1)S(1)} %collective-permute-done.8), channel_id=1, source_target_pairs={{0,4},{1,5},{2,0},{3,1},{4,6},{5,7},{6,2},{7,3},{8,12},{9,13},{10,... | collective-permute-start | bytes 589832 | tf_op jit(solution)/shard_map/ppermute | solution.py:44
  52.3 0.9 collective-permute-start.22
  53.3 4.3 %collective-permute-done.9 = bf16[16,6144]{1,0:T(8,128)(2,1)S(1)} collective-permute-done((bf16[16,6144]{1,0:T(8,128)(2,1)S(1)}, bf16[16,6144]{1,0:T(8,128)(2,1)S(1)}, u32[]{:S(2)}, u32[]{:S(2)}) %collective-permute-start.9) | collective-permute-done | bytes 196640 | tf_op jit(solution)/shard_map/ppermute | solution.py:44
  57.6 0.6 collective-permute-start.13
  58.3 1.0 collective-permute-done.13
  59.4 13.2 %multiply_convert_fusion.2 = (bf16[128,2048]{1,0:T(8,128)(2,1)}, f32[128,2048]{1,0:T(8,128)S(1)}) fusion(bf16[128,6144]{1,0:T(8,128)(2,1)S(1)} %constant_dynamic-update-slice_fusion.8, bf16[6144,2048]{1,0:T(8,128)(2,1)} %param.7), kind=kOutput, calls=%fused_computation.29 | convolution fusion | flops 3222536192 | bytes 28311552 | tf_op jit(solution)/shard_map/dot_general | solution.py:32
  72.6 13.2 %fusion = bf16[128,2048]{1,0:T(8,128)(2,1)S(1)} fusion(bf16[128,6144]{1,0:T(8,128)(2,1)S(1)} %constant_dynamic-update-slice_fusion, bf16[2048,6144]{1,0:T(8,128)(2,1)} %param.8, f32[128,2048]{1,0:T(8,128)S(1)} %get-tuple-element.27), kind=kOutput, calls=%fused_computation.6 | convolution fusion | flops 3223846912 | bytes 28311552 | tf_op jit(solution)/shard_map/dot_general | solution.py:32
  85.8 13.5 %multiply_reduce_fusion = (f32[6144]{0:T(1024)S(1)}, bf16[128,6144]{1,0:T(8,128)(2,1)S(1)}) fusion(bf16[128,6144]{1,0:T(8,128)(2,1)} %copy-done.1, f32[6144]{0:T(1024)} %param.6, bf16[128,2048]{1,0:T(8,128)(2,1)S(1)} %fusion, bf16[6144,2048]{1,0:T(8,128)(2,1)} %param.7), kind=kOutput, calls=%fused_computation.4 | convolution fusion | flops 3225937920 | bytes 28884992 | tf_op jit(solution)/shard_map/dot_general | solution.py:32
  99.4 0.4 collective-permute-start.14
  99.8 3.4 %collective-permute-start.23 = (bf16[4,2,16,1536]{3,2,0,1:T(8,128)(2,1)}, bf16[4,2,16,1536]{3,2,0,1:T(8,128)(2,1)S(1)}, u32[]{:S(2)}, u32[]{:S(2)}) collective-permute-start(bf16[4,2,16,1536]{3,2,0,1:T(8,128)(2,1)} %collective-permute-done.22), channel_id=1, source_target_pairs={{0,4},{1,5},{2,0},{3,1},{4,6},{5,7},{6,2},{7,3},{8,12},{9,13},{10,... | collective-permute-start | bytes 1179656 | tf_op jit(solution)/shard_map/ppermute | solution.py:44
  103.2 1.5 collective-permute-start.34
  104.7 2.3 %collective-permute-done.34 = f32[6144]{0:T(1024)S(1)} collective-permute-done((f32[6144]{0:T(1024)S(1)}, f32[6144]{0:T(1024)S(1)}, u32[]{:S(2)}, u32[]{:S(2)}) %collective-permute-start.34) | collective-permute-done | bytes 24608 | tf_op jit(solution)/shard_map/ppermute | solution.py:50
  107.0 1.8 %collective-permute-start.35 = (f32[6144]{0:T(1024)S(1)}, f32[6144]{0:T(1024)S(1)}, u32[]{:S(2)}, u32[]{:S(2)}) collective-permute-start(f32[6144]{0:T(1024)S(1)} %add.69), channel_id=1, source_target_pairs={{0,16},{8,24},{16,0},{24,8},{1,17},{9,25},{17,1},{25,9},{2,18},{10... | collective-permute-start | bytes 73736 | tf_op jit(solution)/shard_map/ppermute | solution.py:50
  108.8 2.0 %collective-permute-done.35 = f32[6144]{0:T(1024)S(1)} collective-permute-done((f32[6144]{0:T(1024)S(1)}, f32[6144]{0:T(1024)S(1)}, u32[]{:S(2)}, u32[]{:S(2)}) %collective-permute-start.35) | collective-permute-done | bytes 24608 | tf_op jit(solution)/shard_map/ppermute | solution.py:50
  110.9 1.2 collective-permute-done.36
  112.1 3.8 %collective-permute-done.37 = f32[6144]{0:T(1024)S(1)} collective-permute-done((f32[6144]{0:T(1024)S(1)}, f32[6144]{0:T(1024)S(1)}, u32[]{:S(2)}, u32[]{:S(2)}) %collective-permute-start.37) | collective-permute-done | bytes 24608 | tf_op jit(solution)/shard_map/ppermute | solution.py:44
  115.9 0.2 collective-permute-start.38
  116.1 0.5 collective-permute-start.25
  116.6 4.9 %collective-permute-done.38 = f32[6144]{0:T(1024)S(1)} collective-permute-done((f32[6144]{0:T(1024)S(1)}, f32[6144]{0:T(1024)S(1)}, u32[]{:S(2)}, u32[]{:S(2)}) %collective-permute-start.38) | collective-permute-done | bytes 24608 | tf_op jit(solution)/shard_map/ppermute | solution.py:44
  121.5 1.5 collective-permute-start.28
  123.0 0.6 add_multiply_fusion
  123.7 0.5 collective-permute-start.27
  124.2 0.2 convert_add_fusion
  124.4 0.2 copy-done.3
  124.7 1.8 %collective-permute-start.32 = (bf16[128,2048]{1,0:T(8,128)(2,1)S(1)}, bf16[128,2048]{1,0:T(8,128)(2,1)S(1)}, u32[]{:S(2)}, u32[]{:S(2)}) collective-permute-start(bf16[128,2048]{1,0:T(8,128)(2,1)S(1)} %copy-done.3), channel_id=1, source_target_pairs={{0,16},{8,24},{16,0},{24,8},{1,17},{9,25},{17,1},{25,9},{2,18},{10... | collective-permute-start | bytes 1572872 | tf_op jit(solution)/shard_map/ppermute | solution.py:50
  126.5 2.9 %collective-permute-start.17 = (bf16[16,6144]{1,0:T(8,128)(2,1)S(1)}, bf16[16,6144]{1,0:T(8,128)(2,1)S(1)}, u32[]{:S(2)}, u32[]{:S(2)}) collective-permute-start(bf16[16,6144]{1,0:T(8,128)(2,1)S(1)} %get-tuple-element.14), channel_id=1, source_target_pairs={{0,4},{1,5},{2,0},{3,1},{4,6},{5,7},{6,2},{7,3},{8,12},{9,13},{10,... | collective-permute-start | bytes 589832 | tf_op jit(solution)/shard_map/ppermute | solution.py:44
  129.4 0.3 collective-permute-start.16
  129.7 0.2 maximum_bitcast_fusion.2
  129.9 1.4 maximum_bitcast_fusion
  131.3 0.3 fusion.40
  131.6 1.6 collective-permute-done.28
  133.2 1.8 %collective-permute-start.29 = (bf16[128,2048]{1,0:T(8,128)(2,1)S(1)}, bf16[128,2048]{1,0:T(8,128)(2,1)S(1)}, u32[]{:S(2)}, u32[]{:S(2)}) collective-permute-start(bf16[128,2048]{1,0:T(8,128)(2,1)S(1)} %fusion), channel_id=1, source_target_pairs={{0,16},{8,24},{16,0},{24,8},{1,17},{9,25},{17,1},{25,9},{2,18},{10... | collective-permute-start | bytes 1572872 | tf_op jit(solution)/shard_map/ppermute | solution.py:50
  135.0 4.4 %collective-permute-done.32 = bf16[128,2048]{1,0:T(8,128)(2,1)S(1)} collective-permute-done((bf16[128,2048]{1,0:T(8,128)(2,1)S(1)}, bf16[128,2048]{1,0:T(8,128)(2,1)S(1)}, u32[]{:S(2)}, u32[]{:S(2)}) %collective-permute-start.32) | collective-permute-done | bytes 524320 | tf_op jit(solution)/shard_map/ppermute | solution.py:50
  139.5 0.5 collective-permute-start.31
  140.0 3.2 %collective-permute-done.15 = bf16[16,6144]{1,0:T(8,128)(2,1)S(1)} collective-permute-done((bf16[16,6144]{1,0:T(8,128)(2,1)S(1)}, bf16[16,6144]{1,0:T(8,128)(2,1)S(1)}, u32[]{:S(2)}, u32[]{:S(2)}) %collective-permute-start.15) | collective-permute-done | bytes 196640 | tf_op jit(solution)/shard_map/ppermute | solution.py:44
  143.2 0.4 collective-permute-start.30
  143.5 0.6 collective-permute-start.33
  144.2 0.3 fusion.37
  144.5 0.8 fusion.28
  145.3 8.9 %collective-permute-done.31 = bf16[128,2048]{1,0:T(8,128)(2,1)S(1)} collective-permute-done((bf16[128,2048]{1,0:T(8,128)(2,1)S(1)}, bf16[128,2048]{1,0:T(8,128)(2,1)S(1)}, u32[]{:S(2)}, u32[]{:S(2)}) %collective-permute-start.31) | collective-permute-done | bytes 524320 | tf_op jit(solution)/shard_map/ppermute | solution.py:50
  154.3 8.4 %collective-permute-done.33 = bf16[128,2048]{1,0:T(8,128)(2,1)S(1)} collective-permute-done((bf16[128,2048]{1,0:T(8,128)(2,1)S(1)}, bf16[128,2048]{1,0:T(8,128)(2,1)S(1)}, u32[]{:S(2)}, u32[]{:S(2)}) %collective-permute-start.33) | collective-permute-done | bytes 524320 | tf_op jit(solution)/shard_map/ppermute | solution.py:50
  162.7 5.4 %multiply_convert_fusion = bf16[2048,1536]{1,0:T(8,128)(2,1)} fusion(bf16[512,1536]{1,0:T(8,128)(2,1)S(1)} %bitcast.55, bf16[128,2048]{1,0:T(8,128)(2,1)S(1)} %collective-permute-done.33, bf16[128,2048]{1,0:T(8,128)(2,1)S(1)} %collective-permute-done.32, bf16[128,2048]{1,0:T(8,128)(2,1)S(1)} %collective-permute-done.31, bf16[128,2048]{1,0:T(8,128)(2,1)S(1)} %copy-done.3), kind=kOutput, calls=%fused_computation | convolution fusion | flops 3235905536 | bytes 9961472 | tf_op jit(solution)/shard_map/dot_general | solution.py:32
  168.1 5.4 %multiply_convert_fusion.1 = bf16[1536,2048]{1,0:T(8,128)(2,1)} fusion(bf16[512,1536]{1,0:T(8,128)(2,1)S(1)} %bitcast.54, bf16[128,2048]{1,0:T(8,128)(2,1)S(1)} %collective-permute-done.30, bf16[128,2048]{1,0:T(8,128)(2,1)S(1)} %collective-permute-done.29, bf16[128,2048]{1,0:T(8,128)(2,1)S(1)} %collective-permute-done.28, bf16[128,2048]{1,0:T(8,128)(2,1)S(1)} %fusion), kind=kOutput, calls=%fused_computation.1 | convolution fusion | flops 3235905536 | bytes 9961472 | tf_op jit(solution)/shard_map/dot_general | solution.py:32
  (74 shorter events, 0.7 us)
Async XLA Ops:
  0.6 12.2 %copy-start.2 = (bf16[16,6144]{1,0:T(8,128)(2,1)S(1)}, bf16[16,6144]{1,0:T(8,128)(2,1)}, u32[]{:S(2)}) copy-start(bf16[16,6144]{1,0:T(8,128)(2,1)} %param.9) | copy-start | bytes 589828
  0.6 47.5 %collective-permute-start.3 = (bf16[16,6144]{1,0:T(8,128)(2,1)}, bf16[16,6144]{1,0:T(8,128)(2,1)S(1)}, u32[]{:S(2)}, u32[]{:S(2)}) collective-permute-start(bf16[16,6144]{1,0:T(8,128)(2,1)} %param.9), channel_id=1, source_target_pairs={{0,1},{1,0},{2,3},{3,2},{4,5},{5,4},{6,7},{7,6},{8,9},{9,8},{10,11... | collective-permute-start | bytes 589832 | tf_op jit(solution)/shard_map/ppermute | solution.py:47
  1.2 18.0 %collective-permute-start = (bf16[16,6144]{1,0:T(8,128)(2,1)}, bf16[16,6144]{1,0:T(8,128)(2,1)S(1)}, u32[]{:S(2)}, u32[]{:S(2)}) collective-permute-start(bf16[16,6144]{1,0:T(8,128)(2,1)} %param.9), channel_id=1, source_target_pairs={{0,4},{1,5},{2,0},{3,1},{4,6},{5,7},{6,2},{7,3},{8,12},{9,13},{10,... | collective-permute-start | bytes 589832 | tf_op jit(solution)/shard_map/ppermute | solution.py:44
  9.2 6.6 %collective-permute-start.20 = (bf16[2,16,1536]{2,1,0:T(8,128)(2,1)S(1)}, bf16[2,16,1536]{2,1,0:T(8,128)(2,1)S(1)}, u32[]{:S(2)}, u32[]{:S(2)}) collective-permute-start(bf16[2,16,1536]{2,1,0:T(8,128)(2,1)S(1)} %pad_maximum_fusion.3), channel_id=1, source_target_pairs={{0,24},{8,16},{16,8},{24,0},{1,25},{9,17},{17,9},{25,1},{2,26},{10... | collective-permute-start | bytes 294920 | tf_op jit(solution)/shard_map/ppermute | solution.py:50
  11.7 5.5 %collective-permute-start.18 = (bf16[2,16,1536]{2,1,0:T(8,128)(2,1)S(1)}, bf16[2,16,1536]{2,1,0:T(8,128)(2,1)S(1)}, u32[]{:S(2)}, u32[]{:S(2)}) collective-permute-start(bf16[2,16,1536]{2,1,0:T(8,128)(2,1)S(1)} %pad_maximum_fusion.1), channel_id=1, source_target_pairs={{0,8},{8,0},{16,24},{24,16},{1,9},{9,1},{17,25},{25,17},{2,10},{10... | collective-permute-start | bytes 294920 | tf_op jit(solution)/shard_map/ppermute | solution.py:50
  12.3 6.4 %collective-permute-start.19 = (bf16[2,16,1536]{2,1,0:T(8,128)(2,1)S(1)}, bf16[2,16,1536]{2,1,0:T(8,128)(2,1)S(1)}, u32[]{:S(2)}, u32[]{:S(2)}) collective-permute-start(bf16[2,16,1536]{2,1,0:T(8,128)(2,1)S(1)} %pad_maximum_fusion.2), channel_id=1, source_target_pairs={{0,16},{8,24},{16,0},{24,8},{1,17},{9,25},{17,1},{25,9},{2,18},{10... | collective-permute-start | bytes 294920 | tf_op jit(solution)/shard_map/ppermute | solution.py:50
  15.8 41.8 %collective-permute-start.10 = (bf16[16,6144]{1,0:T(8,128)(2,1)S(1)}, bf16[16,6144]{1,0:T(8,128)(2,1)S(1)}, u32[]{:S(2)}, u32[]{:S(2)}) collective-permute-start(bf16[16,6144]{1,0:T(8,128)(2,1)S(1)} %get-tuple-element.8), channel_id=1, source_target_pairs={{0,1},{1,0},{2,3},{3,2},{4,5},{5,4},{6,7},{7,6},{8,9},{9,8},{10,11... | collective-permute-start | bytes 589832 | tf_op jit(solution)/shard_map/ppermute | solution.py:47
  17.1 7.8 %collective-permute-start.7 = (bf16[16,6144]{1,0:T(8,128)(2,1)S(1)}, bf16[16,6144]{1,0:T(8,128)(2,1)S(1)}, u32[]{:S(2)}, u32[]{:S(2)}) collective-permute-start(bf16[16,6144]{1,0:T(8,128)(2,1)S(1)} %get-tuple-element.8), channel_id=1, source_target_pairs={{0,4},{1,5},{2,0},{3,1},{4,6},{5,7},{6,2},{7,3},{8,12},{9,13},{10,... | collective-permute-start | bytes 589832 | tf_op jit(solution)/shard_map/ppermute | solution.py:44
  18.8 34.5 %copy-start.4 = (bf16[4,2,16,1536]{3,2,0,1:T(8,128)(2,1)}, bf16[4,2,16,1536]{3,2,0,1:T(8,128)(2,1)S(1)}, u32[]{:S(2)}) copy-start(bf16[4,2,16,1536]{3,2,0,1:T(8,128)(2,1)S(1)} %get-tuple-element.17) | copy-start | bytes 1179652
  18.8 30.1 %collective-permute-start.21 = (bf16[4,2,16,1536]{3,2,0,1:T(8,128)(2,1)S(1)}, bf16[4,2,16,1536]{3,2,0,1:T(8,128)(2,1)}, u32[]{:S(2)}, u32[]{:S(2)}) collective-permute-start(bf16[4,2,16,1536]{3,2,0,1:T(8,128)(2,1)S(1)} %get-tuple-element.17), channel_id=1, source_target_pairs={{0,4},{1,5},{2,0},{3,1},{4,6},{5,7},{6,2},{7,3},{8,12},{9,13},{10,... | collective-permute-start | bytes 1179656 | tf_op jit(solution)/shard_map/ppermute | solution.py:44
  19.2 29.6 %collective-permute-start.4 = (bf16[16,6144]{1,0:T(8,128)(2,1)S(1)}, bf16[16,6144]{1,0:T(8,128)(2,1)S(1)}, u32[]{:S(2)}, u32[]{:S(2)}) collective-permute-start(bf16[16,6144]{1,0:T(8,128)(2,1)S(1)} %collective-permute-done), channel_id=1, source_target_pairs={{0,1},{1,0},{2,3},{3,2},{4,5},{5,4},{6,7},{7,6},{8,9},{9,8},{10,11... | collective-permute-start | bytes 589832 | tf_op jit(solution)/shard_map/ppermute | solution.py:47
  24.9 11.0 %collective-permute-start.1 = (bf16[16,6144]{1,0:T(8,128)(2,1)S(1)}, bf16[16,6144]{1,0:T(8,128)(2,1)S(1)}, u32[]{:S(2)}, u32[]{:S(2)}) collective-permute-start(bf16[16,6144]{1,0:T(8,128)(2,1)S(1)} %collective-permute-done), channel_id=1, source_target_pairs={{0,4},{1,5},{2,0},{3,1},{4,6},{5,7},{6,2},{7,3},{8,12},{9,13},{10,... | collective-permute-start | bytes 589832 | tf_op jit(solution)/shard_map/ppermute | solution.py:44
  35.9 5.7 %collective-permute-start.8 = (bf16[16,6144]{1,0:T(8,128)(2,1)S(1)}, bf16[16,6144]{1,0:T(8,128)(2,1)S(1)}, u32[]{:S(2)}, u32[]{:S(2)}) collective-permute-start(bf16[16,6144]{1,0:T(8,128)(2,1)S(1)} %collective-permute-done.7), channel_id=1, source_target_pairs={{0,4},{1,5},{2,0},{3,1},{4,6},{5,7},{6,2},{7,3},{8,12},{9,13},{10,... | collective-permute-start | bytes 589832 | tf_op jit(solution)/shard_map/ppermute | solution.py:44
  41.6 6.6 %collective-permute-start.2 = (bf16[16,6144]{1,0:T(8,128)(2,1)S(1)}, bf16[16,6144]{1,0:T(8,128)(2,1)S(1)}, u32[]{:S(2)}, u32[]{:S(2)}) collective-permute-start(bf16[16,6144]{1,0:T(8,128)(2,1)S(1)} %collective-permute-done.1), channel_id=1, source_target_pairs={{0,4},{1,5},{2,0},{3,1},{4,6},{5,7},{6,2},{7,3},{8,12},{9,13},{10,... | collective-permute-start | bytes 589832 | tf_op jit(solution)/shard_map/ppermute | solution.py:44
  48.1 10.1 %collective-permute-start.11 = (bf16[16,6144]{1,0:T(8,128)(2,1)S(1)}, bf16[16,6144]{1,0:T(8,128)(2,1)S(1)}, u32[]{:S(2)}, u32[]{:S(2)}) collective-permute-start(bf16[16,6144]{1,0:T(8,128)(2,1)S(1)} %collective-permute-done.7), channel_id=1, source_target_pairs={{0,1},{1,0},{2,3},{3,2},{4,5},{5,4},{6,7},{7,6},{8,9},{9,8},{10,11... | collective-permute-start | bytes 589832 | tf_op jit(solution)/shard_map/ppermute | solution.py:47
  48.2 4.1 %collective-permute-start.5 = (bf16[16,6144]{1,0:T(8,128)(2,1)S(1)}, bf16[16,6144]{1,0:T(8,128)(2,1)S(1)}, u32[]{:S(2)}, u32[]{:S(2)}) collective-permute-start(bf16[16,6144]{1,0:T(8,128)(2,1)S(1)} %collective-permute-done.1), channel_id=1, source_target_pairs={{0,1},{1,0},{2,3},{3,2},{4,5},{5,4},{6,7},{7,6},{8,9},{9,8},{10,11... | collective-permute-start | bytes 589832 | tf_op jit(solution)/shard_map/ppermute | solution.py:47
  48.8 9.5 %collective-permute-start.12 = (bf16[16,6144]{1,0:T(8,128)(2,1)S(1)}, bf16[16,6144]{1,0:T(8,128)(2,1)S(1)}, u32[]{:S(2)}, u32[]{:S(2)}) collective-permute-start(bf16[16,6144]{1,0:T(8,128)(2,1)S(1)} %collective-permute-done.8), channel_id=1, source_target_pairs={{0,1},{1,0},{2,3},{3,2},{4,5},{5,4},{6,7},{7,6},{8,9},{9,8},{10,11... | collective-permute-start | bytes 589832 | tf_op jit(solution)/shard_map/ppermute | solution.py:47
  48.9 8.7 %collective-permute-start.9 = (bf16[16,6144]{1,0:T(8,128)(2,1)S(1)}, bf16[16,6144]{1,0:T(8,128)(2,1)S(1)}, u32[]{:S(2)}, u32[]{:S(2)}) collective-permute-start(bf16[16,6144]{1,0:T(8,128)(2,1)S(1)} %collective-permute-done.8), channel_id=1, source_target_pairs={{0,4},{1,5},{2,0},{3,1},{4,6},{5,7},{6,2},{7,3},{8,12},{9,13},{10,... | collective-permute-start | bytes 589832 | tf_op jit(solution)/shard_map/ppermute | solution.py:44
  52.3 47.5 %collective-permute-start.22 = (bf16[4,2,16,1536]{3,2,0,1:T(8,128)(2,1)}, bf16[4,2,16,1536]{3,2,0,1:T(8,128)(2,1)}, u32[]{:S(2)}, u32[]{:S(2)}) collective-permute-start(bf16[4,2,16,1536]{3,2,0,1:T(8,128)(2,1)} %collective-permute-done.21), channel_id=1, source_target_pairs={{0,4},{1,5},{2,0},{3,1},{4,6},{5,7},{6,2},{7,3},{8,12},{9,13},{10,... | collective-permute-start | bytes 1179656 | tf_op jit(solution)/shard_map/ppermute | solution.py:44
  57.6 15.0 %collective-permute-start.6 = (bf16[16,6144]{1,0:T(8,128)(2,1)S(1)}, bf16[16,6144]{1,0:T(8,128)(2,1)S(1)}, u32[]{:S(2)}, u32[]{:S(2)}) collective-permute-start(bf16[16,6144]{1,0:T(8,128)(2,1)S(1)} %collective-permute-done.2), channel_id=1, source_target_pairs={{0,1},{1,0},{2,3},{3,2},{4,5},{5,4},{6,7},{7,6},{8,9},{9,8},{10,11... | collective-permute-start | bytes 589832 | tf_op jit(solution)/shard_map/ppermute | solution.py:47
  57.6 1.7 collective-permute-start.13
  59.3 13.2 %copy-start.1 = (bf16[128,6144]{1,0:T(8,128)(2,1)}, bf16[128,6144]{1,0:T(8,128)(2,1)S(1)}, u32[]{:S(2)}) copy-start(bf16[128,6144]{1,0:T(8,128)(2,1)S(1)} %constant_dynamic-update-slice_fusion.8) | copy-start | bytes 4718596
  99.4 16.8 %copy-start.5 = (bf16[4,2,16,1536]{3,2,0,1:T(8,128)(2,1)S(1)}, bf16[4,2,16,1536]{3,2,0,1:T(8,128)(2,1)}, u32[]{:S(2)}) copy-start(bf16[4,2,16,1536]{3,2,0,1:T(8,128)(2,1)} %copy-done.4) | copy-start | bytes 1179652
  99.4 24.2 %collective-permute-start.14 = (bf16[64,6144]{1,0:T(8,128)(2,1)S(1)}, bf16[64,6144]{1,0:T(8,128)(2,1)S(1)}, u32[]{:S(2)}, u32[]{:S(2)}) collective-permute-start(bf16[64,6144]{1,0:T(8,128)(2,1)S(1)} %slice.38), channel_id=1, source_target_pairs={{0,1},{1,0},{2,3},{3,2},{4,5},{5,4},{6,7},{7,6},{8,9},{9,8},{10,11... | collective-permute-start | bytes 2359304 | tf_op jit(solution)/shard_map/ppermute | solution.py:47
  99.8 23.8 %collective-permute-start.23 = (bf16[4,2,16,1536]{3,2,0,1:T(8,128)(2,1)}, bf16[4,2,16,1536]{3,2,0,1:T(8,128)(2,1)S(1)}, u32[]{:S(2)}, u32[]{:S(2)}) collective-permute-start(bf16[4,2,16,1536]{3,2,0,1:T(8,128)(2,1)} %collective-permute-done.22), channel_id=1, source_target_pairs={{0,4},{1,5},{2,0},{3,1},{4,6},{5,7},{6,2},{7,3},{8,12},{9,13},{10,... | collective-permute-start | bytes 1179656 | tf_op jit(solution)/shard_map/ppermute | solution.py:44
  103.2 3.8 %collective-permute-start.34 = (f32[6144]{0:T(1024)S(1)}, f32[6144]{0:T(1024)S(1)}, u32[]{:S(2)}, u32[]{:S(2)}) collective-permute-start(f32[6144]{0:T(1024)S(1)} %get-tuple-element.28), channel_id=1, source_target_pairs={{0,8},{8,0},{16,24},{24,16},{1,9},{9,1},{17,25},{25,17},{2,10},{10... | collective-permute-start | bytes 73736 | tf_op jit(solution)/shard_map/ppermute | solution.py:50
  107.0 3.8 %collective-permute-start.35 = (f32[6144]{0:T(1024)S(1)}, f32[6144]{0:T(1024)S(1)}, u32[]{:S(2)}, u32[]{:S(2)}) collective-permute-start(f32[6144]{0:T(1024)S(1)} %add.69), channel_id=1, source_target_pairs={{0,16},{8,24},{16,0},{24,8},{1,17},{9,25},{17,1},{25,9},{2,18},{10... | collective-permute-start | bytes 73736 | tf_op jit(solution)/shard_map/ppermute | solution.py:50
  110.9 1.2 collective-permute-start.36
  112.1 3.8 %collective-permute-start.37 = (f32[6144]{0:T(1024)S(1)}, f32[6144]{0:T(1024)S(1)}, u32[]{:S(2)}, u32[]{:S(2)}) collective-permute-start(f32[6144]{0:T(1024)S(1)} %add.71), channel_id=1, source_target_pairs={{0,4},{1,5},{2,0},{3,1},{4,6},{5,7},{6,2},{7,3},{8,12},{9,13},{10,... | collective-permute-start | bytes 73736 | tf_op jit(solution)/shard_map/ppermute | solution.py:44
  115.9 5.6 %collective-permute-start.38 = (f32[6144]{0:T(1024)S(1)}, f32[6144]{0:T(1024)S(1)}, u32[]{:S(2)}, u32[]{:S(2)}) collective-permute-start(f32[6144]{0:T(1024)S(1)} %add.72), channel_id=1, source_target_pairs={{0,6},{1,7},{2,4},{3,5},{4,2},{5,3},{6,0},{7,1},{8,14},{9,15},{10,... | collective-permute-start | bytes 73736 | tf_op jit(solution)/shard_map/ppermute | solution.py:44
  116.1 8.3 %collective-permute-start.24 = (bf16[4,2,16,1536]{3,2,0,1:T(8,128)(2,1)S(1)}, bf16[4,2,16,1536]{3,2,0,1:T(8,128)(2,1)S(1)}, u32[]{:S(2)}, u32[]{:S(2)}) collective-permute-start(bf16[4,2,16,1536]{3,2,0,1:T(8,128)(2,1)S(1)} %copy-done.5), channel_id=1, source_target_pairs={{0,1},{1,0},{2,3},{3,2},{4,5},{5,4},{6,7},{7,6},{8,9},{9,8},{10,11... | collective-permute-start | bytes 1179656 | tf_op jit(solution)/shard_map/ppermute | solution.py:47
  116.1 10.4 %collective-permute-start.25 = (bf16[4,2,16,1536]{3,2,0,1:T(8,128)(2,1)}, bf16[4,2,16,1536]{3,2,0,1:T(8,128)(2,1)S(1)}, u32[]{:S(2)}, u32[]{:S(2)}) collective-permute-start(bf16[4,2,16,1536]{3,2,0,1:T(8,128)(2,1)} %collective-permute-done.21), channel_id=1, source_target_pairs={{0,1},{1,0},{2,3},{3,2},{4,5},{5,4},{6,7},{7,6},{8,9},{9,8},{10,11... | collective-permute-start | bytes 1179656 | tf_op jit(solution)/shard_map/ppermute | solution.py:47
  121.5 11.7 %collective-permute-start.28 = (bf16[128,2048]{1,0:T(8,128)(2,1)S(1)}, bf16[128,2048]{1,0:T(8,128)(2,1)S(1)}, u32[]{:S(2)}, u32[]{:S(2)}) collective-permute-start(bf16[128,2048]{1,0:T(8,128)(2,1)S(1)} %fusion), channel_id=1, source_target_pairs={{0,8},{8,0},{16,24},{24,16},{1,9},{9,1},{17,25},{25,17},{2,10},{10... | collective-permute-start | bytes 1572872 | tf_op jit(solution)/shard_map/ppermute | solution.py:50
  123.6 1.0 copy-start.3
  123.6 2.9 %collective-permute-start.26 = (bf16[4,2,16,1536]{3,2,0,1:T(8,128)(2,1)}, bf16[4,2,16,1536]{3,2,0,1:T(8,128)(2,1)S(1)}, u32[]{:S(2)}, u32[]{:S(2)}) collective-permute-start(bf16[4,2,16,1536]{3,2,0,1:T(8,128)(2,1)} %collective-permute-done.22), channel_id=1, source_target_pairs={{0,1},{1,0},{2,3},{3,2},{4,5},{5,4},{6,7},{7,6},{8,9},{9,8},{10,11... | collective-permute-start | bytes 1179656 | tf_op jit(solution)/shard_map/ppermute | solution.py:47
  123.7 5.8 %collective-permute-start.27 = (bf16[4,2,16,1536]{3,2,0,1:T(8,128)(2,1)S(1)}, bf16[4,2,16,1536]{3,2,0,1:T(8,128)(2,1)S(1)}, u32[]{:S(2)}, u32[]{:S(2)}) collective-permute-start(bf16[4,2,16,1536]{3,2,0,1:T(8,128)(2,1)S(1)} %collective-permute-done.23), channel_id=1, source_target_pairs={{0,1},{1,0},{2,3},{3,2},{4,5},{5,4},{6,7},{7,6},{8,9},{9,8},{10,11... | collective-permute-start | bytes 1179656 | tf_op jit(solution)/shard_map/ppermute | solution.py:47
  124.7 14.8 %collective-permute-start.32 = (bf16[128,2048]{1,0:T(8,128)(2,1)S(1)}, bf16[128,2048]{1,0:T(8,128)(2,1)S(1)}, u32[]{:S(2)}, u32[]{:S(2)}) collective-permute-start(bf16[128,2048]{1,0:T(8,128)(2,1)S(1)} %copy-done.3), channel_id=1, source_target_pairs={{0,16},{8,24},{16,0},{24,8},{1,17},{9,25},{17,1},{25,9},{2,18},{10... | collective-permute-start | bytes 1572872 | tf_op jit(solution)/shard_map/ppermute | solution.py:50
  126.5 16.7 %collective-permute-start.15 = (bf16[16,6144]{1,0:T(8,128)(2,1)S(1)}, bf16[16,6144]{1,0:T(8,128)(2,1)S(1)}, u32[]{:S(2)}, u32[]{:S(2)}) collective-permute-start(bf16[16,6144]{1,0:T(8,128)(2,1)S(1)} %get-tuple-element.13), channel_id=1, source_target_pairs={{0,2},{1,3},{2,6},{3,7},{4,0},{5,1},{6,4},{7,5},{8,10},{9,11},{10,... | collective-permute-start | bytes 589832 | tf_op jit(solution)/shard_map/ppermute | solution.py:44
  126.5 17.0 %collective-permute-start.17 = (bf16[16,6144]{1,0:T(8,128)(2,1)S(1)}, bf16[16,6144]{1,0:T(8,128)(2,1)S(1)}, u32[]{:S(2)}, u32[]{:S(2)}) collective-permute-start(bf16[16,6144]{1,0:T(8,128)(2,1)S(1)} %get-tuple-element.14), channel_id=1, source_target_pairs={{0,4},{1,5},{2,0},{3,1},{4,6},{5,7},{6,2},{7,3},{8,12},{9,13},{10,... | collective-permute-start | bytes 589832 | tf_op jit(solution)/shard_map/ppermute | solution.py:44
  129.4 14.7 %collective-permute-start.16 = (bf16[16,6144]{1,0:T(8,128)(2,1)S(1)}, bf16[16,6144]{1,0:T(8,128)(2,1)S(1)}, u32[]{:S(2)}, u32[]{:S(2)}) collective-permute-start(bf16[16,6144]{1,0:T(8,128)(2,1)S(1)} %get-tuple-element.15), channel_id=1, source_target_pairs={{0,6},{1,7},{2,4},{3,5},{4,2},{5,3},{6,0},{7,1},{8,14},{9,15},{10,... | collective-permute-start | bytes 589832 | tf_op jit(solution)/shard_map/ppermute | solution.py:44
  131.3 12.9 %copy-start = (bf16[16,6144]{1,0:T(8,128)(2,1)S(1)}, bf16[16,6144]{1,0:T(8,128)(2,1)}, u32[]{:S(2)}) copy-start(bf16[16,6144]{1,0:T(8,128)(2,1)} %param.5) | copy-start | bytes 589828
  131.3 12.9 %copy-start.6 = (f32[6144]{0:T(1024)S(1)}, f32[6144]{0:T(1024)}, u32[]{:S(2)}) copy-start(f32[6144]{0:T(1024)} %param.6) | copy-start | bytes 73732
  133.2 34.8 %collective-permute-start.29 = (bf16[128,2048]{1,0:T(8,128)(2,1)S(1)}, bf16[128,2048]{1,0:T(8,128)(2,1)S(1)}, u32[]{:S(2)}, u32[]{:S(2)}) collective-permute-start(bf16[128,2048]{1,0:T(8,128)(2,1)S(1)} %fusion), channel_id=1, source_target_pairs={{0,16},{8,24},{16,0},{24,8},{1,17},{9,25},{17,1},{25,9},{2,18},{10... | collective-permute-start | bytes 1572872 | tf_op jit(solution)/shard_map/ppermute | solution.py:50
  139.5 14.8 %collective-permute-start.31 = (bf16[128,2048]{1,0:T(8,128)(2,1)S(1)}, bf16[128,2048]{1,0:T(8,128)(2,1)S(1)}, u32[]{:S(2)}, u32[]{:S(2)}) collective-permute-start(bf16[128,2048]{1,0:T(8,128)(2,1)S(1)} %copy-done.3), channel_id=1, source_target_pairs={{0,8},{8,0},{16,24},{24,16},{1,9},{9,1},{17,25},{25,17},{2,10},{10... | collective-permute-start | bytes 1572872 | tf_op jit(solution)/shard_map/ppermute | solution.py:50
  143.2 24.9 %collective-permute-start.30 = (bf16[128,2048]{1,0:T(8,128)(2,1)S(1)}, bf16[128,2048]{1,0:T(8,128)(2,1)S(1)}, u32[]{:S(2)}, u32[]{:S(2)}) collective-permute-start(bf16[128,2048]{1,0:T(8,128)(2,1)S(1)} %collective-permute-done.28), channel_id=1, source_target_pairs={{0,16},{8,24},{16,0},{24,8},{1,17},{9,25},{17,1},{25,9},{2,18},{10... | collective-permute-start | bytes 1572872 | tf_op jit(solution)/shard_map/ppermute | solution.py:50
  143.5 19.1 %collective-permute-start.33 = (bf16[128,2048]{1,0:T(8,128)(2,1)S(1)}, bf16[128,2048]{1,0:T(8,128)(2,1)S(1)}, u32[]{:S(2)}, u32[]{:S(2)}) collective-permute-start(bf16[128,2048]{1,0:T(8,128)(2,1)S(1)} %collective-permute-done.32), channel_id=1, source_target_pairs={{0,8},{8,0},{16,24},{24,16},{1,9},{9,1},{17,25},{25,17},{2,10},{10... | collective-permute-start | bytes 1572872 | tf_op jit(solution)/shard_map/ppermute | solution.py:50
where the time goes:
time: 174 us; the launch traced here: 173 us
  waiting for transfers between devices  71 us (41%)
  matrix products  50.7 us (29%)
  starting transfers between devices  41.9 us (24%)
  other arithmetic  7.04 us (4%)
  local copies, waits for them, and re-layouts  1.8 us (1%)
    dot_general x5, matrix products, contract(): lax.dot_general(a, b, (dims, ((), ())), preferred_element_type=jnp.float32)  50.7 us
    ppermute x14, waiting for transfers between devices, along_ring(): return lax.ppermute(array, 'mp', ring_perm(n_mp, shift))  36.8 us
    ppermute x11, waiting for transfers between devices, replica(): return lax.ppermute(array, 'dp', swap_perm(n_dp, mask))  32 us
    ppermute x14, starting transfers between devices, along_ring(): return lax.ppermute(array, 'mp', ring_perm(n_mp, shift))  25.1 us
    ppermute x11, starting transfers between devices, replica(): return lax.ppermute(array, 'dp', swap_perm(n_dp, mask))  13.6 us
  transfers between devices with their start and end apart: 39, of which 18 were waited for; matrix products, arithmetic and copies ran while one was open for 31% of the time, Pallas kernels for 0%

commit v1 on v0

v1 whole, which is shorter than its diff:
```python
import functools
import math

import jax
import jax.numpy as jnp
from jax import lax
from jax.experimental import pallas as pl
from jax.experimental.pallas import tpu as pltpu
from jax.sharding import PartitionSpec as P


def gelu_value(preact):
    return 0.5 * preact * (1.0 + lax.erf(preact * 0.7071067811865476))


def gelu_slope(preact):
    return (
        0.5 * (1.0 + lax.erf(preact * 0.7071067811865476))
        + preact * jnp.exp(-0.5 * preact * preact) * 0.3989422804014327
    )


def swap_perm(size, mask):
    return [(i, i ^ mask) for i in range(size)]


def ring_perm(size, shift):
    chips = size // 2
    order = list(range(0, chips, 2)) + list(range(1, chips, 2))[::-1]
    moved = {order[k]: order[(k + shift) % chips] for k in range(chips)}
    return [(2 * c + core, 2 * moved[c] + core) for c in range(chips) for core in range(2)]


def contract(a, b, dims):
    return lax.dot_general(a, b, (dims, ((), ())), preferred_element_type=jnp.float32)


def normalise(values, gain):
    values = values.astype(jnp.float32)
    centered = values - jnp.mean(values, axis=1, keepdims=True)
    inv_std = lax.rsqrt(jnp.mean(centered * centered, axis=1, keepdims=True) + 1e-06)
    x_hat = centered * inv_std
    return (x_hat * gain).astype(jnp.bfloat16), x_hat, inv_std


def chunk(total, most, unit):
    for parts in range(1, total // unit + 1):
        if total % parts == 0 and total // parts <= most and (total // parts) % unit == 0:
            return total // parts
    return total


WHOLE = pl.BlockSpec(memory_space=pltpu.VMEM)
STAYS = pl.BlockSpec(memory_space=pl.ANY)


class Stream:
    def __init__(self, weight, buffer, sems, step):
        self.refs, self.sems, self.step = (weight, buffer), sems, step

    def copy(self, part):
        start = part * self.step
        if not isinstance(part, int):
            start = pl.multiple_of(start, self.step)
        rows = pl.ds(start, self.step)
        return pltpu.make_async_copy(self.refs[0].at[rows], self.refs[1].at[rows], self.sems.at[part])

    def start(self):
        for part in range(self.refs[0].shape[0] // self.step):
            self.copy(part).start()


def call(kernel, operands, in_specs, outs, weight, step, extra=()):
    rows, width = weight.shape
    return pl.pallas_call(
        kernel,
        in_specs=in_specs,
        out_specs=[WHOLE] * len(outs),
        out_shape=[jax.ShapeDtypeStruct(*o) for o in outs],
        scratch_shapes=[
            pltpu.VMEM((rows, width), weight.dtype),
            pltpu.SemaphoreType.DMA((rows // step,)),
            *extra,
        ],
        compiler_params=pltpu.CompilerParams(vmem_limit_bytes=60 * 2**20),
        cost_estimate=pl.CostEstimate(
            flops=2 * rows * width * outs[0][0][0], bytes_accessed=2 * rows * width, transcendentals=0
        ),
    )(*operands)


def norm_kernel(parts, tokens, cotan, gain, x_hat, scale, blocks):
    normed, x_hat[...], inv_std = normalise(tokens[...], gain[...])
    scale[...] = jnp.broadcast_to(inv_std, scale.shape)
    cols = normed.shape[1] // parts
    for part in range(parts):
        span = slice(part * cols, (part + 1) * cols)
        blocks[part, 0] = normed[:, span]
        blocks[part, 1] = cotan[:, span]


def preact_kernel(step, count, *refs):
    pieces, (gain, weight, hidden, slope, normed, buffer, sems, total) = refs[:count], refs[count:]
    stream = Stream(weight, buffer, sems, step)
    stream.start()
    row = 0
    for piece in pieces:
        normed[row : row + piece.shape[0], :] = normalise(piece[...], gain[...])[0]
        row += piece.shape[0]
    total[...] = jnp.zeros_like(total)

    def body(part, carry):
        stream.copy(part).wait()
        span = pl.ds(pl.multiple_of(part * step, step), step)
        total[...] += contract(normed[:, span], buffer[span, :], ((1,), (0,)))
        return carry

    lax.fori_loop(0, weight.shape[0] // step, body, 0)
    hidden[...] = gelu_value(total[...]).astype(jnp.bfloat16)
    slope[...] = gelu_slope(total[...])


def hidgrad_kernel(step, span_of, count, *refs):
    pieces, (weight, slope, pre, buffer, sems, cotan) = refs[:count], refs[count:]
    stream = Stream(weight, buffer, sems, step)
    stream.start()
    row = 0
    for piece in pieces:
        cotan[row : row + piece.shape[0], :] = piece[...]
        row += piece.shape[0]

    def body(part, carry):
        for inner in range(span_of // step):
            stream.copy(part * (span_of // step) + inner).wait()
        span = pl.ds(pl.multiple_of(part * span_of, span_of), span_of)
        hid_grad = contract(buffer[span, :], cotan[...], ((1,), (1,))).T
        pre[:, span] = (hid_grad * slope[:, span]).astype(jnp.bfloat16)
        return carry

    lax.fori_loop(0, weight.shape[0] // span_of, body, 0)


def normgrad_kernel(step, pre, weight, normed, gain, partial, gain_part, buffer, sems):
    stream = Stream(weight, buffer, sems, step)
    stream.start()

    def body(part, carry):
        stream.copy(part).wait()
        span = pl.ds(pl.multiple_of(part * step, step), step)
        grad = contract(pre[...], buffer[span, :], ((1,), (1,)))
        partial[:, span] = grad.astype(jnp.bfloat16)
        x_hat = normed[:, span].astype(jnp.float32) / gain[:, span]
        gain_part[:, span] = jnp.sum(grad * x_hat, axis=0, keepdims=True)
        return carry

    lax.fori_loop(0, weight.shape[0] // step, body, 0)


def layer(tokens, norm_gain, up_weight, down_weight, out_grad):
    n_dp, n_mp = lax.axis_size("dp"), lax.axis_size("mp")
    chips = n_mp // 2
    rows, width = tokens.shape
    units = up_weight.shape[1]
    group = rows * n_mp
    cols = width // n_dp
    me = lax.axis_index("dp")
    factor = 1.0 / math.sqrt(group * n_dp)

    def along_ring(array, shift=1):
        return lax.ppermute(array, "mp", ring_perm(n_mp, shift))

    def across(array):
        return lax.ppermute(array, "mp", swap_perm(n_mp, 1))

    def replica(array, mask):
        return lax.ppermute(array, "dp", swap_perm(n_dp, mask))

    def spread(own):
        pieces = [own]
        for _ in range(1, chips):
            pieces.append(along_ring(pieces[-1]))
        return pieces, [across(p) for p in pieces]

    def gathered(own):
        mine, other = spread(own)
        return mine + other if rows % 16 == 0 else [jnp.concatenate(mine + other, axis=0)]

    def replicas(own, low):
        out = [own]
        for k in range(1, n_dp):
            bit = (k & -k) if low else 1 << (k.bit_length() - 1)
            out.append(replica(out[k ^ bit], bit))
        return out

    token_pieces = gathered(tokens)
    cotan_pieces = gathered(out_grad)
    gain_row = norm_gain.reshape(1, width)
    x_hat, scale, blocks = pl.pallas_call(
        functools.partial(norm_kernel, n_dp),
        in_specs=[WHOLE] * 3,
        out_specs=[WHOLE] * 3,
        out_shape=[
            jax.ShapeDtypeStruct((rows, width), jnp.float32),
            jax.ShapeDtypeStruct((rows, 128), jnp.float32),
            jax.ShapeDtypeStruct((n_dp, 2, rows, cols), jnp.bfloat16),
        ],
        name="ln",
    )(tokens, out_grad, gain_row)
    inv_std = scale[:, :1]

    def column_shards(k):
        both = lax.dynamic_index_in_dim(blocks, me ^ k, 0, keepdims=False)
        return replica(both, k) if k else both

    shard_list = [column_shards(k) for k in range(n_dp)]
    shard = jnp.stack(shard_list)
    shards_mine, shards_other = spread(shard)
    columns = jnp.stack([jnp.stack(shards_mine), jnp.stack(shards_other)])
    columns = columns.transpose(3, 2, 0, 1, 4, 5).reshape(2, -1, cols)
    normed_cols, cotan_cols = columns[0], columns[1]

    float_units, half_units = ((group, units), jnp.float32), ((group, units), jnp.bfloat16)
    half_width = ((group, width), jnp.bfloat16)
    step, count = chunk(width, 384, 128), len(token_pieces)
    hidden, slope, normed_all = call(
        functools.partial(preact_kernel, step, count),
        (*token_pieces, gain_row, up_weight),
        [WHOLE] * (count + 1) + [STAYS],
        (half_units, float_units, half_width),
        up_weight,
        step,
        (pltpu.VMEM(*float_units),),
    )
    span_of, count = chunk(units, 512, 128), len(cotan_pieces)
    step = chunk(span_of, 256, 128)
    (pre_grad,) = call(
        functools.partial(hidgrad_kernel, step, span_of, count),
        (*cotan_pieces, down_weight, slope),
        [WHOLE] * count + [STAYS, WHOLE],
        (half_units,),
        down_weight,
        step,
        (pltpu.VMEM(*half_width),),
    )
    step = chunk(width, 768, 128)
    partial, gain_grad = call(
        functools.partial(normgrad_kernel, step),
        (pre_grad, up_weight, normed_all, gain_row),
        [WHOLE, STAYS, WHOLE, WHOLE],
        (half_width, ((1, width), jnp.float32)),
        up_weight,
        step,
    )

    hidden_all = jnp.concatenate(replicas(hidden, True), axis=0)
    pre_all = jnp.concatenate(replicas(pre_grad, False), axis=0)

    gain_grad = gain_grad + across(gain_grad)
    shift = 1
    while shift < chips:
        gain_grad = gain_grad + along_ring(gain_grad, shift)
        shift *= 2
    for bit in range((n_dp - 1).bit_length()):
        gain_grad = gain_grad + replica(gain_grad, 1 << bit)
    gain_grad = gain_grad.reshape(width) * factor

    half = rows * chips
    total = partial[:half].astype(jnp.float32) + across(partial[half:]).astype(jnp.float32)
    parts = total.astype(jnp.bfloat16).reshape(chips, rows, width)
    norm_grad = total[:rows]
    for s in range(1, chips):
        norm_grad = norm_grad + along_ring(parts[s], -s).astype(jnp.float32)
    scaled = norm_gain * norm_grad
    input_grad = (
        scaled
        - jnp.mean(scaled, axis=1, keepdims=True)
        - x_hat * jnp.mean(scaled * x_hat, axis=1, keepdims=True)
    ) * inv_std

    down_grad = (contract(hidden_all, cotan_cols, ((0,), (0,))) * factor).astype(jnp.bfloat16)
    up_grad = (contract(normed_cols, pre_all, ((0,), (0,))) * factor).astype(jnp.bfloat16)
    return (input_grad.astype(jnp.bfloat16), up_grad, down_grad, gain_grad)


def solution(mesh):
    placed = (P(("dp", "mp"), None), P(), P(None, "mp"), P("mp", None), P(("dp", "mp"), None))
    return jax.shard_map(
        layer,
        mesh=mesh,
        in_specs=placed,
        out_specs=(P(("dp", "mp"), None), P("dp", "mp"), P("mp", "dp"), P()),
        check_vma=False,
    )
```

time: 174 us -> 171 us (0.983)
  Pallas kernels: 0 us -> 41.6 us
  matrix products: 50.7 us -> 10.7 us
  starting transfers between devices: 41.9 us -> 37.7 us
  other arithmetic: 7.04 us -> 3.56 us
  local copies, waits for them, and re-layouts: 1.8 us -> 4.58 us
    pallas_call x0 -> x4, Pallas kernels: none -> 41.6 us  [the longest x3 39.4 us: call(): pl.pallas_call(kernel, in_specs=in_specs, out_specs=[WHOLE] * len(outs),...]
    dot_general x5 -> x2, matrix products: 50.7 us -> 10.7 us  [contract(): lax.dot_general(a, b, (dims, ((), ())), preferred_element_type=jnp.float32)]
    ppermute x14, starting transfers between devices: 25.1 us -> 21.4 us  [along_ring(): return lax.ppermute(array, 'mp', ring_perm(n_mp, shift))]
    reduce_sum x2 -> x0, other arithmetic: 2.25 us -> none  [the longest x1 1.16 us: layer(): jnp.mean(centered * centered, axis=1, keepdims=True) + 1e-06]
    ppermute x14, waiting for transfers between devices: 36.8 us -> 38.6 us  [along_ring(): return lax.ppermute(array, 'mp', ring_perm(n_mp, shift))]
  transfers between devices with their start and end apart: 39 -> 39, of which waited for: 18 -> 17; matrix products, arithmetic and copies ran while one was open for 31% -> 7% of each run, Pallas kernels for 0% -> 24%
where the time goes in v1:
time: 171 us; the launch traced here: 170 us
  waiting for transfers between devices  70.9 us (41%)
  Pallas kernels  41.6 us (24%)
  starting transfers between devices  37.7 us (22%)
  matrix products  10.7 us (6%)
  local copies, waits for them, and re-layouts  4.58 us (3%)
  other arithmetic  3.56 us (2%)
    pallas_call x3, Pallas kernels, call(): pl.pallas_call(kernel, in_specs=in_specs, out_specs=[WHOLE] * len(outs),...  39.4 us
    ppermute x14, waiting for transfers between devices, along_ring(): return lax.ppermute(array, 'mp', ring_perm(n_mp, shift))  38.6 us
    ppermute x11, waiting for transfers between devices, replica(): return lax.ppermute(array, 'dp', swap_perm(n_dp, mask))  31.2 us
    ppermute x14, starting transfers between devices, along_ring(): return lax.ppermute(array, 'mp', ring_perm(n_mp, shift))  21.4 us
    ppermute x11, starting transfers between devices, replica(): return lax.ppermute(array, 'dp', swap_perm(n_dp, mask))  12.9 us
    dot_general x2, matrix products, contract(): lax.dot_general(a, b, (dims, ((), ())), preferred_element_type=jnp.float32)  10.7 us
  transfers between devices with their start and end apart: 39, of which 17 were waited for; matrix products, arithmetic and copies ran while one was open for 7% of the time, Pallas kernels for 24%

profile of v1, /device:TPU:0, one launch (start us, length us, event | category | flops | bytes accessed | tf_op | source)
XLA Modules:
  0.0 170.1 jit_solution(6428391705379633498)
XLA Ops:
  0.7 4.1 %collective-permute-start.7 = (bf16[16,6144]{1,0:T(8,128)(2,1)}, bf16[16,6144]{1,0:T(8,128)(2,1)S(1)}, u32[]{:S(2)}, u32[]{:S(2)}) collective-permute-start(bf16[16,6144]{1,0:T(8,128)(2,1)} %tokens.1), channel_id=1, source_target_pairs={{0,4},{1,5},{2,0},{3,1},{4,6},{5,7},{6,2},{7,3},{8,12},{9,13},{10,... | collective-permute-start | bytes 589832 | tf_op jit(solution)/shard_map/ppermute | solution.py:170
  4.8 2.2 %ln.1 = (f32[16,6144]{1,0:T(8,128)}, f32[16,128]{1,0:T(8,128)}, bf16[4,2,16,1536]{3,2,1,0:T(8,128)(2,1)}) custom-call(bf16[16,6144]{1,0:T(8,128)(2,1)} %tokens.1, bf16[16,6144]{1,0:T(8,128)(2,1)} %cotan.1, f32[1,6144]{1,0:T(1,128)} %bitcast.39), custom_call_target="tpu_custom_call" | custom-call | tf_op jit(solution)/shard_map/ln/pallas_call | solution.py:198
  7.0 1.1 constant_dynamic-slice_fusion
  8.0 2.5 %collective-permute-start.20 = (bf16[2,16,1536]{2,1,0:T(8,128)(2,1)S(1)}, bf16[2,16,1536]{2,1,0:T(8,128)(2,1)S(1)}, u32[]{:S(2)}, u32[]{:S(2)}) collective-permute-start(bf16[2,16,1536]{2,1,0:T(8,128)(2,1)S(1)} %get-tuple-element.33), channel_id=1, source_target_pairs={{0,24},{8,16},{16,8},{24,0},{1,25},{9,17},{17,9},{25,1},{2,26},{10... | collective-permute-start | bytes 294920 | tf_op jit(solution)/shard_map/ppermute | solution.py:176
  10.6 0.5 collective-permute-start.19
  11.1 0.5 collective-permute-start.18
  11.6 1.6 collective-permute-start
  13.2 0.3 collective-permute-start.8
  13.5 0.2 collective-permute-done.20
  13.7 1.9 %collective-permute-done.19 = bf16[2,16,1536]{2,1,0:T(8,128)(2,1)S(1)} collective-permute-done((bf16[2,16,1536]{2,1,0:T(8,128)(2,1)S(1)}, bf16[2,16,1536]{2,1,0:T(8,128)(2,1)S(1)}, u32[]{:S(2)}, u32[]{:S(2)}) %collective-permute-start.19) | collective-permute-done | bytes 98336 | tf_op jit(solution)/shard_map/ppermute | solution.py:176
  15.6 0.2 collective-permute-done.18
  15.9 1.6 collective-permute-start.21
  17.5 2.1 %collective-permute-done.refs_1_ = bf16[16,6144]{1,0:T(8,128)(2,1)S(1)} collective-permute-done((bf16[16,6144]{1,0:T(8,128)(2,1)}, bf16[16,6144]{1,0:T(8,128)(2,1)S(1)}, u32[]{:S(2)}, u32[]{:S(2)}) %collective-permute-start) | collective-permute-done | bytes 196640 | tf_op jit(solution)/shard_map/ppermute | solution.py:170
  19.6 2.5 %collective-permute-start.1 = (bf16[16,6144]{1,0:T(8,128)(2,1)S(1)}, bf16[16,6144]{1,0:T(8,128)(2,1)S(1)}, u32[]{:S(2)}, u32[]{:S(2)}) collective-permute-start(bf16[16,6144]{1,0:T(8,128)(2,1)S(1)} %collective-permute-done.refs_1_), channel_id=1, source_target_pairs={{0,4},{1,5},{2,0},{3,1},{4,6},{5,7},{6,2},{7,3},{8,12},{9,13},{10,... | collective-permute-start | bytes 589832 | tf_op jit(solution)/shard_map/ppermute | solution.py:170
  22.1 1.7 %collective-permute-done.8.refs_2_ = bf16[16,6144]{1,0:T(8,128)(2,1)S(1)} collective-permute-done((bf16[16,6144]{1,0:T(8,128)(2,1)S(1)}, bf16[16,6144]{1,0:T(8,128)(2,1)S(1)}, u32[]{:S(2)}, u32[]{:S(2)}) %collective-permute-start.8) | collective-permute-done | bytes 196640 | tf_op jit(solution)/shard_map/ppermute | solution.py:170
  23.8 2.5 %collective-permute-start.9 = (bf16[16,6144]{1,0:T(8,128)(2,1)S(1)}, bf16[16,6144]{1,0:T(8,128)(2,1)S(1)}, u32[]{:S(2)}, u32[]{:S(2)}) collective-permute-start(bf16[16,6144]{1,0:T(8,128)(2,1)S(1)} %collective-permute-done.8.refs_2_), channel_id=1, source_target_pairs={{0,4},{1,5},{2,0},{3,1},{4,6},{5,7},{6,2},{7,3},{8,12},{9,13},{10,... | collective-permute-start | bytes 589832 | tf_op jit(solution)/shard_map/ppermute | solution.py:170
  26.3 0.5 collective-permute-start.12
  26.8 9.6 %collective-permute-done.1.refs_2_ = bf16[16,6144]{1,0:T(8,128)(2,1)S(1)} collective-permute-done((bf16[16,6144]{1,0:T(8,128)(2,1)S(1)}, bf16[16,6144]{1,0:T(8,128)(2,1)S(1)}, u32[]{:S(2)}, u32[]{:S(2)}) %collective-permute-start.1) | collective-permute-done | bytes 196640 | tf_op jit(solution)/shard_map/ppermute | solution.py:170
  36.4 2.5 %collective-permute-start.2 = (bf16[16,6144]{1,0:T(8,128)(2,1)S(1)}, bf16[16,6144]{1,0:T(8,128)(2,1)S(1)}, u32[]{:S(2)}, u32[]{:S(2)}) collective-permute-start(bf16[16,6144]{1,0:T(8,128)(2,1)S(1)} %collective-permute-done.1.refs_2_), channel_id=1, source_target_pairs={{0,4},{1,5},{2,0},{3,1},{4,6},{5,7},{6,2},{7,3},{8,12},{9,13},{10,... | collective-permute-start | bytes 589832 | tf_op jit(solution)/shard_map/ppermute | solution.py:170
  38.9 1.6 collective-permute-done.9.refs_3_
  40.5 0.6 collective-permute-start.3
  41.2 0.4 collective-permute-start.5
  41.6 1.0 collective-permute-done.2.refs_3_
  42.6 2.9 %collective-permute-start.22 = (bf16[4,2,16,1536]{3,2,1,0:T(8,128)(2,1)S(1)}, bf16[4,2,16,1536]{3,2,1,0:T(8,128)(2,1)S(1)}, u32[]{:S(2)}, u32[]{:S(2)}) collective-permute-start(bf16[4,2,16,1536]{3,2,1,0:T(8,128)(2,1)S(1)} %collective-permute-done.21), channel_id=1, source_target_pairs={{0,4},{1,5},{2,0},{3,1},{4,6},{5,7},{6,2},{7,3},{8,12},{9,13},{10,... | collective-permute-start | bytes 1179656 | tf_op jit(solution)/shard_map/ppermute | solution.py:170
  45.5 0.7 copy-done.17
  46.2 12.3 %shard_map.84 = (bf16[128,2048]{1,0:T(8,128)(2,1)}, f32[128,2048]{1,0:T(8,128)}, bf16[128,6144]{1,0:T(8,128)(2,1)}) custom-call(bf16[16,6144]{1,0:T(8,128)(2,1)} %tokens.1, bf16[16,6144]{1,0:T(8,128)(2,1)} %copy-done.6, bf16[16,6144]{1,0:T(8,128)(2,1)} %copy-done.8, bf16[16,6144]{1,0:T(8,128)(2,1)} %copy-done.12, bf16[16,6144]{1,0:T(8,128)(2,1)} %copy-done.10, ...), custom_call_target="tpu_custom_call" | custom-call | flops 3221225472 | bytes 25165824 | tf_op jit(solution)/shard_map/pallas_call | solution.py:75
  58.7 0.6 copy-done.15
  59.4 13.0 %shard_map.85.pre = bf16[128,2048]{1,0:T(8,128)(2,1)} custom-call(bf16[16,6144]{1,0:T(8,128)(2,1)} %cotan.1, bf16[16,6144]{1,0:T(8,128)(2,1)} %copy-done.7, bf16[16,6144]{1,0:T(8,128)(2,1)} %copy-done.9, bf16[16,6144]{1,0:T(8,128)(2,1)} %copy-done.11, bf16[16,6144]{1,0:T(8,128)(2,1)} %copy-done.15, bf16[16,6144]{1,0:T(8,128)(2,1)} %copy-done.16, ...), custom_call_target="tpu_custom_call" | custom-call | flops 3221225472 | bytes 25165824 | tf_op jit(solution)/shard_map/pallas_call | solution.py:75
  72.4 14.1 %shard_map.86 = (bf16[128,6144]{1,0:T(8,128)(2,1)}, f32[1,6144]{1,0:T(1,128)}) custom-call(bf16[128,2048]{1,0:T(8,128)(2,1)} %shard_map.85.pre, bf16[6144,2048]{1,0:T(8,128)(2,1)} %weight.1, bf16[128,6144]{1,0:T(8,128)(2,1)} %get-tuple-element.13.normed, f32[1,6144]{1,0:T(1,128)} %bitcast.41), custom_call_target="tpu_custom_call" | custom-call | flops 3221225472 | bytes 25165824 | tf_op jit(solution)/shard_map/pallas_call | solution.py:75
  86.5 0.5 collective-permute-start.34
  87.0 1.1 collective-permute-done.34
  88.1 0.8 add.48
  88.9 3.8 %collective-permute-done.35 = f32[1,6144]{1,0:T(1,128)S(1)} collective-permute-done((f32[1,6144]{1,0:T(1,128)S(1)}, f32[1,6144]{1,0:T(1,128)S(1)}, u32[]{:S(2)}, u32[]{:S(2)}) %collective-permute-start.35) | collective-permute-done | bytes 24608 | tf_op jit(solution)/shard_map/ppermute | solution.py:170
  92.8 5.6 %collective-permute-done.36 = f32[1,6144]{1,0:T(1,128)S(1)} collective-permute-done((f32[1,6144]{1,0:T(1,128)S(1)}, f32[1,6144]{1,0:T(1,128)S(1)}, u32[]{:S(2)}, u32[]{:S(2)}) %collective-permute-start.36) | collective-permute-done | bytes 24608 | tf_op jit(solution)/shard_map/ppermute | solution.py:170
  98.5 1.6 collective-permute-start.37
  100.0 2.3 %collective-permute-done.37 = f32[1,6144]{1,0:T(1,128)S(1)} collective-permute-done((f32[1,6144]{1,0:T(1,128)S(1)}, f32[1,6144]{1,0:T(1,128)S(1)}, u32[]{:S(2)}, u32[]{:S(2)}) %collective-permute-start.37) | collective-permute-done | bytes 24608 | tf_op jit(solution)/shard_map/ppermute | solution.py:176
  102.4 1.6 collective-permute-start.38
  104.2 0.5 collective-permute-start.25
  104.7 1.5 collective-permute-start.28
  106.1 1.3 slice.33
  107.6 0.6 add_multiply_fusion
  108.3 10.8 %collective-permute-done.23 = bf16[4,2,16,1536]{3,2,1,0:T(8,128)(2,1)S(1)} collective-permute-done((bf16[4,2,16,1536]{3,2,1,0:T(8,128)(2,1)S(1)}, bf16[4,2,16,1536]{3,2,1,0:T(8,128)(2,1)S(1)}, u32[]{:S(2)}, u32[]{:S(2)}) %collective-permute-start.23) | collective-permute-done | bytes 393248 | tf_op jit(solution)/shard_map/ppermute | solution.py:170
  119.1 0.2 maximum_bitcast_fusion.1
  119.3 0.6 collective-permute-start.27
  119.9 0.2 convert_add_fusion
  120.1 0.2 copy-done.19
  120.3 0.5 collective-permute-start.32
  120.9 2.9 %collective-permute-start.17 = (bf16[16,6144]{1,0:T(8,128)(2,1)S(1)}, bf16[16,6144]{1,0:T(8,128)(2,1)S(1)}, u32[]{:S(2)}, u32[]{:S(2)}) collective-permute-start(bf16[16,6144]{1,0:T(8,128)(2,1)S(1)} %get-tuple-element.28), channel_id=1, source_target_pairs={{0,4},{1,5},{2,0},{3,1},{4,6},{5,7},{6,2},{7,3},{8,12},{9,13},{10,... | collective-permute-start | bytes 589832 | tf_op jit(solution)/shard_map/ppermute | solution.py:170
  123.8 0.3 collective-permute-start.16
  124.1 0.2 maximum_bitcast_fusion.2
  124.3 0.3 maximum_bitcast_fusion
  124.6 0.2 fusion.23
  125.1 1.6 collective-permute-start.29
  126.7 8.4 %collective-permute-done.32 = bf16[128,2048]{1,0:T(8,128)(2,1)S(1)} collective-permute-done((bf16[128,2048]{1,0:T(8,128)(2,1)S(1)}, bf16[128,2048]{1,0:T(8,128)(2,1)S(1)}, u32[]{:S(2)}, u32[]{:S(2)}) %collective-permute-start.32) | collective-permute-done | bytes 524320 | tf_op jit(solution)/shard_map/ppermute | solution.py:176
  135.1 0.6 collective-permute-start.31
  135.7 2.3 %collective-permute-done.15 = bf16[16,6144]{1,0:T(8,128)(2,1)S(1)} collective-permute-done((bf16[16,6144]{1,0:T(8,128)(2,1)S(1)}, bf16[16,6144]{1,0:T(8,128)(2,1)S(1)}, u32[]{:S(2)}, u32[]{:S(2)}) %collective-permute-start.15) | collective-permute-done | bytes 196640 | tf_op jit(solution)/shard_map/ppermute | solution.py:170
  138.0 1.5 collective-permute-start.30
  139.5 0.6 collective-permute-start.33
  140.1 0.3 fusion.21
  140.4 0.8 multiply_convert_fusion.2
  141.2 8.7 %collective-permute-done.31 = bf16[128,2048]{1,0:T(8,128)(2,1)S(1)} collective-permute-done((bf16[128,2048]{1,0:T(8,128)(2,1)S(1)}, bf16[128,2048]{1,0:T(8,128)(2,1)S(1)}, u32[]{:S(2)}, u32[]{:S(2)}) %collective-permute-start.31) | collective-permute-done | bytes 524320 | tf_op jit(solution)/shard_map/ppermute | solution.py:176
  149.9 9.5 %collective-permute-done.33 = bf16[128,2048]{1,0:T(8,128)(2,1)S(1)} collective-permute-done((bf16[128,2048]{1,0:T(8,128)(2,1)S(1)}, bf16[128,2048]{1,0:T(8,128)(2,1)S(1)}, u32[]{:S(2)}, u32[]{:S(2)}) %collective-permute-start.33) | collective-permute-done | bytes 524320 | tf_op jit(solution)/shard_map/ppermute | solution.py:176
  159.4 5.4 %multiply_convert_fusion = bf16[2048,1536]{1,0:T(8,128)(2,1)} fusion(bf16[512,1536]{1,0:T(8,128)(2,1)S(1)} %bitcast.31, bf16[128,2048]{1,0:T(8,128)(2,1)S(1)} %collective-permute-done.33, bf16[128,2048]{1,0:T(8,128)(2,1)S(1)} %collective-permute-done.32, bf16[128,2048]{1,0:T(8,128)(2,1)S(1)} %collective-permute-done.31, bf16[128,2048]{1,0:T(8,128)(2,1)S(1)} %copy-done.19), kind=kOutput, calls=%fused_computation | convolution fusion | flops 3235905536 | bytes 9961472 | tf_op jit(solution)/shard_map/dot_general | solution.py:35
  164.7 5.4 %multiply_convert_fusion.1 = bf16[1536,2048]{1,0:T(8,128)(2,1)} fusion(bf16[512,1536]{1,0:T(8,128)(2,1)S(1)} %bitcast.30, bf16[128,2048]{1,0:T(8,128)(2,1)S(1)} %collective-permute-done.30, bf16[128,2048]{1,0:T(8,128)(2,1)S(1)} %collective-permute-done.29, bf16[128,2048]{1,0:T(8,128)(2,1)S(1)} %collective-permute-done.28, bf16[128,2048]{1,0:T(8,128)(2,1)S(1)} %copy-done), kind=kOutput, calls=%fused_computation.1 | convolution fusion | flops 3235905536 | bytes 9961472 | tf_op jit(solution)/shard_map/dot_general | solution.py:35
  (80 shorter events, 1.2 us)
Async XLA Ops:
  0.6 16.9 %copy-start.3 = (bf16[16,6144]{1,0:T(8,128)(2,1)S(1)}, bf16[16,6144]{1,0:T(8,128)(2,1)}, u32[]{:S(2)}) copy-start(bf16[16,6144]{1,0:T(8,128)(2,1)} %tokens.1) | copy-start | bytes 589828
  0.6 39.9 %copy-start.4 = (bf16[16,6144]{1,0:T(8,128)(2,1)S(1)}, bf16[16,6144]{1,0:T(8,128)(2,1)}, u32[]{:S(2)}) copy-start(bf16[16,6144]{1,0:T(8,128)(2,1)} %cotan.1) | copy-start | bytes 589828
  0.7 12.5 %collective-permute-start.7 = (bf16[16,6144]{1,0:T(8,128)(2,1)}, bf16[16,6144]{1,0:T(8,128)(2,1)S(1)}, u32[]{:S(2)}, u32[]{:S(2)}) collective-permute-start(bf16[16,6144]{1,0:T(8,128)(2,1)} %tokens.1), channel_id=1, source_target_pairs={{0,4},{1,5},{2,0},{3,1},{4,6},{5,7},{6,2},{7,3},{8,12},{9,13},{10,... | collective-permute-start | bytes 589832 | tf_op jit(solution)/shard_map/ppermute | solution.py:170
  8.0 5.7 %collective-permute-start.20 = (bf16[2,16,1536]{2,1,0:T(8,128)(2,1)S(1)}, bf16[2,16,1536]{2,1,0:T(8,128)(2,1)S(1)}, u32[]{:S(2)}, u32[]{:S(2)}) collective-permute-start(bf16[2,16,1536]{2,1,0:T(8,128)(2,1)S(1)} %get-tuple-element.33), channel_id=1, source_target_pairs={{0,24},{8,16},{16,8},{24,0},{1,25},{9,17},{17,9},{25,1},{2,26},{10... | collective-permute-start | bytes 294920 | tf_op jit(solution)/shard_map/ppermute | solution.py:176
  10.6 5.0 %collective-permute-start.19 = (bf16[2,16,1536]{2,1,0:T(8,128)(2,1)S(1)}, bf16[2,16,1536]{2,1,0:T(8,128)(2,1)S(1)}, u32[]{:S(2)}, u32[]{:S(2)}) collective-permute-start(bf16[2,16,1536]{2,1,0:T(8,128)(2,1)S(1)} %get-tuple-element.34), channel_id=1, source_target_pairs={{0,16},{8,24},{16,0},{24,8},{1,17},{9,25},{17,1},{25,9},{2,18},{10... | collective-permute-start | bytes 294920 | tf_op jit(solution)/shard_map/ppermute | solution.py:176
  11.1 4.7 %collective-permute-start.18 = (bf16[2,16,1536]{2,1,0:T(8,128)(2,1)S(1)}, bf16[2,16,1536]{2,1,0:T(8,128)(2,1)S(1)}, u32[]{:S(2)}, u32[]{:S(2)}) collective-permute-start(bf16[2,16,1536]{2,1,0:T(8,128)(2,1)S(1)} %get-tuple-element.35), channel_id=1, source_target_pairs={{0,8},{8,0},{16,24},{24,16},{1,9},{9,1},{17,25},{25,17},{2,10},{10... | collective-permute-start | bytes 294920 | tf_op jit(solution)/shard_map/ppermute | solution.py:176
  11.6 8.0 %collective-permute-start = (bf16[16,6144]{1,0:T(8,128)(2,1)}, bf16[16,6144]{1,0:T(8,128)(2,1)S(1)}, u32[]{:S(2)}, u32[]{:S(2)}) collective-permute-start(bf16[16,6144]{1,0:T(8,128)(2,1)} %cotan.1), channel_id=1, source_target_pairs={{0,4},{1,5},{2,0},{3,1},{4,6},{5,7},{6,2},{7,3},{8,12},{9,13},{10,... | collective-permute-start | bytes 589832 | tf_op jit(solution)/shard_map/ppermute | solution.py:170
  13.2 33.0 %copy-start.6 = (bf16[16,6144]{1,0:T(8,128)(2,1)}, bf16[16,6144]{1,0:T(8,128)(2,1)S(1)}, u32[]{:S(2)}) copy-start(bf16[16,6144]{1,0:T(8,128)(2,1)S(1)} %collective-permute-done.7.refs_1_) | copy-start | bytes 589828
  13.2 10.6 %collective-permute-start.8 = (bf16[16,6144]{1,0:T(8,128)(2,1)S(1)}, bf16[16,6144]{1,0:T(8,128)(2,1)S(1)}, u32[]{:S(2)}, u32[]{:S(2)}) collective-permute-start(bf16[16,6144]{1,0:T(8,128)(2,1)S(1)} %collective-permute-done.7.refs_1_), channel_id=1, source_target_pairs={{0,4},{1,5},{2,0},{3,1},{4,6},{5,7},{6,2},{7,3},{8,12},{9,13},{10,... | collective-permute-start | bytes 589832 | tf_op jit(solution)/shard_map/ppermute | solution.py:170
  15.9 25.2 %collective-permute-start.21 = (bf16[4,2,16,1536]{3,2,1,0:T(8,128)(2,1)S(1)}, bf16[4,2,16,1536]{3,2,1,0:T(8,128)(2,1)S(1)}, u32[]{:S(2)}, u32[]{:S(2)}) collective-permute-start(bf16[4,2,16,1536]{3,2,1,0:T(8,128)(2,1)S(1)} %get-tuple-element.31), channel_id=1, source_target_pairs={{0,4},{1,5},{2,0},{3,1},{4,6},{5,7},{6,2},{7,3},{8,12},{9,13},{10,... | collective-permute-start | bytes 1179656 | tf_op jit(solution)/shard_map/ppermute | solution.py:170
  17.5 8.8 %collective-permute-start.10 = (bf16[16,6144]{1,0:T(8,128)(2,1)S(1)}, bf16[16,6144]{1,0:T(8,128)(2,1)S(1)}, u32[]{:S(2)}, u32[]{:S(2)}) collective-permute-start(bf16[16,6144]{1,0:T(8,128)(2,1)S(1)} %copy-done.3), channel_id=1, source_target_pairs={{0,1},{1,0},{2,3},{3,2},{4,5},{5,4},{6,7},{7,6},{8,9},{9,8},{10,11... | collective-permute-start | bytes 589832 | tf_op jit(solution)/shard_map/ppermute | solution.py:173
  19.6 39.0 %copy-start.7 = (bf16[16,6144]{1,0:T(8,128)(2,1)}, bf16[16,6144]{1,0:T(8,128)(2,1)S(1)}, u32[]{:S(2)}) copy-start(bf16[16,6144]{1,0:T(8,128)(2,1)S(1)} %collective-permute-done.refs_1_) | copy-start | bytes 589828
  19.6 16.9 %collective-permute-start.1 = (bf16[16,6144]{1,0:T(8,128)(2,1)S(1)}, bf16[16,6144]{1,0:T(8,128)(2,1)S(1)}, u32[]{:S(2)}, u32[]{:S(2)}) collective-permute-start(bf16[16,6144]{1,0:T(8,128)(2,1)S(1)} %collective-permute-done.refs_1_), channel_id=1, source_target_pairs={{0,4},{1,5},{2,0},{3,1},{4,6},{5,7},{6,2},{7,3},{8,12},{9,13},{10,... | collective-permute-start | bytes 589832 | tf_op jit(solution)/shard_map/ppermute | solution.py:170
  23.8 22.4 %copy-start.8 = (bf16[16,6144]{1,0:T(8,128)(2,1)}, bf16[16,6144]{1,0:T(8,128)(2,1)S(1)}, u32[]{:S(2)}) copy-start(bf16[16,6144]{1,0:T(8,128)(2,1)S(1)} %collective-permute-done.8.refs_2_) | copy-start | bytes 589828
  23.8 16.7 %collective-permute-start.9 = (bf16[16,6144]{1,0:T(8,128)(2,1)S(1)}, bf16[16,6144]{1,0:T(8,128)(2,1)S(1)}, u32[]{:S(2)}, u32[]{:S(2)}) collective-permute-start(bf16[16,6144]{1,0:T(8,128)(2,1)S(1)} %collective-permute-done.8.refs_2_), channel_id=1, source_target_pairs={{0,4},{1,5},{2,0},{3,1},{4,6},{5,7},{6,2},{7,3},{8,12},{9,13},{10,... | collective-permute-start | bytes 589832 | tf_op jit(solution)/shard_map/ppermute | solution.py:170
  26.3 14.2 %collective-permute-start.11 = (bf16[16,6144]{1,0:T(8,128)(2,1)S(1)}, bf16[16,6144]{1,0:T(8,128)(2,1)S(1)}, u32[]{:S(2)}, u32[]{:S(2)}) collective-permute-start(bf16[16,6144]{1,0:T(8,128)(2,1)S(1)} %collective-permute-done.7.refs_1_), channel_id=1, source_target_pairs={{0,1},{1,0},{2,3},{3,2},{4,5},{5,4},{6,7},{7,6},{8,9},{9,8},{10,11... | collective-permute-start | bytes 589832 | tf_op jit(solution)/shard_map/ppermute | solution.py:173
  26.3 19.9 %copy-start.10 = (bf16[16,6144]{1,0:T(8,128)(2,1)}, bf16[16,6144]{1,0:T(8,128)(2,1)S(1)}, u32[]{:S(2)}) copy-start(bf16[16,6144]{1,0:T(8,128)(2,1)S(1)} %collective-permute-done.10.refs_4_) | copy-start | bytes 589828
  26.3 14.9 %collective-permute-start.12 = (bf16[16,6144]{1,0:T(8,128)(2,1)S(1)}, bf16[16,6144]{1,0:T(8,128)(2,1)S(1)}, u32[]{:S(2)}, u32[]{:S(2)}) collective-permute-start(bf16[16,6144]{1,0:T(8,128)(2,1)S(1)} %collective-permute-done.8.refs_2_), channel_id=1, source_target_pairs={{0,1},{1,0},{2,3},{3,2},{4,5},{5,4},{6,7},{7,6},{8,9},{9,8},{10,11... | collective-permute-start | bytes 589832 | tf_op jit(solution)/shard_map/ppermute | solution.py:173
  36.4 22.1 %copy-start.9 = (bf16[16,6144]{1,0:T(8,128)(2,1)}, bf16[16,6144]{1,0:T(8,128)(2,1)S(1)}, u32[]{:S(2)}) copy-start(bf16[16,6144]{1,0:T(8,128)(2,1)S(1)} %collective-permute-done.1.refs_2_) | copy-start | bytes 589828
  36.4 6.2 %collective-permute-start.2 = (bf16[16,6144]{1,0:T(8,128)(2,1)S(1)}, bf16[16,6144]{1,0:T(8,128)(2,1)S(1)}, u32[]{:S(2)}, u32[]{:S(2)}) collective-permute-start(bf16[16,6144]{1,0:T(8,128)(2,1)S(1)} %collective-permute-done.1.refs_2_), channel_id=1, source_target_pairs={{0,4},{1,5},{2,0},{3,1},{4,6},{5,7},{6,2},{7,3},{8,12},{9,13},{10,... | collective-permute-start | bytes 589832 | tf_op jit(solution)/shard_map/ppermute | solution.py:170
  40.5 5.7 %copy-start.12 = (bf16[16,6144]{1,0:T(8,128)(2,1)}, bf16[16,6144]{1,0:T(8,128)(2,1)S(1)}, u32[]{:S(2)}) copy-start(bf16[16,6144]{1,0:T(8,128)(2,1)S(1)} %collective-permute-done.9.refs_3_) | copy-start | bytes 589828
  40.5 5.0 %collective-permute-start.13 = (bf16[16,6144]{1,0:T(8,128)(2,1)S(1)}, bf16[16,6144]{1,0:T(8,128)(2,1)S(1)}, u32[]{:S(2)}, u32[]{:S(2)}) collective-permute-start(bf16[16,6144]{1,0:T(8,128)(2,1)S(1)} %collective-permute-done.9.refs_3_), channel_id=1, source_target_pairs={{0,1},{1,0},{2,3},{3,2},{4,5},{5,4},{6,7},{7,6},{8,9},{9,8},{10,11... | collective-permute-start | bytes 589832 | tf_op jit(solution)/shard_map/ppermute | solution.py:173
  40.5 5.7 %copy-start.13 = (bf16[16,6144]{1,0:T(8,128)(2,1)}, bf16[16,6144]{1,0:T(8,128)(2,1)S(1)}, u32[]{:S(2)}) copy-start(bf16[16,6144]{1,0:T(8,128)(2,1)S(1)} %collective-permute-done.11.refs_5_) | copy-start | bytes 589828
  40.5 18.1 %collective-permute-start.3 = (bf16[16,6144]{1,0:T(8,128)(2,1)S(1)}, bf16[16,6144]{1,0:T(8,128)(2,1)S(1)}, u32[]{:S(2)}, u32[]{:S(2)}) collective-permute-start(bf16[16,6144]{1,0:T(8,128)(2,1)S(1)} %copy-done.4), channel_id=1, source_target_pairs={{0,1},{1,0},{2,3},{3,2},{4,5},{5,4},{6,7},{7,6},{8,9},{9,8},{10,11... | collective-permute-start | bytes 589832 | tf_op jit(solution)/shard_map/ppermute | solution.py:173
  41.1 17.5 %collective-permute-start.4 = (bf16[16,6144]{1,0:T(8,128)(2,1)S(1)}, bf16[16,6144]{1,0:T(8,128)(2,1)S(1)}, u32[]{:S(2)}, u32[]{:S(2)}) collective-permute-start(bf16[16,6144]{1,0:T(8,128)(2,1)S(1)} %collective-permute-done.refs_1_), channel_id=1, source_target_pairs={{0,1},{1,0},{2,3},{3,2},{4,5},{5,4},{6,7},{7,6},{8,9},{9,8},{10,11... | collective-permute-start | bytes 589832 | tf_op jit(solution)/shard_map/ppermute | solution.py:173
  41.2 5.0 %copy-start.14 = (bf16[16,6144]{1,0:T(8,128)(2,1)}, bf16[16,6144]{1,0:T(8,128)(2,1)S(1)}, u32[]{:S(2)}) copy-start(bf16[16,6144]{1,0:T(8,128)(2,1)S(1)} %collective-permute-done.12.refs_6_) | copy-start | bytes 589828
  41.2 17.5 %collective-permute-start.5 = (bf16[16,6144]{1,0:T(8,128)(2,1)S(1)}, bf16[16,6144]{1,0:T(8,128)(2,1)}, u32[]{:S(2)}, u32[]{:S(2)}) collective-permute-start(bf16[16,6144]{1,0:T(8,128)(2,1)S(1)} %collective-permute-done.1.refs_2_), channel_id=1, source_target_pairs={{0,1},{1,0},{2,3},{3,2},{4,5},{5,4},{6,7},{7,6},{8,9},{9,8},{10,11... | collective-permute-start | bytes 589832 | tf_op jit(solution)/shard_map/ppermute | solution.py:173
  42.6 16.0 %copy-start.11 = (bf16[16,6144]{1,0:T(8,128)(2,1)}, bf16[16,6144]{1,0:T(8,128)(2,1)S(1)}, u32[]{:S(2)}) copy-start(bf16[16,6144]{1,0:T(8,128)(2,1)S(1)} %collective-permute-done.2.refs_3_) | copy-start | bytes 589828
  42.6 64.8 %collective-permute-start.22 = (bf16[4,2,16,1536]{3,2,1,0:T(8,128)(2,1)S(1)}, bf16[4,2,16,1536]{3,2,1,0:T(8,128)(2,1)S(1)}, u32[]{:S(2)}, u32[]{:S(2)}) collective-permute-start(bf16[4,2,16,1536]{3,2,1,0:T(8,128)(2,1)S(1)} %collective-permute-done.21), channel_id=1, source_target_pairs={{0,4},{1,5},{2,0},{3,1},{4,6},{5,7},{6,2},{7,3},{8,12},{9,13},{10,... | collective-permute-start | bytes 1179656 | tf_op jit(solution)/shard_map/ppermute | solution.py:170
  45.5 0.7 copy-start.17
  46.2 12.5 %collective-permute-start.6 = (bf16[16,6144]{1,0:T(8,128)(2,1)S(1)}, bf16[16,6144]{1,0:T(8,128)(2,1)}, u32[]{:S(2)}, u32[]{:S(2)}) collective-permute-start(bf16[16,6144]{1,0:T(8,128)(2,1)S(1)} %collective-permute-done.2.refs_3_), channel_id=1, source_target_pairs={{0,1},{1,0},{2,3},{3,2},{4,5},{5,4},{6,7},{7,6},{8,9},{9,8},{10,11... | collective-permute-start | bytes 589832 | tf_op jit(solution)/shard_map/ppermute | solution.py:173
  58.6 0.7 copy-start.15
  58.6 0.7 copy-start.16
  72.3 31.6 %copy-start.18 = (f32[16,128]{1,0:T(8,128)S(1)}, f32[16,128]{1,0:T(8,128)}, u32[]{:S(2)}) copy-start(f32[16,128]{1,0:T(8,128)} %get-tuple-element.16) | copy-start | bytes 24580
  72.4 32.3 %copy-start = (bf16[128,2048]{1,0:T(8,128)(2,1)S(1)}, bf16[128,2048]{1,0:T(8,128)(2,1)}, u32[]{:S(2)}) copy-start(bf16[128,2048]{1,0:T(8,128)(2,1)} %shard_map.85.pre) | copy-start | bytes 1572868
  86.5 1.6 collective-permute-start.34
  88.8 3.9 %collective-permute-start.35 = (f32[1,6144]{1,0:T(1,128)S(1)}, f32[1,6144]{1,0:T(1,128)S(1)}, u32[]{:S(2)}, u32[]{:S(2)}) collective-permute-start(f32[1,6144]{1,0:T(1,128)S(1)} %add.48), channel_id=1, source_target_pairs={{0,4},{1,5},{2,0},{3,1},{4,6},{5,7},{6,2},{7,3},{8,12},{9,13},{10,... | collective-permute-start | bytes 73736 | tf_op jit(solution)/shard_map/ppermute | solution.py:170
  92.7 5.7 %collective-permute-start.36 = (f32[1,6144]{1,0:T(1,128)S(1)}, f32[1,6144]{1,0:T(1,128)S(1)}, u32[]{:S(2)}, u32[]{:S(2)}) collective-permute-start(f32[1,6144]{1,0:T(1,128)S(1)} %add.49), channel_id=1, source_target_pairs={{0,6},{1,7},{2,4},{3,5},{4,2},{5,3},{6,0},{7,1},{8,14},{9,15},{10,... | collective-permute-start | bytes 73736 | tf_op jit(solution)/shard_map/ppermute | solution.py:170
  98.5 3.9 %collective-permute-start.37 = (f32[1,6144]{1,0:T(1,128)S(1)}, f32[1,6144]{1,0:T(1,128)S(1)}, u32[]{:S(2)}, u32[]{:S(2)}) collective-permute-start(f32[1,6144]{1,0:T(1,128)S(1)} %add.50), channel_id=1, source_target_pairs={{0,8},{8,0},{16,24},{24,16},{1,9},{9,1},{17,25},{25,17},{2,10},{10... | collective-permute-start | bytes 73736 | tf_op jit(solution)/shard_map/ppermute | solution.py:176
  102.4 5.2 %collective-permute-start.38 = (f32[1,6144]{1,0:T(1,128)S(1)}, f32[1,6144]{1,0:T(1,128)S(1)}, u32[]{:S(2)}, u32[]{:S(2)}) collective-permute-start(f32[1,6144]{1,0:T(1,128)S(1)} %add.51), channel_id=1, source_target_pairs={{0,16},{8,24},{16,0},{24,8},{1,17},{9,25},{17,1},{25,9},{2,18},{10... | collective-permute-start | bytes 73736 | tf_op jit(solution)/shard_map/ppermute | solution.py:176
  104.1 16.0 %collective-permute-start.24 = (bf16[4,2,16,1536]{3,2,1,0:T(8,128)(2,1)S(1)}, bf16[4,2,16,1536]{3,2,1,0:T(8,128)(2,1)S(1)}, u32[]{:S(2)}, u32[]{:S(2)}) collective-permute-start(bf16[4,2,16,1536]{3,2,1,0:T(8,128)(2,1)S(1)} %get-tuple-element.31), channel_id=1, source_target_pairs={{0,1},{1,0},{2,3},{3,2},{4,5},{5,4},{6,7},{7,6},{8,9},{9,8},{10,11... | collective-permute-start | bytes 1179656 | tf_op jit(solution)/shard_map/ppermute | solution.py:173
  104.2 16.7 %collective-permute-start.25 = (bf16[4,2,16,1536]{3,2,1,0:T(8,128)(2,1)S(1)}, bf16[4,2,16,1536]{3,2,1,0:T(8,128)(2,1)S(1)}, u32[]{:S(2)}, u32[]{:S(2)}) collective-permute-start(bf16[4,2,16,1536]{3,2,1,0:T(8,128)(2,1)S(1)} %collective-permute-done.21), channel_id=1, source_target_pairs={{0,1},{1,0},{2,3},{3,2},{4,5},{5,4},{6,7},{7,6},{8,9},{9,8},{10,11... | collective-permute-start | bytes 1179656 | tf_op jit(solution)/shard_map/ppermute | solution.py:173
  104.7 20.4 %collective-permute-start.28 = (bf16[128,2048]{1,0:T(8,128)(2,1)S(1)}, bf16[128,2048]{1,0:T(8,128)(2,1)S(1)}, u32[]{:S(2)}, u32[]{:S(2)}) collective-permute-start(bf16[128,2048]{1,0:T(8,128)(2,1)S(1)} %copy-done), channel_id=1, source_target_pairs={{0,8},{8,0},{16,24},{24,16},{1,9},{9,1},{17,25},{25,17},{2,10},{10... | collective-permute-start | bytes 1572872 | tf_op jit(solution)/shard_map/ppermute | solution.py:176
  106.1 13.7 %copy-start.2 = (bf16[128,6144]{1,0:T(8,128)(2,1)S(1)}, bf16[128,6144]{1,0:T(8,128)(2,1)}, u32[]{:S(2)}) copy-start(bf16[128,6144]{1,0:T(8,128)(2,1)} %get-tuple-element.14) | copy-start | bytes 4718596
  107.5 11.8 %collective-permute-start.14 = (bf16[64,6144]{1,0:T(8,128)(2,1)S(1)}, bf16[64,6144]{1,0:T(8,128)(2,1)S(1)}, u32[]{:S(2)}, u32[]{:S(2)}) collective-permute-start(bf16[64,6144]{1,0:T(8,128)(2,1)S(1)} %slice.33), channel_id=1, source_target_pairs={{0,1},{1,0},{2,3},{3,2},{4,5},{5,4},{6,7},{7,6},{8,9},{9,8},{10,11... | collective-permute-start | bytes 2359304 | tf_op jit(solution)/shard_map/ppermute | solution.py:173
  107.6 11.5 %collective-permute-start.23 = (bf16[4,2,16,1536]{3,2,1,0:T(8,128)(2,1)S(1)}, bf16[4,2,16,1536]{3,2,1,0:T(8,128)(2,1)S(1)}, u32[]{:S(2)}, u32[]{:S(2)}) collective-permute-start(bf16[4,2,16,1536]{3,2,1,0:T(8,128)(2,1)S(1)} %collective-permute-done.22), channel_id=1, source_target_pairs={{0,4},{1,5},{2,0},{3,1},{4,6},{5,7},{6,2},{7,3},{8,12},{9,13},{10,... | collective-permute-start | bytes 1179656 | tf_op jit(solution)/shard_map/ppermute | solution.py:170
  119.1 1.8 %collective-permute-start.26 = (bf16[4,2,16,1536]{3,2,1,0:T(8,128)(2,1)S(1)}, bf16[4,2,16,1536]{3,2,1,0:T(8,128)(2,1)S(1)}, u32[]{:S(2)}, u32[]{:S(2)}) collective-permute-start(bf16[4,2,16,1536]{3,2,1,0:T(8,128)(2,1)S(1)} %collective-permute-done.22), channel_id=1, source_target_pairs={{0,1},{1,0},{2,3},{3,2},{4,5},{5,4},{6,7},{7,6},{8,9},{9,8},{10,11... | collective-permute-start | bytes 1179656 | tf_op jit(solution)/shard_map/ppermute | solution.py:173
  119.3 1.0 copy-start.19
  119.3 4.5 %collective-permute-start.27 = (bf16[4,2,16,1536]{3,2,1,0:T(8,128)(2,1)S(1)}, bf16[4,2,16,1536]{3,2,1,0:T(8,128)(2,1)S(1)}, u32[]{:S(2)}, u32[]{:S(2)}) collective-permute-start(bf16[4,2,16,1536]{3,2,1,0:T(8,128)(2,1)S(1)} %collective-permute-done.23), channel_id=1, source_target_pairs={{0,1},{1,0},{2,3},{3,2},{4,5},{5,4},{6,7},{7,6},{8,9},{9,8},{10,11... | collective-permute-start | bytes 1179656 | tf_op jit(solution)/shard_map/ppermute | solution.py:173
  120.3 14.8 %collective-permute-start.32 = (bf16[128,2048]{1,0:T(8,128)(2,1)S(1)}, bf16[128,2048]{1,0:T(8,128)(2,1)S(1)}, u32[]{:S(2)}, u32[]{:S(2)}) collective-permute-start(bf16[128,2048]{1,0:T(8,128)(2,1)S(1)} %copy-done.19), channel_id=1, source_target_pairs={{0,16},{8,24},{16,0},{24,8},{1,17},{9,25},{17,1},{25,9},{2,18},{10... | collective-permute-start | bytes 1572872 | tf_op jit(solution)/shard_map/ppermute | solution.py:176
  120.9 17.1 %collective-permute-start.15 = (bf16[16,6144]{1,0:T(8,128)(2,1)S(1)}, bf16[16,6144]{1,0:T(8,128)(2,1)S(1)}, u32[]{:S(2)}, u32[]{:S(2)}) collective-permute-start(bf16[16,6144]{1,0:T(8,128)(2,1)S(1)} %get-tuple-element.27), channel_id=1, source_target_pairs={{0,2},{1,3},{2,6},{3,7},{4,0},{5,1},{6,4},{7,5},{8,10},{9,11},{10,... | collective-permute-start | bytes 589832 | tf_op jit(solution)/shard_map/ppermute | solution.py:170
  120.9 18.6 %collective-permute-start.17 = (bf16[16,6144]{1,0:T(8,128)(2,1)S(1)}, bf16[16,6144]{1,0:T(8,128)(2,1)S(1)}, u32[]{:S(2)}, u32[]{:S(2)}) collective-permute-start(bf16[16,6144]{1,0:T(8,128)(2,1)S(1)} %get-tuple-element.28), channel_id=1, source_target_pairs={{0,4},{1,5},{2,0},{3,1},{4,6},{5,7},{6,2},{7,3},{8,12},{9,13},{10,... | collective-permute-start | bytes 589832 | tf_op jit(solution)/shard_map/ppermute | solution.py:170
  123.8 16.3 %collective-permute-start.16 = (bf16[16,6144]{1,0:T(8,128)(2,1)S(1)}, bf16[16,6144]{1,0:T(8,128)(2,1)S(1)}, u32[]{:S(2)}, u32[]{:S(2)}) collective-permute-start(bf16[16,6144]{1,0:T(8,128)(2,1)S(1)} %get-tuple-element.29), channel_id=1, source_target_pairs={{0,6},{1,7},{2,4},{3,5},{4,2},{5,3},{6,0},{7,1},{8,14},{9,15},{10,... | collective-permute-start | bytes 589832 | tf_op jit(solution)/shard_map/ppermute | solution.py:170
  124.9 15.1 %copy-start.1 = (f32[16,6144]{1,0:T(8,128)S(1)}, f32[16,6144]{1,0:T(8,128)}, u32[]{:S(2)}) copy-start(f32[16,6144]{1,0:T(8,128)} %get-tuple-element.15) | copy-start | bytes 1179652
  124.9 15.1 %copy-start.5 = (f32[6144]{0:T(1024)S(1)}, f32[6144]{0:T(1024)}, u32[]{:S(2)}) copy-start(f32[6144]{0:T(1024)} %param.6) | copy-start | bytes 73732
  125.1 39.6 %collective-permute-start.29 = (bf16[128,2048]{1,0:T(8,128)(2,1)S(1)}, bf16[128,2048]{1,0:T(8,128)(2,1)S(1)}, u32[]{:S(2)}, u32[]{:S(2)}) collective-permute-start(bf16[128,2048]{1,0:T(8,128)(2,1)S(1)} %copy-done), channel_id=1, source_target_pairs={{0,16},{8,24},{16,0},{24,8},{1,17},{9,25},{17,1},{25,9},{2,18},{10... | collective-permute-start | bytes 1572872 | tf_op jit(solution)/shard_map/ppermute | solution.py:176
  135.1 14.8 %collective-permute-start.31 = (bf16[128,2048]{1,0:T(8,128)(2,1)S(1)}, bf16[128,2048]{1,0:T(8,128)(2,1)S(1)}, u32[]{:S(2)}, u32[]{:S(2)}) collective-permute-start(bf16[128,2048]{1,0:T(8,128)(2,1)S(1)} %copy-done.19), channel_id=1, source_target_pairs={{0,8},{8,0},{16,24},{24,16},{1,9},{9,1},{17,25},{25,17},{2,10},{10... | collective-permute-start | bytes 1572872 | tf_op jit(solution)/shard_map/ppermute | solution.py:176
  138.0 26.7 %collective-permute-start.30 = (bf16[128,2048]{1,0:T(8,128)(2,1)S(1)}, bf16[128,2048]{1,0:T(8,128)(2,1)S(1)}, u32[]{:S(2)}, u32[]{:S(2)}) collective-permute-start(bf16[128,2048]{1,0:T(8,128)(2,1)S(1)} %collective-permute-done.28), channel_id=1, source_target_pairs={{0,16},{8,24},{16,0},{24,8},{1,17},{9,25},{17,1},{25,9},{2,18},{10... | collective-permute-start | bytes 1572872 | tf_op jit(solution)/shard_map/ppermute | solution.py:176
  139.5 19.9 %collective-permute-start.33 = (bf16[128,2048]{1,0:T(8,128)(2,1)S(1)}, bf16[128,2048]{1,0:T(8,128)(2,1)S(1)}, u32[]{:S(2)}, u32[]{:S(2)}) collective-permute-start(bf16[128,2048]{1,0:T(8,128)(2,1)S(1)} %collective-permute-done.32), channel_id=1, source_target_pairs={{0,8},{8,0},{16,24},{24,16},{1,9},{9,1},{17,25},{25,17},{2,10},{10... | collective-permute-start | bytes 1572872 | tf_op jit(solution)/shard_map/ppermute | solution.py:176

commit v2 on v1

--- a/solution.py
+++ b/solution.py
@@ -140,7 +140,8 @@
     lax.fori_loop(0, weight.shape[0] // span_of, body, 0)
 
 
-def normgrad_kernel(step, pre, weight, normed, gain, partial, gain_part, buffer, sems):
+def normgrad_kernel(step, pre, weight, normed, gain, mine, other, gain_part, buffer, sems):
+    half = mine.shape[0]
     stream = Stream(weight, buffer, sems, step)
     stream.start()
 
@@ -148,7 +149,8 @@
         stream.copy(part).wait()
         span = pl.ds(pl.multiple_of(part * step, step), step)
         grad = contract(pre[...], buffer[span, :], ((1,), (1,)))
-        partial[:, span] = grad.astype(jnp.bfloat16)
+        mine[:, span] = grad[:half].astype(jnp.bfloat16)
+        other[:, span] = grad[half:].astype(jnp.bfloat16)
         x_hat = normed[:, span].astype(jnp.float32) / gain[:, span]
         gain_part[:, span] = jnp.sum(grad * x_hat, axis=0, keepdims=True)
         return carry
@@ -175,14 +177,17 @@
     def replica(array, mask):
         return lax.ppermute(array, "dp", swap_perm(n_dp, mask))
 
-    def spread(own):
+    def spread(own, relayed):
         pieces = [own]
-        for _ in range(1, chips):
-            pieces.append(along_ring(pieces[-1]))
+        for s in range(1, chips):
+            if relayed:
+                pieces.append(along_ring(pieces[-1]))
+            else:
+                pieces.append(along_ring(own, s))
         return pieces, [across(p) for p in pieces]
 
-    def gathered(own):
-        mine, other = spread(own)
+    def gathered(own, relayed):
+        mine, other = spread(own, relayed)
         return mine + other if rows % 16 == 0 else [jnp.concatenate(mine + other, axis=0)]
 
     def replicas(own, low):
@@ -192,8 +197,8 @@
             out.append(replica(out[k ^ bit], bit))
         return out
 
-    token_pieces = gathered(tokens)
-    cotan_pieces = gathered(out_grad)
+    token_pieces = gathered(tokens, True)
+    cotan_pieces = gathered(out_grad, False)
     gain_row = norm_gain.reshape(1, width)
     x_hat, scale, blocks = pl.pallas_call(
         functools.partial(norm_kernel, n_dp),
@@ -214,13 +219,14 @@
 
     shard_list = [column_shards(k) for k in range(n_dp)]
     shard = jnp.stack(shard_list)
-    shards_mine, shards_other = spread(shard)
+    shards_mine, shards_other = spread(shard, False)
     columns = jnp.stack([jnp.stack(shards_mine), jnp.stack(shards_other)])
     columns = columns.transpose(3, 2, 0, 1, 4, 5).reshape(2, -1, cols)
     normed_cols, cotan_cols = columns[0], columns[1]
 
     float_units, half_units = ((group, units), jnp.float32), ((group, units), jnp.bfloat16)
     half_width = ((group, width), jnp.bfloat16)
+    core_width = ((rows * chips, width), jnp.bfloat16)
     step, count = chunk(width, 384, 128), len(token_pieces)
     hidden, slope, normed_all = call(
         functools.partial(preact_kernel, step, count),
@@ -243,11 +249,11 @@
         (pltpu.VMEM(*half_width),),
     )
     step = chunk(width, 768, 128)
-    partial, gain_grad = call(
+    mine, other, gain_grad = call(
         functools.partial(normgrad_kernel, step),
         (pre_grad, up_weight, normed_all, gain_row),
         [WHOLE, STAYS, WHOLE, WHOLE],
-        (half_width, ((1, width), jnp.float32)),
+        (core_width, core_width, ((1, width), jnp.float32)),
         up_weight,
         step,
     )
@@ -255,17 +261,15 @@
     hidden_all = jnp.concatenate(replicas(hidden, True), axis=0)
     pre_all = jnp.concatenate(replicas(pre_grad, False), axis=0)
 
+    received = [along_ring(gain_grad, s) for s in range(1, chips)]
+    for part in received:
+        gain_grad = gain_grad + part
     gain_grad = gain_grad + across(gain_grad)
-    shift = 1
-    while shift < chips:
-        gain_grad = gain_grad + along_ring(gain_grad, shift)
-        shift *= 2
     for bit in range((n_dp - 1).bit_length()):
         gain_grad = gain_grad + replica(gain_grad, 1 << bit)
     gain_grad = gain_grad.reshape(width) * factor
 
-    half = rows * chips
-    total = partial[:half].astype(jnp.float32) + across(partial[half:]).astype(jnp.float32)
+    total = mine.astype(jnp.float32) + across(other).astype(jnp.float32)
     parts = total.astype(jnp.bfloat16).reshape(chips, rows, width)
     norm_grad = total[:rows]
     for s in range(1, chips):

time: 171 us -> 174 us (1.018)
  the two profiles are of different devices: /device:TPU:0 before, /device:TPU:10 now
where the time goes in v2:
time: 174 us; the launch traced here: 173 us
  waiting for transfers between devices  79.8 us (46%)
  Pallas kernels  41.5 us (24%)
  starting transfers between devices  32.9 us (19%)
  matrix products  10.7 us (6%)
  local copies, waits for them, and re-layouts  3.83 us (2%)
  other arithmetic  3.54 us (2%)
    ppermute x15, waiting for transfers between devices, along_ring(): return lax.ppermute(array, 'mp', ring_perm(n_mp, shift))  52.1 us
    pallas_call x3, Pallas kernels, call(): pl.pallas_call(kernel, in_specs=in_specs, out_specs=[WHOLE] * len(outs),...  39.3 us
    ppermute x11, waiting for transfers between devices, replica(): return lax.ppermute(array, 'dp', swap_perm(n_dp, mask))  26.5 us
    ppermute x15, starting transfers between devices, along_ring(): return lax.ppermute(array, 'mp', ring_perm(n_mp, shift))  18.7 us
    ppermute x11, starting transfers between devices, replica(): return lax.ppermute(array, 'dp', swap_perm(n_dp, mask))  11.8 us
    dot_general x2, matrix products, contract(): lax.dot_general(a, b, (dims, ((), ())), preferred_element_type=jnp.float32)  10.7 us
  transfers between devices with their start and end apart: 40, of which 12 were waited for; matrix products, arithmetic and copies ran while one was open for 6% of the time, Pallas kernels for 24%

profile of v2, /device:TPU:10, one launch (start us, length us, event | category | flops | bytes accessed | tf_op | source)
XLA Modules:
  0.0 173.4 jit_solution(8752386398968909512)
XLA Ops:
  0.6 0.5 collective-permute-start.7
  1.1 7.3 %collective-permute-done.7.refs_1_ = bf16[16,6144]{1,0:T(8,128)(2,1)S(1)} collective-permute-done((bf16[16,6144]{1,0:T(8,128)(2,1)}, bf16[16,6144]{1,0:T(8,128)(2,1)S(1)}, u32[]{:S(2)}, u32[]{:S(2)}) %collective-permute-start.7) | collective-permute-done | bytes 196640 | tf_op jit(solution)/shard_map/ppermute | solution.py:172
  8.4 2.9 %collective-permute-start.2 = (bf16[16,6144]{1,0:T(8,128)(2,1)}, bf16[16,6144]{1,0:T(8,128)(2,1)S(1)}, u32[]{:S(2)}, u32[]{:S(2)}) collective-permute-start(bf16[16,6144]{1,0:T(8,128)(2,1)} %cotan.1), channel_id=1, source_target_pairs={{0,2},{1,3},{2,6},{3,7},{4,0},{5,1},{6,4},{7,5},{8,10},{9,11},{10,... | collective-permute-start | bytes 589832 | tf_op jit(solution)/shard_map/ppermute | solution.py:172
  11.4 5.4 %collective-permute-done.8.refs_2_ = bf16[16,6144]{1,0:T(8,128)(2,1)S(1)} collective-permute-done((bf16[16,6144]{1,0:T(8,128)(2,1)S(1)}, bf16[16,6144]{1,0:T(8,128)(2,1)S(1)}, u32[]{:S(2)}, u32[]{:S(2)}) %collective-permute-start.8) | collective-permute-done | bytes 196640 | tf_op jit(solution)/shard_map/ppermute | solution.py:172
  16.8 1.9 %collective-permute-start.1 = (bf16[16,6144]{1,0:T(8,128)(2,1)}, bf16[16,6144]{1,0:T(8,128)(2,1)S(1)}, u32[]{:S(2)}, u32[]{:S(2)}) collective-permute-start(bf16[16,6144]{1,0:T(8,128)(2,1)} %cotan.1), channel_id=1, source_target_pairs={{0,6},{1,7},{2,4},{3,5},{4,2},{5,3},{6,0},{7,1},{8,14},{9,15},{10,... | collective-permute-start | bytes 589832 | tf_op jit(solution)/shard_map/ppermute | solution.py:172
  18.7 2.5 %collective-permute-start = (bf16[16,6144]{1,0:T(8,128)(2,1)}, bf16[16,6144]{1,0:T(8,128)(2,1)S(1)}, u32[]{:S(2)}, u32[]{:S(2)}) collective-permute-start(bf16[16,6144]{1,0:T(8,128)(2,1)} %cotan.1), channel_id=1, source_target_pairs={{0,4},{1,5},{2,0},{3,1},{4,6},{5,7},{6,2},{7,3},{8,12},{9,13},{10,... | collective-permute-start | bytes 589832 | tf_op jit(solution)/shard_map/ppermute | solution.py:172
  21.2 2.2 %ln.1 = (f32[16,6144]{1,0:T(8,128)}, f32[16,128]{1,0:T(8,128)}, bf16[4,2,16,1536]{3,2,1,0:T(8,128)(2,1)}) custom-call(bf16[16,6144]{1,0:T(8,128)(2,1)} %tokens.1, bf16[16,6144]{1,0:T(8,128)(2,1)} %cotan.1, f32[1,6144]{1,0:T(1,128)} %bitcast.39), custom_call_target="tpu_custom_call" | custom-call | tf_op jit(solution)/shard_map/ln/pallas_call | solution.py:203
  23.4 0.5 collective-permute-start.12
  23.9 1.7 collective-permute-done.9.refs_3_
  25.7 1.1 constant_dynamic-slice_fusion
  26.8 9.8 %collective-permute-done.1.refs_2_ = bf16[16,6144]{1,0:T(8,128)(2,1)S(1)} collective-permute-done((bf16[16,6144]{1,0:T(8,128)(2,1)}, bf16[16,6144]{1,0:T(8,128)(2,1)S(1)}, u32[]{:S(2)}, u32[]{:S(2)}) %collective-permute-start.1) | collective-permute-done | bytes 196640 | tf_op jit(solution)/shard_map/ppermute | solution.py:172
  36.6 1.6 collective-permute-start.20
  38.2 0.2 collective-permute-start.6
  38.3 0.4 collective-permute-start.5
  38.7 0.2 collective-permute-start.4
  38.9 0.1 copy-done.13
  39.0 0.4 copy-done.14
  39.4 12.3 %shard_map.84 = (bf16[128,2048]{1,0:T(8,128)(2,1)}, f32[128,2048]{1,0:T(8,128)}, bf16[128,6144]{1,0:T(8,128)(2,1)}) custom-call(bf16[16,6144]{1,0:T(8,128)(2,1)} %tokens.1, bf16[16,6144]{1,0:T(8,128)(2,1)} %copy-done.6, bf16[16,6144]{1,0:T(8,128)(2,1)} %copy-done.8, bf16[16,6144]{1,0:T(8,128)(2,1)} %copy-done.10, bf16[16,6144]{1,0:T(8,128)(2,1)} %copy-done.9, ...), custom_call_target="tpu_custom_call" | custom-call | flops 3221225472 | bytes 25165824 | tf_op jit(solution)/shard_map/pallas_call | solution.py:75
  51.8 0.6 collective-permute-start.19
  52.3 1.5 collective-permute-start.18
  53.9 0.6 copy-done.16
  54.5 0.1 copy-done.17
  54.6 13.0 %shard_map.85.pre = bf16[128,2048]{1,0:T(8,128)(2,1)} custom-call(bf16[16,6144]{1,0:T(8,128)(2,1)} %cotan.1, bf16[16,6144]{1,0:T(8,128)(2,1)} %copy-done.7, bf16[16,6144]{1,0:T(8,128)(2,1)} %copy-done.5, bf16[16,6144]{1,0:T(8,128)(2,1)} %copy-done.4, bf16[16,6144]{1,0:T(8,128)(2,1)} %copy-done.12, bf16[16,6144]{1,0:T(8,128)(2,1)} %copy-done.17, ...), custom_call_target="tpu_custom_call" | custom-call | flops 3221225472 | bytes 25165824 | tf_op jit(solution)/shard_map/pallas_call | solution.py:75
  67.6 14.0 %shard_map.86 = (bf16[64,6144]{1,0:T(8,128)(2,1)}, bf16[64,6144]{1,0:T(8,128)(2,1)}, f32[1,6144]{1,0:T(1,128)}) custom-call(bf16[128,2048]{1,0:T(8,128)(2,1)} %shard_map.85.pre, bf16[6144,2048]{1,0:T(8,128)(2,1)} %weight.1, bf16[128,6144]{1,0:T(8,128)(2,1)} %get-tuple-element.14.normed, f32[1,6144]{1,0:T(1,128)} %bitcast.41), custom_call_target="tpu_custom_call" | custom-call | flops 1610612736 | bytes 25165824 | tf_op jit(solution)/shard_map/pallas_call | solution.py:75
  81.7 1.2 collective-permute-start.35
  82.9 2.8 %collective-permute-start.34 = (f32[1,6144]{1,0:T(1,128)}, f32[1,6144]{1,0:T(1,128)S(1)}, u32[]{:S(2)}, u32[]{:S(2)}) collective-permute-start(f32[1,6144]{1,0:T(1,128)} %get-tuple-element.21), channel_id=1, source_target_pairs={{0,4},{1,5},{2,0},{3,1},{4,6},{5,7},{6,2},{7,3},{8,12},{9,13},{10,... | collective-permute-start | bytes 73736 | tf_op jit(solution)/shard_map/ppermute | solution.py:172
  85.9 0.4 collective-permute-start.23
  86.2 1.2 collective-permute-start.22
  87.4 2.3 %collective-permute-start.21 = (bf16[4,2,16,1536]{3,2,1,0:T(8,128)(2,1)S(1)}, bf16[4,2,16,1536]{3,2,1,0:T(8,128)(2,1)S(1)}, u32[]{:S(2)}, u32[]{:S(2)}) collective-permute-start(bf16[4,2,16,1536]{3,2,1,0:T(8,128)(2,1)S(1)} %get-tuple-element.33), channel_id=1, source_target_pairs={{0,4},{1,5},{2,0},{3,1},{4,6},{5,7},{6,2},{7,3},{8,12},{9,13},{10,... | collective-permute-start | bytes 1179656 | tf_op jit(solution)/shard_map/ppermute | solution.py:172
  89.7 0.8 add_add_fusion
  90.6 1.2 collective-permute-done.37
  91.8 0.6 collective-permute-start.38
  92.4 0.1 slice_reduce_fusion
  92.6 3.1 %collective-permute-done.38 = f32[1,6144]{1,0:T(1,128)S(1)} collective-permute-done((f32[1,6144]{1,0:T(1,128)S(1)}, f32[1,6144]{1,0:T(1,128)S(1)}, u32[]{:S(2)}, u32[]{:S(2)}) %collective-permute-start.38) | collective-permute-done | bytes 24608 | tf_op jit(solution)/shard_map/ppermute | solution.py:178
  95.7 1.6 collective-permute-start.39
  97.3 15.3 %collective-permute-done.23 = bf16[4,2,16,1536]{3,2,1,0:T(8,128)(2,1)S(1)} collective-permute-done((bf16[4,2,16,1536]{3,2,1,0:T(8,128)(2,1)S(1)}, bf16[4,2,16,1536]{3,2,1,0:T(8,128)(2,1)S(1)}, u32[]{:S(2)}, u32[]{:S(2)}) %collective-permute-start.23) | collective-permute-done | bytes 393248 | tf_op jit(solution)/shard_map/ppermute | solution.py:172
  112.6 8.7 %collective-permute-done.22 = bf16[4,2,16,1536]{3,2,1,0:T(8,128)(2,1)S(1)} collective-permute-done((bf16[4,2,16,1536]{3,2,1,0:T(8,128)(2,1)S(1)}, bf16[4,2,16,1536]{3,2,1,0:T(8,128)(2,1)S(1)}, u32[]{:S(2)}, u32[]{:S(2)}) %collective-permute-start.22) | collective-permute-done | bytes 393248 | tf_op jit(solution)/shard_map/ppermute | solution.py:172
  121.2 0.2 maximum_bitcast_fusion.1
  121.5 0.5 collective-permute-start.26
  122.1 0.4 collective-permute-start.14
  122.5 0.6 add_multiply_fusion
  123.2 0.5 collective-permute-start.28
  123.7 1.5 collective-permute-start.32
  125.2 0.2 maximum_bitcast_fusion.2
  125.4 0.3 maximum_bitcast_fusion
  125.8 0.8 copy-done.2
  126.6 0.2 convert_add_fusion
  126.9 2.0 %collective-permute-start.17 = (bf16[16,6144]{1,0:T(8,128)(2,1)S(1)}, bf16[16,6144]{1,0:T(8,128)(2,1)S(1)}, u32[]{:S(2)}, u32[]{:S(2)}) collective-permute-start(bf16[16,6144]{1,0:T(8,128)(2,1)S(1)} %get-tuple-element.30), channel_id=1, source_target_pairs={{0,4},{1,5},{2,0},{3,1},{4,6},{5,7},{6,2},{7,3},{8,12},{9,13},{10,... | collective-permute-start | bytes 589832 | tf_op jit(solution)/shard_map/ppermute | solution.py:172
  128.9 0.8 collective-permute-start.16
  129.8 0.2 fusion.23
  130.0 0.1 copy.10
  130.1 0.1 copy.9
  130.2 6.9 %collective-permute-done.28 = bf16[128,2048]{1,0:T(8,128)(2,1)S(1)} collective-permute-done((bf16[128,2048]{1,0:T(8,128)(2,1)S(1)}, bf16[128,2048]{1,0:T(8,128)(2,1)S(1)}, u32[]{:S(2)}, u32[]{:S(2)}) %collective-permute-start.28) | collective-permute-done | bytes 524320 | tf_op jit(solution)/shard_map/ppermute | solution.py:178
  137.1 1.5 collective-permute-start.29
  138.6 0.5 collective-permute-start.31
  139.1 1.2 collective-permute-start.30
  140.4 0.8 collective-permute-start.33
  141.2 3.8 %collective-permute-done.16 = bf16[16,6144]{1,0:T(8,128)(2,1)S(1)} collective-permute-done((bf16[16,6144]{1,0:T(8,128)(2,1)S(1)}, bf16[16,6144]{1,0:T(8,128)(2,1)S(1)}, u32[]{:S(2)}, u32[]{:S(2)}) %collective-permute-start.16) | collective-permute-done | bytes 196640 | tf_op jit(solution)/shard_map/ppermute | solution.py:172
  145.0 0.3 fusion.21
  145.3 0.8 multiply_convert_fusion.2
  146.1 7.3 %collective-permute-done.31 = bf16[128,2048]{1,0:T(8,128)(2,1)S(1)} collective-permute-done((bf16[128,2048]{1,0:T(8,128)(2,1)S(1)}, bf16[128,2048]{1,0:T(8,128)(2,1)S(1)}, u32[]{:S(2)}, u32[]{:S(2)}) %collective-permute-start.31) | collective-permute-done | bytes 524320 | tf_op jit(solution)/shard_map/ppermute | solution.py:178
  153.4 9.2 %collective-permute-done.33 = bf16[128,2048]{1,0:T(8,128)(2,1)S(1)} collective-permute-done((bf16[128,2048]{1,0:T(8,128)(2,1)S(1)}, bf16[128,2048]{1,0:T(8,128)(2,1)S(1)}, u32[]{:S(2)}, u32[]{:S(2)}) %collective-permute-start.33) | collective-permute-done | bytes 524320 | tf_op jit(solution)/shard_map/ppermute | solution.py:178
  162.6 5.4 %multiply_convert_fusion = bf16[2048,1536]{1,0:T(8,128)(2,1)} fusion(bf16[512,1536]{1,0:T(8,128)(2,1)S(1)} %bitcast.31, bf16[128,2048]{1,0:T(8,128)(2,1)S(1)} %collective-permute-done.33, bf16[128,2048]{1,0:T(8,128)(2,1)S(1)} %collective-permute-done.32, bf16[128,2048]{1,0:T(8,128)(2,1)S(1)} %collective-permute-done.31, bf16[128,2048]{1,0:T(8,128)(2,1)S(1)} %copy-done.20), kind=kOutput, calls=%fused_computation | convolution fusion | flops 3235905536 | bytes 9961472 | tf_op jit(solution)/shard_map/dot_general | solution.py:35
  168.0 5.4 %multiply_convert_fusion.1 = bf16[1536,2048]{1,0:T(8,128)(2,1)} fusion(bf16[512,1536]{1,0:T(8,128)(2,1)S(1)} %bitcast.30, bf16[128,2048]{1,0:T(8,128)(2,1)S(1)} %collective-permute-done.30, bf16[128,2048]{1,0:T(8,128)(2,1)S(1)} %collective-permute-done.29, bf16[128,2048]{1,0:T(8,128)(2,1)S(1)} %collective-permute-done.28, bf16[128,2048]{1,0:T(8,128)(2,1)S(1)} %copy-done), kind=kOutput, calls=%fused_computation.1 | convolution fusion | flops 3235905536 | bytes 9961472 | tf_op jit(solution)/shard_map/dot_general | solution.py:35
  (82 shorter events, 0.7 us)
Async XLA Ops:
  0.6 7.8 %collective-permute-start.7 = (bf16[16,6144]{1,0:T(8,128)(2,1)}, bf16[16,6144]{1,0:T(8,128)(2,1)S(1)}, u32[]{:S(2)}, u32[]{:S(2)}) collective-permute-start(bf16[16,6144]{1,0:T(8,128)(2,1)} %tokens.1), channel_id=1, source_target_pairs={{0,4},{1,5},{2,0},{3,1},{4,6},{5,7},{6,2},{7,3},{8,12},{9,13},{10,... | collective-permute-start | bytes 589832 | tf_op jit(solution)/shard_map/ppermute | solution.py:172
  8.4 30.4 %copy-start.6 = (bf16[16,6144]{1,0:T(8,128)(2,1)}, bf16[16,6144]{1,0:T(8,128)(2,1)S(1)}, u32[]{:S(2)}) copy-start(bf16[16,6144]{1,0:T(8,128)(2,1)S(1)} %collective-permute-done.7.refs_1_) | copy-start | bytes 589828
  8.4 8.4 %collective-permute-start.8 = (bf16[16,6144]{1,0:T(8,128)(2,1)S(1)}, bf16[16,6144]{1,0:T(8,128)(2,1)S(1)}, u32[]{:S(2)}, u32[]{:S(2)}) collective-permute-start(bf16[16,6144]{1,0:T(8,128)(2,1)S(1)} %collective-permute-done.7.refs_1_), channel_id=1, source_target_pairs={{0,4},{1,5},{2,0},{3,1},{4,6},{5,7},{6,2},{7,3},{8,12},{9,13},{10,... | collective-permute-start | bytes 589832 | tf_op jit(solution)/shard_map/ppermute | solution.py:172
  8.4 15.0 %collective-permute-start.10 = (bf16[16,6144]{1,0:T(8,128)(2,1)}, bf16[16,6144]{1,0:T(8,128)(2,1)S(1)}, u32[]{:S(2)}, u32[]{:S(2)}) collective-permute-start(bf16[16,6144]{1,0:T(8,128)(2,1)} %tokens.1), channel_id=1, source_target_pairs={{0,1},{1,0},{2,3},{3,2},{4,5},{5,4},{6,7},{7,6},{8,9},{9,8},{10,11... | collective-permute-start | bytes 589832 | tf_op jit(solution)/shard_map/ppermute | solution.py:175
  8.4 15.0 %collective-permute-start.2 = (bf16[16,6144]{1,0:T(8,128)(2,1)}, bf16[16,6144]{1,0:T(8,128)(2,1)S(1)}, u32[]{:S(2)}, u32[]{:S(2)}) collective-permute-start(bf16[16,6144]{1,0:T(8,128)(2,1)} %cotan.1), channel_id=1, source_target_pairs={{0,2},{1,3},{2,6},{3,7},{4,0},{5,1},{6,4},{7,5},{8,10},{9,11},{10,... | collective-permute-start | bytes 589832 | tf_op jit(solution)/shard_map/ppermute | solution.py:172
  16.8 22.0 %copy-start.8 = (bf16[16,6144]{1,0:T(8,128)(2,1)}, bf16[16,6144]{1,0:T(8,128)(2,1)S(1)}, u32[]{:S(2)}) copy-start(bf16[16,6144]{1,0:T(8,128)(2,1)S(1)} %collective-permute-done.8.refs_2_) | copy-start | bytes 589828
  16.8 8.8 %collective-permute-start.9 = (bf16[16,6144]{1,0:T(8,128)(2,1)S(1)}, bf16[16,6144]{1,0:T(8,128)(2,1)S(1)}, u32[]{:S(2)}, u32[]{:S(2)}) collective-permute-start(bf16[16,6144]{1,0:T(8,128)(2,1)S(1)} %collective-permute-done.8.refs_2_), channel_id=1, source_target_pairs={{0,4},{1,5},{2,0},{3,1},{4,6},{5,7},{6,2},{7,3},{8,12},{9,13},{10,... | collective-permute-start | bytes 589832 | tf_op jit(solution)/shard_map/ppermute | solution.py:172
  16.8 19.8 %collective-permute-start.1 = (bf16[16,6144]{1,0:T(8,128)(2,1)}, bf16[16,6144]{1,0:T(8,128)(2,1)S(1)}, u32[]{:S(2)}, u32[]{:S(2)}) collective-permute-start(bf16[16,6144]{1,0:T(8,128)(2,1)} %cotan.1), channel_id=1, source_target_pairs={{0,6},{1,7},{2,4},{3,5},{4,2},{5,3},{6,0},{7,1},{8,14},{9,15},{10,... | collective-permute-start | bytes 589832 | tf_op jit(solution)/shard_map/ppermute | solution.py:172
  18.7 17.9 %collective-permute-start = (bf16[16,6144]{1,0:T(8,128)(2,1)}, bf16[16,6144]{1,0:T(8,128)(2,1)S(1)}, u32[]{:S(2)}, u32[]{:S(2)}) collective-permute-start(bf16[16,6144]{1,0:T(8,128)(2,1)} %cotan.1), channel_id=1, source_target_pairs={{0,4},{1,5},{2,0},{3,1},{4,6},{5,7},{6,2},{7,3},{8,12},{9,13},{10,... | collective-permute-start | bytes 589832 | tf_op jit(solution)/shard_map/ppermute | solution.py:172
  23.4 15.4 %copy-start.9 = (bf16[16,6144]{1,0:T(8,128)(2,1)}, bf16[16,6144]{1,0:T(8,128)(2,1)S(1)}, u32[]{:S(2)}) copy-start(bf16[16,6144]{1,0:T(8,128)(2,1)S(1)} %collective-permute-done.10.refs_4_) | copy-start | bytes 589828
  23.4 14.8 %collective-permute-start.11 = (bf16[16,6144]{1,0:T(8,128)(2,1)S(1)}, bf16[16,6144]{1,0:T(8,128)(2,1)S(1)}, u32[]{:S(2)}, u32[]{:S(2)}) collective-permute-start(bf16[16,6144]{1,0:T(8,128)(2,1)S(1)} %collective-permute-done.7.refs_1_), channel_id=1, source_target_pairs={{0,1},{1,0},{2,3},{3,2},{4,5},{5,4},{6,7},{7,6},{8,9},{9,8},{10,11... | collective-permute-start | bytes 589832 | tf_op jit(solution)/shard_map/ppermute | solution.py:175
  23.4 28.3 %copy-start.4 = (bf16[16,6144]{1,0:T(8,128)(2,1)}, bf16[16,6144]{1,0:T(8,128)(2,1)S(1)}, u32[]{:S(2)}) copy-start(bf16[16,6144]{1,0:T(8,128)(2,1)S(1)} %collective-permute-done.2.refs_3_) | copy-start | bytes 589828
  23.4 14.9 %collective-permute-start.12 = (bf16[16,6144]{1,0:T(8,128)(2,1)S(1)}, bf16[16,6144]{1,0:T(8,128)(2,1)S(1)}, u32[]{:S(2)}, u32[]{:S(2)}) collective-permute-start(bf16[16,6144]{1,0:T(8,128)(2,1)S(1)} %collective-permute-done.8.refs_2_), channel_id=1, source_target_pairs={{0,1},{1,0},{2,3},{3,2},{4,5},{5,4},{6,7},{7,6},{8,9},{9,8},{10,11... | collective-permute-start | bytes 589832 | tf_op jit(solution)/shard_map/ppermute | solution.py:175
  25.7 13.2 %copy-start.10 = (bf16[16,6144]{1,0:T(8,128)(2,1)}, bf16[16,6144]{1,0:T(8,128)(2,1)S(1)}, u32[]{:S(2)}) copy-start(bf16[16,6144]{1,0:T(8,128)(2,1)S(1)} %collective-permute-done.9.refs_3_) | copy-start | bytes 589828
  25.7 13.0 %collective-permute-start.13 = (bf16[16,6144]{1,0:T(8,128)(2,1)S(1)}, bf16[16,6144]{1,0:T(8,128)(2,1)S(1)}, u32[]{:S(2)}, u32[]{:S(2)}) collective-permute-start(bf16[16,6144]{1,0:T(8,128)(2,1)S(1)} %collective-permute-done.9.refs_3_), channel_id=1, source_target_pairs={{0,1},{1,0},{2,3},{3,2},{4,5},{5,4},{6,7},{7,6},{8,9},{9,8},{10,11... | collective-permute-start | bytes 589832 | tf_op jit(solution)/shard_map/ppermute | solution.py:175
  36.6 15.1 %copy-start.5 = (bf16[16,6144]{1,0:T(8,128)(2,1)}, bf16[16,6144]{1,0:T(8,128)(2,1)S(1)}, u32[]{:S(2)}) copy-start(bf16[16,6144]{1,0:T(8,128)(2,1)S(1)} %collective-permute-done.1.refs_2_) | copy-start | bytes 589828
  36.6 15.2 %collective-permute-start.3 = (bf16[16,6144]{1,0:T(8,128)(2,1)}, bf16[16,6144]{1,0:T(8,128)(2,1)S(1)}, u32[]{:S(2)}, u32[]{:S(2)}) collective-permute-start(bf16[16,6144]{1,0:T(8,128)(2,1)} %cotan.1), channel_id=1, source_target_pairs={{0,1},{1,0},{2,3},{3,2},{4,5},{5,4},{6,7},{7,6},{8,9},{9,8},{10,11... | collective-permute-start | bytes 589832 | tf_op jit(solution)/shard_map/ppermute | solution.py:175
  36.6 15.1 %copy-start.7 = (bf16[16,6144]{1,0:T(8,128)(2,1)}, bf16[16,6144]{1,0:T(8,128)(2,1)S(1)}, u32[]{:S(2)}) copy-start(bf16[16,6144]{1,0:T(8,128)(2,1)S(1)} %collective-permute-done.refs_1_) | copy-start | bytes 589828
  36.6 46.3 %collective-permute-start.20 = (bf16[2,16,1536]{2,1,0:T(8,128)(2,1)S(1)}, bf16[2,16,1536]{2,1,0:T(8,128)(2,1)S(1)}, u32[]{:S(2)}, u32[]{:S(2)}) collective-permute-start(bf16[2,16,1536]{2,1,0:T(8,128)(2,1)S(1)} %get-tuple-element.35), channel_id=1, source_target_pairs={{0,24},{8,16},{16,8},{24,0},{1,25},{9,17},{17,9},{25,1},{2,26},{10... | collective-permute-start | bytes 294920 | tf_op jit(solution)/shard_map/ppermute | solution.py:178
  38.2 0.7 copy-start.11
  38.2 14.1 %collective-permute-start.6 = (bf16[16,6144]{1,0:T(8,128)(2,1)S(1)}, bf16[16,6144]{1,0:T(8,128)(2,1)S(1)}, u32[]{:S(2)}, u32[]{:S(2)}) collective-permute-start(bf16[16,6144]{1,0:T(8,128)(2,1)S(1)} %collective-permute-done.2.refs_3_), channel_id=1, source_target_pairs={{0,1},{1,0},{2,3},{3,2},{4,5},{5,4},{6,7},{7,6},{8,9},{9,8},{10,11... | collective-permute-start | bytes 589832 | tf_op jit(solution)/shard_map/ppermute | solution.py:175
  38.3 0.7 copy-start.13
  38.3 15.5 %collective-permute-start.5 = (bf16[16,6144]{1,0:T(8,128)(2,1)S(1)}, bf16[16,6144]{1,0:T(8,128)(2,1)S(1)}, u32[]{:S(2)}, u32[]{:S(2)}) collective-permute-start(bf16[16,6144]{1,0:T(8,128)(2,1)S(1)} %collective-permute-done.1.refs_2_), channel_id=1, source_target_pairs={{0,1},{1,0},{2,3},{3,2},{4,5},{5,4},{6,7},{7,6},{8,9},{9,8},{10,11... | collective-permute-start | bytes 589832 | tf_op jit(solution)/shard_map/ppermute | solution.py:175
  38.7 0.7 copy-start.14
  38.7 15.1 %collective-permute-start.4 = (bf16[16,6144]{1,0:T(8,128)(2,1)S(1)}, bf16[16,6144]{1,0:T(8,128)(2,1)S(1)}, u32[]{:S(2)}, u32[]{:S(2)}) collective-permute-start(bf16[16,6144]{1,0:T(8,128)(2,1)S(1)} %collective-permute-done.refs_1_), channel_id=1, source_target_pairs={{0,1},{1,0},{2,3},{3,2},{4,5},{5,4},{6,7},{7,6},{8,9},{9,8},{10,11... | collective-permute-start | bytes 589832 | tf_op jit(solution)/shard_map/ppermute | solution.py:175
  51.7 2.1 %copy-start.12 = (bf16[16,6144]{1,0:T(8,128)(2,1)}, bf16[16,6144]{1,0:T(8,128)(2,1)S(1)}, u32[]{:S(2)}) copy-start(bf16[16,6144]{1,0:T(8,128)(2,1)S(1)} %collective-permute-done.3.refs_4_) | copy-start | bytes 589828
  51.8 34.0 %collective-permute-start.19 = (bf16[2,16,1536]{2,1,0:T(8,128)(2,1)S(1)}, bf16[2,16,1536]{2,1,0:T(8,128)(2,1)S(1)}, u32[]{:S(2)}, u32[]{:S(2)}) collective-permute-start(bf16[2,16,1536]{2,1,0:T(8,128)(2,1)S(1)} %get-tuple-element.36), channel_id=1, source_target_pairs={{0,16},{8,24},{16,0},{24,8},{1,17},{9,25},{17,1},{25,9},{2,18},{10... | collective-permute-start | bytes 294920 | tf_op jit(solution)/shard_map/ppermute | solution.py:178
  52.3 1.5 copy-start.15
  52.3 33.4 %collective-permute-start.18 = (bf16[2,16,1536]{2,1,0:T(8,128)(2,1)S(1)}, bf16[2,16,1536]{2,1,0:T(8,128)(2,1)S(1)}, u32[]{:S(2)}, u32[]{:S(2)}) collective-permute-start(bf16[2,16,1536]{2,1,0:T(8,128)(2,1)S(1)} %get-tuple-element.37), channel_id=1, source_target_pairs={{0,8},{8,0},{16,24},{24,16},{1,9},{9,1},{17,25},{25,17},{2,10},{10... | collective-permute-start | bytes 294920 | tf_op jit(solution)/shard_map/ppermute | solution.py:178
  53.8 0.7 copy-start.16
  53.8 0.7 copy-start.17
  67.6 24.8 %copy-start.18 = (f32[16,128]{1,0:T(8,128)S(1)}, f32[16,128]{1,0:T(8,128)}, u32[]{:S(2)}) copy-start(f32[16,128]{1,0:T(8,128)} %get-tuple-element.18) | copy-start | bytes 24580
  81.6 5.8 %collective-permute-start.36 = (f32[1,6144]{1,0:T(1,128)}, f32[1,6144]{1,0:T(1,128)S(1)}, u32[]{:S(2)}, u32[]{:S(2)}) collective-permute-start(f32[1,6144]{1,0:T(1,128)} %get-tuple-element.21), channel_id=1, source_target_pairs={{0,2},{1,3},{2,6},{3,7},{4,0},{5,1},{6,4},{7,5},{8,10},{9,11},{10,... | collective-permute-start | bytes 73736 | tf_op jit(solution)/shard_map/ppermute | solution.py:172
  81.7 8.0 %collective-permute-start.35 = (f32[1,6144]{1,0:T(1,128)}, f32[1,6144]{1,0:T(1,128)S(1)}, u32[]{:S(2)}, u32[]{:S(2)}) collective-permute-start(f32[1,6144]{1,0:T(1,128)} %get-tuple-element.21), channel_id=1, source_target_pairs={{0,6},{1,7},{2,4},{3,5},{4,2},{5,3},{6,0},{7,1},{8,14},{9,15},{10,... | collective-permute-start | bytes 73736 | tf_op jit(solution)/shard_map/ppermute | solution.py:172
  82.9 6.8 %collective-permute-start.34 = (f32[1,6144]{1,0:T(1,128)}, f32[1,6144]{1,0:T(1,128)S(1)}, u32[]{:S(2)}, u32[]{:S(2)}) collective-permute-start(f32[1,6144]{1,0:T(1,128)} %get-tuple-element.21), channel_id=1, source_target_pairs={{0,4},{1,5},{2,0},{3,1},{4,6},{5,7},{6,2},{7,3},{8,12},{9,13},{10,... | collective-permute-start | bytes 73736 | tf_op jit(solution)/shard_map/ppermute | solution.py:172
  85.8 36.3 %copy-start.19 = (bf16[64,6144]{1,0:T(8,128)(2,1)S(1)}, bf16[64,6144]{1,0:T(8,128)(2,1)}, u32[]{:S(2)}) copy-start(bf16[64,6144]{1,0:T(8,128)(2,1)} %get-tuple-element.16) | copy-start | bytes 2359300
  85.8 37.4 %copy-start = (bf16[128,2048]{1,0:T(8,128)(2,1)S(1)}, bf16[128,2048]{1,0:T(8,128)(2,1)}, u32[]{:S(2)}) copy-start(bf16[128,2048]{1,0:T(8,128)(2,1)} %shard_map.85.pre) | copy-start | bytes 1572868
  85.8 37.9 %copy-start.20 = (bf16[128,2048]{1,0:T(8,128)(2,1)S(1)}, bf16[128,2048]{1,0:T(8,128)(2,1)}, u32[]{:S(2)}) copy-start(bf16[128,2048]{1,0:T(8,128)(2,1)} %get-tuple-element.20) | copy-start | bytes 1572868
  85.9 26.7 %collective-permute-start.23 = (bf16[4,2,16,1536]{3,2,1,0:T(8,128)(2,1)S(1)}, bf16[4,2,16,1536]{3,2,1,0:T(8,128)(2,1)S(1)}, u32[]{:S(2)}, u32[]{:S(2)}) collective-permute-start(bf16[4,2,16,1536]{3,2,1,0:T(8,128)(2,1)S(1)} %get-tuple-element.33), channel_id=1, source_target_pairs={{0,2},{1,3},{2,6},{3,7},{4,0},{5,1},{6,4},{7,5},{8,10},{9,11},{10,... | collective-permute-start | bytes 1179656 | tf_op jit(solution)/shard_map/ppermute | solution.py:172
  86.2 35.0 %collective-permute-start.22 = (bf16[4,2,16,1536]{3,2,1,0:T(8,128)(2,1)S(1)}, bf16[4,2,16,1536]{3,2,1,0:T(8,128)(2,1)S(1)}, u32[]{:S(2)}, u32[]{:S(2)}) collective-permute-start(bf16[4,2,16,1536]{3,2,1,0:T(8,128)(2,1)S(1)} %get-tuple-element.33), channel_id=1, source_target_pairs={{0,6},{1,7},{2,4},{3,5},{4,2},{5,3},{6,0},{7,1},{8,14},{9,15},{10,... | collective-permute-start | bytes 1179656 | tf_op jit(solution)/shard_map/ppermute | solution.py:172
  87.4 33.8 %collective-permute-start.21 = (bf16[4,2,16,1536]{3,2,1,0:T(8,128)(2,1)S(1)}, bf16[4,2,16,1536]{3,2,1,0:T(8,128)(2,1)S(1)}, u32[]{:S(2)}, u32[]{:S(2)}) collective-permute-start(bf16[4,2,16,1536]{3,2,1,0:T(8,128)(2,1)S(1)} %get-tuple-element.33), channel_id=1, source_target_pairs={{0,4},{1,5},{2,0},{3,1},{4,6},{5,7},{6,2},{7,3},{8,12},{9,13},{10,... | collective-permute-start | bytes 1179656 | tf_op jit(solution)/shard_map/ppermute | solution.py:172
  90.5 1.3 collective-permute-start.37
  91.8 3.9 %collective-permute-start.38 = (f32[1,6144]{1,0:T(1,128)S(1)}, f32[1,6144]{1,0:T(1,128)S(1)}, u32[]{:S(2)}, u32[]{:S(2)}) collective-permute-start(f32[1,6144]{1,0:T(1,128)S(1)} %add.54), channel_id=1, source_target_pairs={{0,8},{8,0},{16,24},{24,16},{1,9},{9,1},{17,25},{25,17},{2,10},{10... | collective-permute-start | bytes 73736 | tf_op jit(solution)/shard_map/ppermute | solution.py:178
  92.5 30.7 %collective-permute-start.24 = (bf16[4,2,16,1536]{3,2,1,0:T(8,128)(2,1)S(1)}, bf16[4,2,16,1536]{3,2,1,0:T(8,128)(2,1)S(1)}, u32[]{:S(2)}, u32[]{:S(2)}) collective-permute-start(bf16[4,2,16,1536]{3,2,1,0:T(8,128)(2,1)S(1)} %get-tuple-element.33), channel_id=1, source_target_pairs={{0,1},{1,0},{2,3},{3,2},{4,5},{5,4},{6,7},{7,6},{8,9},{9,8},{10,11... | collective-permute-start | bytes 1179656 | tf_op jit(solution)/shard_map/ppermute | solution.py:175
  95.7 26.4 %collective-permute-start.39 = (f32[1,6144]{1,0:T(1,128)S(1)}, f32[1,6144]{1,0:T(1,128)S(1)}, u32[]{:S(2)}, u32[]{:S(2)}) collective-permute-start(f32[1,6144]{1,0:T(1,128)S(1)} %add.55), channel_id=1, source_target_pairs={{0,16},{8,24},{16,0},{24,8},{1,17},{9,25},{17,1},{25,9},{2,18},{10... | collective-permute-start | bytes 73736 | tf_op jit(solution)/shard_map/ppermute | solution.py:178
  121.4 2.3 %collective-permute-start.27 = (bf16[4,2,16,1536]{3,2,1,0:T(8,128)(2,1)S(1)}, bf16[4,2,16,1536]{3,2,1,0:T(8,128)(2,1)S(1)}, u32[]{:S(2)}, u32[]{:S(2)}) collective-permute-start(bf16[4,2,16,1536]{3,2,1,0:T(8,128)(2,1)S(1)} %collective-permute-done.23), channel_id=1, source_target_pairs={{0,1},{1,0},{2,3},{3,2},{4,5},{5,4},{6,7},{7,6},{8,9},{9,8},{10,11... | collective-permute-start | bytes 1179656 | tf_op jit(solution)/shard_map/ppermute | solution.py:175
  121.5 3.7 %collective-permute-start.26 = (bf16[4,2,16,1536]{3,2,1,0:T(8,128)(2,1)S(1)}, bf16[4,2,16,1536]{3,2,1,0:T(8,128)(2,1)S(1)}, u32[]{:S(2)}, u32[]{:S(2)}) collective-permute-start(bf16[4,2,16,1536]{3,2,1,0:T(8,128)(2,1)S(1)} %collective-permute-done.22), channel_id=1, source_target_pairs={{0,1},{1,0},{2,3},{3,2},{4,5},{5,4},{6,7},{7,6},{8,9},{9,8},{10,11... | collective-permute-start | bytes 1179656 | tf_op jit(solution)/shard_map/ppermute | solution.py:175
  122.0 3.2 %collective-permute-start.25 = (bf16[4,2,16,1536]{3,2,1,0:T(8,128)(2,1)S(1)}, bf16[4,2,16,1536]{3,2,1,0:T(8,128)(2,1)S(1)}, u32[]{:S(2)}, u32[]{:S(2)}) collective-permute-start(bf16[4,2,16,1536]{3,2,1,0:T(8,128)(2,1)S(1)} %collective-permute-done.21), channel_id=1, source_target_pairs={{0,1},{1,0},{2,3},{3,2},{4,5},{5,4},{6,7},{7,6},{8,9},{9,8},{10,11... | collective-permute-start | bytes 1179656 | tf_op jit(solution)/shard_map/ppermute | solution.py:175
  122.1 3.6 %collective-permute-start.14 = (bf16[64,6144]{1,0:T(8,128)(2,1)S(1)}, bf16[64,6144]{1,0:T(8,128)(2,1)S(1)}, u32[]{:S(2)}, u32[]{:S(2)}) collective-permute-start(bf16[64,6144]{1,0:T(8,128)(2,1)S(1)} %copy-done.19), channel_id=1, source_target_pairs={{0,1},{1,0},{2,3},{3,2},{4,5},{5,4},{6,7},{7,6},{8,9},{9,8},{10,11... | collective-permute-start | bytes 2359304 | tf_op jit(solution)/shard_map/ppermute | solution.py:175
  123.2 13.9 %collective-permute-start.28 = (bf16[128,2048]{1,0:T(8,128)(2,1)S(1)}, bf16[128,2048]{1,0:T(8,128)(2,1)S(1)}, u32[]{:S(2)}, u32[]{:S(2)}) collective-permute-start(bf16[128,2048]{1,0:T(8,128)(2,1)S(1)} %copy-done), channel_id=1, source_target_pairs={{0,8},{8,0},{16,24},{24,16},{1,9},{9,1},{17,25},{25,17},{2,10},{10... | collective-permute-start | bytes 1572872 | tf_op jit(solution)/shard_map/ppermute | solution.py:178
  123.7 14.9 %collective-permute-start.32 = (bf16[128,2048]{1,0:T(8,128)(2,1)S(1)}, bf16[128,2048]{1,0:T(8,128)(2,1)S(1)}, u32[]{:S(2)}, u32[]{:S(2)}) collective-permute-start(bf16[128,2048]{1,0:T(8,128)(2,1)S(1)} %copy-done.20), channel_id=1, source_target_pairs={{0,16},{8,24},{16,0},{24,8},{1,17},{9,25},{17,1},{25,9},{2,18},{10... | collective-permute-start | bytes 1572872 | tf_op jit(solution)/shard_map/ppermute | solution.py:178
  125.4 1.1 copy-start.2
  126.8 12.3 %collective-permute-start.15 = (bf16[16,6144]{1,0:T(8,128)(2,1)S(1)}, bf16[16,6144]{1,0:T(8,128)(2,1)S(1)}, u32[]{:S(2)}, u32[]{:S(2)}) collective-permute-start(bf16[16,6144]{1,0:T(8,128)(2,1)S(1)} %get-tuple-element.29), channel_id=1, source_target_pairs={{0,2},{1,3},{2,6},{3,7},{4,0},{5,1},{6,4},{7,5},{8,10},{9,11},{10,... | collective-permute-start | bytes 589832 | tf_op jit(solution)/shard_map/ppermute | solution.py:172
  126.9 13.5 %collective-permute-start.17 = (bf16[16,6144]{1,0:T(8,128)(2,1)S(1)}, bf16[16,6144]{1,0:T(8,128)(2,1)S(1)}, u32[]{:S(2)}, u32[]{:S(2)}) collective-permute-start(bf16[16,6144]{1,0:T(8,128)(2,1)S(1)} %get-tuple-element.30), channel_id=1, source_target_pairs={{0,4},{1,5},{2,0},{3,1},{4,6},{5,7},{6,2},{7,3},{8,12},{9,13},{10,... | collective-permute-start | bytes 589832 | tf_op jit(solution)/shard_map/ppermute | solution.py:172
  128.9 16.1 %collective-permute-start.16 = (bf16[16,6144]{1,0:T(8,128)(2,1)S(1)}, bf16[16,6144]{1,0:T(8,128)(2,1)S(1)}, u32[]{:S(2)}, u32[]{:S(2)}) collective-permute-start(bf16[16,6144]{1,0:T(8,128)(2,1)S(1)} %get-tuple-element.31), channel_id=1, source_target_pairs={{0,6},{1,7},{2,4},{3,5},{4,2},{5,3},{6,0},{7,1},{8,14},{9,15},{10,... | collective-permute-start | bytes 589832 | tf_op jit(solution)/shard_map/ppermute | solution.py:172
  130.1 14.9 %copy-start.1 = (f32[16,6144]{1,0:T(8,128)S(1)}, f32[16,6144]{1,0:T(8,128)}, u32[]{:S(2)}) copy-start(f32[16,6144]{1,0:T(8,128)} %get-tuple-element.17) | copy-start | bytes 1179652
  130.1 14.9 %copy-start.3 = (f32[6144]{0:T(1024)S(1)}, f32[6144]{0:T(1024)}, u32[]{:S(2)}) copy-start(f32[6144]{0:T(1024)} %param.6) | copy-start | bytes 73732
  137.1 30.9 %collective-permute-start.29 = (bf16[128,2048]{1,0:T(8,128)(2,1)S(1)}, bf16[128,2048]{1,0:T(8,128)(2,1)S(1)}, u32[]{:S(2)}, u32[]{:S(2)}) collective-permute-start(bf16[128,2048]{1,0:T(8,128)(2,1)S(1)} %copy-done), channel_id=1, source_target_pairs={{0,16},{8,24},{16,0},{24,8},{1,17},{9,25},{17,1},{25,9},{2,18},{10... | collective-permute-start | bytes 1572872 | tf_op jit(solution)/shard_map/ppermute | solution.py:178
  138.6 14.8 %collective-permute-start.31 = (bf16[128,2048]{1,0:T(8,128)(2,1)S(1)}, bf16[128,2048]{1,0:T(8,128)(2,1)S(1)}, u32[]{:S(2)}, u32[]{:S(2)}) collective-permute-start(bf16[128,2048]{1,0:T(8,128)(2,1)S(1)} %copy-done.20), channel_id=1, source_target_pairs={{0,8},{8,0},{16,24},{24,16},{1,9},{9,1},{17,25},{25,17},{2,10},{10... | collective-permute-start | bytes 1572872 | tf_op jit(solution)/shard_map/ppermute | solution.py:178
  139.1 28.9 %collective-permute-start.30 = (bf16[128,2048]{1,0:T(8,128)(2,1)S(1)}, bf16[128,2048]{1,0:T(8,128)(2,1)S(1)}, u32[]{:S(2)}, u32[]{:S(2)}) collective-permute-start(bf16[128,2048]{1,0:T(8,128)(2,1)S(1)} %collective-permute-done.28), channel_id=1, source_target_pairs={{0,16},{8,24},{16,0},{24,8},{1,17},{9,25},{17,1},{25,9},{2,18},{10... | collective-permute-start | bytes 1572872 | tf_op jit(solution)/shard_map/ppermute | solution.py:178
  140.4 22.2 %collective-permute-start.33 = (bf16[128,2048]{1,0:T(8,128)(2,1)S(1)}, bf16[128,2048]{1,0:T(8,128)(2,1)S(1)}, u32[]{:S(2)}, u32[]{:S(2)}) collective-permute-start(bf16[128,2048]{1,0:T(8,128)(2,1)S(1)} %collective-permute-done.32), channel_id=1, source_target_pairs={{0,8},{8,0},{16,24},{24,16},{1,9},{9,1},{17,25},{25,17},{2,10},{10... | collective-permute-start | bytes 1572872 | tf_op jit(solution)/shard_map/ppermute | solution.py:178

commit v3 on v2

--- a/solution.py
+++ b/solution.py
@@ -51,45 +51,45 @@
 
 
 WHOLE = pl.BlockSpec(memory_space=pltpu.VMEM)
-STAYS = pl.BlockSpec(memory_space=pl.ANY)
-
-
-class Stream:
-    def __init__(self, weight, buffer, sems, step):
-        self.refs, self.sems, self.step = (weight, buffer), sems, step
-
-    def copy(self, part):
-        start = part * self.step
-        if not isinstance(part, int):
-            start = pl.multiple_of(start, self.step)
-        rows = pl.ds(start, self.step)
-        return pltpu.make_async_copy(self.refs[0].at[rows], self.refs[1].at[rows], self.sems.at[part])
-
-    def start(self):
-        for part in range(self.refs[0].shape[0] // self.step):
-            self.copy(part).start()
-
-
-def call(kernel, operands, in_specs, outs, weight, step, extra=()):
-    rows, width = weight.shape
+STAYS = pl.BlockSpec(memory_space=pltpu.HBM)
+
+
+def call(kernel, operands, outs, grant, flops, extra=(), stay=0):
+    moved = sum(o.size * o.dtype.itemsize for o in operands)
     return pl.pallas_call(
         kernel,
-        in_specs=in_specs,
+        in_specs=[WHOLE] * (len(operands) - stay) + [STAYS] * stay,
         out_specs=[WHOLE] * len(outs),
-        out_shape=[jax.ShapeDtypeStruct(*o) for o in outs],
-        scratch_shapes=[
-            pltpu.VMEM((rows, width), weight.dtype),
-            pltpu.SemaphoreType.DMA((rows // step,)),
-            *extra,
-        ],
-        compiler_params=pltpu.CompilerParams(vmem_limit_bytes=60 * 2**20),
-        cost_estimate=pl.CostEstimate(
-            flops=2 * rows * width * outs[0][0][0], bytes_accessed=2 * rows * width, transcendentals=0
-        ),
+        out_shape=[jax.ShapeDtypeStruct(*o) if isinstance(o, tuple) else o for o in outs],
+        scratch_shapes=extra,
+        compiler_params=pltpu.CompilerParams(vmem_limit_bytes=grant * 2**20),
+        cost_estimate=pl.CostEstimate(flops=flops, bytes_accessed=moved, transcendentals=0),
     )(*operands)
 
 
-def norm_kernel(parts, tokens, cotan, gain, x_hat, scale, blocks):
+def fetch_copies(start, weight, held, sems):
+    count = sems.shape[0]
+    step = held.shape[0] // count
+    return [
+        pltpu.make_async_copy(
+            weight.at[pl.ds(start + part * step, step)], held.at[pl.ds(part * step, step)], sems.at[part]
+        )
+        for part in range(count)
+    ]
+
+
+def fetch_kernel(start, weight, held, sems):
+    copies = fetch_copies(start, weight, held, sems)
+    for copy in copies:
+        copy.start()
+    for copy in copies:
+        copy.wait()
+
+
+def norm_kernel(parts, tokens, cotan, gain, weight, x_hat, scale, blocks, held, sems):
+    copies = fetch_copies(0, weight, held, sems)
+    for copy in copies:
+        copy.start()
     normed, x_hat[...], inv_std = normalise(tokens[...], gain[...])
     scale[...] = jnp.broadcast_to(inv_std, scale.shape)
     cols = normed.shape[1] // parts
@@ -97,68 +97,94 @@
         span = slice(part * cols, (part + 1) * cols)
         blocks[part, 0] = normed[:, span]
         blocks[part, 1] = cotan[:, span]
+    for copy in copies:
+        copy.wait()
 
 
 def preact_kernel(step, count, *refs):
-    pieces, (gain, weight, hidden, slope, normed, buffer, sems, total) = refs[:count], refs[count:]
-    stream = Stream(weight, buffer, sems, step)
-    stream.start()
+    pieces, rest = refs[:count], refs[count:]
+    gain, first, second, down, hidden, slope, normed, held, sems = rest
+    copies = fetch_copies(0, down, held, sems)
+    for copy in copies:
+        copy.start()
+    cut = first.shape[0]
     row = 0
     for piece in pieces:
         normed[row : row + piece.shape[0], :] = normalise(piece[...], gain[...])[0]
         row += piece.shape[0]
-    total[...] = jnp.zeros_like(total)
 
     def body(part, carry):
-        stream.copy(part).wait()
         span = pl.ds(pl.multiple_of(part * step, step), step)
-        total[...] += contract(normed[:, span], buffer[span, :], ((1,), (0,)))
+        total = contract(normed[:, :cut], first[:, span], ((1,), (0,)))
+        total += contract(normed[:, cut:], second[:, span], ((1,), (0,)))
+        hidden[:, span] = gelu_value(total).astype(jnp.bfloat16)
+        slope[:, span] = gelu_slope(total)
         return carry
 
-    lax.fori_loop(0, weight.shape[0] // step, body, 0)
-    hidden[...] = gelu_value(total[...]).astype(jnp.bfloat16)
-    slope[...] = gelu_slope(total[...])
-
-
-def hidgrad_kernel(step, span_of, count, *refs):
-    pieces, (weight, slope, pre, buffer, sems, cotan) = refs[:count], refs[count:]
-    stream = Stream(weight, buffer, sems, step)
-    stream.start()
+    lax.fori_loop(0, first.shape[1] // step, body, 0)
+    for copy in copies:
+        copy.wait()
+
+
+def hidgrad_kernel(step, count, *refs):
+    pieces, (first, slope, weight, pre, cotan, held, sems) = refs[:count], refs[count:]
+    slots = held.shape[0]
+    parts = weight.shape[0] // step
+
+    def copy(part):
+        start = part * step if isinstance(part, int) else pl.multiple_of(part * step, step)
+        slot = lax.rem(part, slots)
+        return pltpu.make_async_copy(weight.at[pl.ds(start, step)], held.at[slot], sems.at[part])
+
+    def product(part_of_weight, part):
+        span = pl.ds(pl.multiple_of(part * step, step), step)
+        hid_grad = contract(part_of_weight[...], cotan[...], ((1,), (1,))).T
+        pre[:, span] = (hid_grad * slope[:, span]).astype(jnp.bfloat16)
+
+    if parts > 1:
+        copy(1).start()
     row = 0
     for piece in pieces:
         cotan[row : row + piece.shape[0], :] = piece[...]
         row += piece.shape[0]
+    product(first, 0)
 
     def body(part, carry):
-        for inner in range(span_of // step):
-            stream.copy(part * (span_of // step) + inner).wait()
-        span = pl.ds(pl.multiple_of(part * span_of, span_of), span_of)
-        hid_grad = contract(buffer[span, :], cotan[...], ((1,), (1,))).T
-        pre[:, span] = (hid_grad * slope[:, span]).astype(jnp.bfloat16)
+        copy(part).wait()
+
+        @pl.when(part + 1 < parts)
+        def _():
+            copy(part + 1).start()
+
+        product(held.at[lax.rem(part, slots)], part)
         return carry
 
-    lax.fori_loop(0, weight.shape[0] // span_of, body, 0)
-
-
-def normgrad_kernel(step, pre, weight, normed, gain, mine, other, gain_part, buffer, sems):
+    lax.fori_loop(1, parts, body, 0)
+
+
+def normgrad_kernel(step, pre, first, second, normed, gain, mine, other, gain_part):
     half = mine.shape[0]
-    stream = Stream(weight, buffer, sems, step)
-    stream.start()
-
-    def body(part, carry):
-        stream.copy(part).wait()
-        span = pl.ds(pl.multiple_of(part * step, step), step)
-        grad = contract(pre[...], buffer[span, :], ((1,), (1,)))
-        mine[:, span] = grad[:half].astype(jnp.bfloat16)
-        other[:, span] = grad[half:].astype(jnp.bfloat16)
-        x_hat = normed[:, span].astype(jnp.float32) / gain[:, span]
-        gain_part[:, span] = jnp.sum(grad * x_hat, axis=0, keepdims=True)
-        return carry
-
-    lax.fori_loop(0, weight.shape[0] // step, body, 0)
+
+    def half_of(weight, offset):
+        def body(part, carry):
+            rows = pl.ds(pl.multiple_of(part * step, step), step)
+            span = pl.ds(pl.multiple_of(offset + part * step, 128), step)
+            grad = contract(weight[rows, :], pre[...], ((1,), (1,))).T
+            mine[:, span] = grad[:half].astype(jnp.bfloat16)
+            other[:, span] = grad[half:].astype(jnp.bfloat16)
+            x_hat = normed[:, span].astype(jnp.float32) / gain[:, span]
+            gain_part[:, span] = jnp.sum(grad * x_hat, axis=0, keepdims=True)
+            return carry
+
+        lax.fori_loop(0, weight.shape[0] // step, body, 0)
+
+    half_of(first, 0)
+    half_of(second, first.shape[0])
 
 
 def layer(tokens, norm_gain, up_weight, down_weight, out_grad):
+    up_weight = pltpu.with_memory_space_constraint(up_weight, pltpu.HBM)
+    down_weight = pltpu.with_memory_space_constraint(down_weight, pltpu.HBM)
     n_dp, n_mp = lax.axis_size("dp"), lax.axis_size("mp")
     chips = n_mp // 2
     rows, width = tokens.shape
@@ -200,18 +226,32 @@
     token_pieces = gathered(tokens, True)
     cotan_pieces = gathered(out_grad, False)
     gain_row = norm_gain.reshape(1, width)
-    x_hat, scale, blocks = pl.pallas_call(
+    first = width // 2
+    fetch_sems = [pltpu.SemaphoreType.DMA((4,))]
+    x_hat, scale, blocks, up_first = pl.pallas_call(
         functools.partial(norm_kernel, n_dp),
-        in_specs=[WHOLE] * 3,
-        out_specs=[WHOLE] * 3,
+        in_specs=[WHOLE] * 3 + [STAYS],
+        out_specs=[WHOLE] * 4,
+        scratch_shapes=fetch_sems,
+        compiler_params=pltpu.CompilerParams(vmem_limit_bytes=5 * 2**20),
         out_shape=[
             jax.ShapeDtypeStruct((rows, width), jnp.float32),
             jax.ShapeDtypeStruct((rows, 128), jnp.float32),
             jax.ShapeDtypeStruct((n_dp, 2, rows, cols), jnp.bfloat16),
+            pltpu.VMEM((first, units), jnp.bfloat16),
         ],
         name="ln",
-    )(tokens, out_grad, gain_row)
+    )(tokens, out_grad, gain_row, up_weight)
     inv_std = scale[:, :1]
+    up_second = pl.pallas_call(
+        functools.partial(fetch_kernel, first),
+        in_specs=[STAYS],
+        out_specs=WHOLE,
+        scratch_shapes=fetch_sems,
+        compiler_params=pltpu.CompilerParams(vmem_limit_bytes=2 * 2**20),
+        out_shape=pltpu.VMEM((width - first, units), jnp.bfloat16),
+        name="fetch",
+    )(up_weight)
 
     def column_shards(k):
         both = lax.dynamic_index_in_dim(blocks, me ^ k, 0, keepdims=False)
@@ -227,35 +267,37 @@
     float_units, half_units = ((group, units), jnp.float32), ((group, units), jnp.bfloat16)
     half_width = ((group, width), jnp.bfloat16)
     core_width = ((rows * chips, width), jnp.bfloat16)
-    step, count = chunk(width, 384, 128), len(token_pieces)
-    hidden, slope, normed_all = call(
-        functools.partial(preact_kernel, step, count),
-        (*token_pieces, gain_row, up_weight),
-        [WHOLE] * (count + 1) + [STAYS],
-        (half_units, float_units, half_width),
-        up_weight,
-        step,
-        (pltpu.VMEM(*float_units),),
-    )
-    span_of, count = chunk(units, 512, 128), len(cotan_pieces)
-    step = chunk(span_of, 256, 128)
+    flops = 2 * group * width * units
+    part_rows = chunk(units, 512, 128)
+    hidden, slope, normed_all, down_first = call(
+        functools.partial(preact_kernel, chunk(units, 512, 128), len(token_pieces)),
+        (*token_pieces, gain_row, up_first, up_second, down_weight),
+        (half_units, float_units, half_width, pltpu.VMEM((part_rows, width), jnp.bfloat16)),
+        5,
+        flops,
+        fetch_sems,
+        1,
+    )
+    step = part_rows
     (pre_grad,) = call(
-        functools.partial(hidgrad_kernel, step, span_of, count),
-        (*cotan_pieces, down_weight, slope),
-        [WHOLE] * count + [STAYS, WHOLE],
+        functools.partial(hidgrad_kernel, step, len(cotan_pieces)),
+        (*cotan_pieces, down_first, slope, down_weight),
         (half_units,),
-        down_weight,
-        step,
-        (pltpu.VMEM(*half_width),),
-    )
-    step = chunk(width, 768, 128)
+        16,
+        flops,
+        (
+            pltpu.VMEM(*half_width),
+            pltpu.VMEM((2, step, width), jnp.bfloat16),
+            pltpu.SemaphoreType.DMA((units // step,)),
+        ),
+        1,
+    )
     mine, other, gain_grad = call(
-        functools.partial(normgrad_kernel, step),
-        (pre_grad, up_weight, normed_all, gain_row),
-        [WHOLE, STAYS, WHOLE, WHOLE],
+        functools.partial(normgrad_kernel, chunk(first, 1536, 128)),
+        (pre_grad, up_first, up_second, normed_all, gain_row),
         (core_width, core_width, ((1, width), jnp.float32)),
-        up_weight,
-        step,
+        5,
+        flops,
     )
 
     hidden_all = jnp.concatenate(replicas(hidden, True), axis=0)

time: 174 us -> 182 us (1.046)
  local copies, waits for them, and re-layouts: 3.83 us -> 26.7 us
  waiting for transfers between devices: 79.8 us -> 67.9 us
  Pallas kernels: 41.5 us -> 35.1 us
  starting transfers between devices: 32.9 us -> 36 us
    unnamed x42, local copies, waits for them, and re-layouts: 2.1 us -> 26.1 us
    ppermute x15, waiting for transfers between devices: 52.1 us -> 41.8 us  [along_ring(): return lax.ppermute(array, 'mp', ring_perm(n_mp, shift))]
    pallas_call x3 -> x4, Pallas kernels: 39.3 us -> 30.4 us  [the longest x3 25.7 us: call(): pl.pallas_call(kernel, in_specs=[WHOLE] * (len(operands) - stay) + [STAYS...]
    pallas_call x1, Pallas kernels: 2.21 us -> 4.7 us  [layer(): pl.pallas_call(functools.partial(norm_kernel, n_dp), in_specs=[WHOLE] * 3...]
  transfers between devices with their start and end apart: 40 -> 40, of which waited for: 12 -> 10; matrix products, arithmetic and copies ran while one was open for 6% -> 5% of each run, Pallas kernels for 24% -> 19%
where the time goes in v3:
time: 182 us; the launch traced here: 180 us
  waiting for transfers between devices  67.9 us (37%)
  starting transfers between devices  36 us (20%)
  Pallas kernels  35.1 us (19%)
  local copies, waits for them, and re-layouts  26.7 us (15%)
  matrix products  10.8 us (6%)
  other arithmetic  2.81 us (2%)
    ppermute x15, waiting for transfers between devices, along_ring(): return lax.ppermute(array, 'mp', ring_perm(n_mp, shift))  41.8 us
    unnamed x42, local copies, waits for them, and re-layouts  26.1 us
    pallas_call x3, Pallas kernels, call(): pl.pallas_call(kernel, in_specs=[WHOLE] * (len(operands) - stay) + [STAYS...  25.7 us
    ppermute x11, waiting for transfers between devices, replica(): return lax.ppermute(array, 'dp', swap_perm(n_dp, mask))  24.8 us
    ppermute x15, starting transfers between devices, along_ring(): return lax.ppermute(array, 'mp', ring_perm(n_mp, shift))  20.3 us
    ppermute x11, starting transfers between devices, replica(): return lax.ppermute(array, 'dp', swap_perm(n_dp, mask))  12.8 us
    dot_general x2, matrix products, contract(): lax.dot_general(a, b, (dims, ((), ())), preferred_element_type=jnp.float32)  10.8 us
    pallas_call x1, Pallas kernels, layer(): pl.pallas_call(functools.partial(fetch_kernel, first), in_specs=[STAYS],...  4.72 us
  transfers between devices with their start and end apart: 40, of which 10 were waited for; matrix products, arithmetic and copies ran while one was open for 5% of the time, Pallas kernels for 19%

profile of v3, /device:TPU:10, one launch (start us, length us, event | category | flops | bytes accessed | tf_op | source)
XLA Modules:
  0.0 180.3 jit_solution(16258250737072781428)
XLA Ops:
  0.6 0.5 collective-permute-start.7
  1.1 7.3 %collective-permute-done.7.refs_1_ = bf16[16,6144]{1,0:T(8,128)(2,1)S(1)} collective-permute-done((bf16[16,6144]{1,0:T(8,128)(2,1)}, bf16[16,6144]{1,0:T(8,128)(2,1)S(1)}, u32[]{:S(2)}, u32[]{:S(2)}) %collective-permute-start.7) | collective-permute-done | bytes 196640 | tf_op jit(solution)/shard_map/ppermute | solution.py:198
  8.4 3.0 %collective-permute-start = (bf16[16,6144]{1,0:T(8,128)(2,1)}, bf16[16,6144]{1,0:T(8,128)(2,1)S(1)}, u32[]{:S(2)}, u32[]{:S(2)}) collective-permute-start(bf16[16,6144]{1,0:T(8,128)(2,1)} %refs_0_.3), channel_id=1, source_target_pairs={{0,4},{1,5},{2,0},{3,1},{4,6},{5,7},{6,2},{7,3},{8,12},{9,13},{10,... | collective-permute-start | bytes 589832 | tf_op jit(solution)/shard_map/ppermute | solution.py:198
  11.5 5.7 %collective-permute-done.8.refs_2_ = bf16[16,6144]{1,0:T(8,128)(2,1)S(1)} collective-permute-done((bf16[16,6144]{1,0:T(8,128)(2,1)S(1)}, bf16[16,6144]{1,0:T(8,128)(2,1)S(1)}, u32[]{:S(2)}, u32[]{:S(2)}) %collective-permute-start.8) | collective-permute-done | bytes 196640 | tf_op jit(solution)/shard_map/ppermute | solution.py:198
  17.2 1.4 collective-permute-start.1
  18.6 3.8 %collective-permute-start.2 = (bf16[16,6144]{1,0:T(8,128)(2,1)}, bf16[16,6144]{1,0:T(8,128)(2,1)S(1)}, u32[]{:S(2)}, u32[]{:S(2)}) collective-permute-start(bf16[16,6144]{1,0:T(8,128)(2,1)} %refs_0_.3), channel_id=1, source_target_pairs={{0,2},{1,3},{2,6},{3,7},{4,0},{5,1},{6,4},{7,5},{8,10},{9,11},{10,... | collective-permute-start | bytes 589832 | tf_op jit(solution)/shard_map/ppermute | solution.py:198
  22.4 4.7 %fetch.1.refs_10_.second = bf16[3072,2048]{1,0:T(8,128)(2,1)S(1)} custom-call(bf16[6144,2048]{1,0:T(8,128)(2,1)} %weight.3), custom_call_target="tpu_custom_call" | custom-call | tf_op jit(solution)/shard_map/fetch/pallas_call | solution.py:246
  27.1 4.5 %copy-done = bf16[3072,2048]{1,0:T(8,128)(2,1)} copy-done((bf16[3072,2048]{1,0:T(8,128)(2,1)}, bf16[3072,2048]{1,0:T(8,128)(2,1)S(1)}, u32[]{:S(2)}) %copy-start) | copy-done | bytes 12582936
  31.7 4.7 %ln.1 = (f32[16,6144]{1,0:T(8,128)S(1)}, f32[16,128]{1,0:T(8,128)S(1)}, bf16[4,2,16,1536]{3,2,1,0:T(8,128)(2,1)S(1)}, bf16[3072,2048]{1,0:T(8,128)(2,1)S(1)}) custom-call(bf16[16,6144]{1,0:T(8,128)(2,1)S(1)} %copy-done.6, bf16[16,6144]{1,0:T(8,128)(2,1)S(1)} %copy-done.7, f32[1,6144]{1,0:T(1,128)S(1)} %bitcast.34, bf16[6144,2048]{1,0:T(8,128)(2,1)} %weight.3), custom_call_target="tpu_custom_call" | custom-call | tf_op jit(solution)/shard_map/ln/pallas_call | solution.py:231
  36.4 4.6 %copy-done.2 = bf16[3072,2048]{1,0:T(8,128)(2,1)} copy-done((bf16[3072,2048]{1,0:T(8,128)(2,1)}, bf16[3072,2048]{1,0:T(8,128)(2,1)S(1)}, u32[]{:S(2)}) %copy-start.2) | copy-done | bytes 12582936
  41.0 0.5 collective-permute-start.12
  41.5 0.1 collective-permute-start.13
  41.6 0.5 collective-permute-start.3
  42.1 0.5 collective-permute-start.18
  42.7 0.5 collective-permute-start.5
  43.3 4.6 %copy-done.1 = bf16[3072,2048]{1,0:T(8,128)(2,1)S(1)} copy-done((bf16[3072,2048]{1,0:T(8,128)(2,1)S(1)}, bf16[3072,2048]{1,0:T(8,128)(2,1)}, u32[]{:S(2)}) %copy-start.1) | copy-done | bytes 12582936
  47.8 4.6 %copy-done.3 = bf16[3072,2048]{1,0:T(8,128)(2,1)S(1)} copy-done((bf16[3072,2048]{1,0:T(8,128)(2,1)S(1)}, bf16[3072,2048]{1,0:T(8,128)(2,1)}, u32[]{:S(2)}) %copy-start.3) | copy-done | bytes 12582936
  52.4 0.9 copy-done.10
  53.3 0.9 copy-done.12
  54.3 5.7 %shard_map.84 = (bf16[128,2048]{1,0:T(8,128)(2,1)S(1)}, f32[128,2048]{1,0:T(8,128)S(1)}, bf16[128,6144]{1,0:T(8,128)(2,1)S(1)}, bf16[512,6144]{1,0:T(8,128)(2,1)S(1)}) custom-call(bf16[16,6144]{1,0:T(8,128)(2,1)S(1)} %copy-done.6, bf16[16,6144]{1,0:T(8,128)(2,1)S(1)} %collective-permute-done.7.refs_1_, bf16[16,6144]{1,0:T(8,128)(2,1)S(1)} %collective-permute-done.8.refs_2_, ...), custom_call_target="tpu_custom_call" | custom-call | flops 3221225472 | bytes 51929088 | tf_op jit(solution)/shard_map/pallas_call | solution.py:59
  60.0 3.2 %copy-done.4 = bf16[512,6144]{1,0:T(8,128)(2,1)} copy-done((bf16[512,6144]{1,0:T(8,128)(2,1)}, bf16[512,6144]{1,0:T(8,128)(2,1)S(1)}, u32[]{:S(2)}) %copy-start.4) | copy-done | bytes 6291480
  63.2 1.5 collective-permute-start.19
  64.7 1.4 collective-permute-start.20
  66.2 2.8 %copy-done.5 = bf16[512,6144]{1,0:T(8,128)(2,1)S(1)} copy-done((bf16[512,6144]{1,0:T(8,128)(2,1)S(1)}, bf16[512,6144]{1,0:T(8,128)(2,1)}, u32[]{:S(2)}) %copy-start.5) | copy-done | bytes 6291480
  69.0 12.3 %shard_map.85.pre = bf16[128,2048]{1,0:T(8,128)(2,1)S(1)} custom-call(bf16[16,6144]{1,0:T(8,128)(2,1)S(1)} %copy-done.7, bf16[16,6144]{1,0:T(8,128)(2,1)S(1)} %collective-permute-done.refs_1_, bf16[16,6144]{1,0:T(8,128)(2,1)S(1)} %collective-permute-done.1.refs_2_, bf16[16,6144]{1,0:T(8,128)(2,1)S(1)} %collective-permute-done.2.refs_3_, ...), custom_call_target="tpu_custom_call" | custom-call | flops 3221225472 | bytes 34078720 | tf_op jit(solution)/shard_map/pallas_call | solution.py:59
  81.4 7.6 %shard_map.86 = (bf16[64,6144]{1,0:T(8,128)(2,1)S(1)}, bf16[64,6144]{1,0:T(8,128)(2,1)S(1)}, f32[1,6144]{1,0:T(1,128)S(1)}) custom-call(bf16[128,2048]{1,0:T(8,128)(2,1)S(1)} %shard_map.85.pre, bf16[3072,2048]{1,0:T(8,128)(2,1)S(1)} %bitcast.33, bf16[3072,2048]{1,0:T(8,128)(2,1)S(1)} %bitcast.31, bf16[128,6144]{1,0:T(8,128)(2,1)S(1)} %get-tuple-element.18.normed, ...), custom_call_target="tpu_custom_call" | custom-call | flops 3221225472 | bytes 27287552 | tf_op jit(solution)/shard_map/pallas_call | solution.py:59
  89.1 0.7 collective-permute-start.35
  89.8 3.7 %collective-permute-start.36 = (f32[1,6144]{1,0:T(1,128)S(1)}, f32[1,6144]{1,0:T(1,128)S(1)}, u32[]{:S(2)}, u32[]{:S(2)}) collective-permute-start(f32[1,6144]{1,0:T(1,128)S(1)} %get-tuple-element.25), channel_id=1, source_target_pairs={{0,2},{1,3},{2,6},{3,7},{4,0},{5,1},{6,4},{7,5},{8,10},{9,11},{10,... | collective-permute-start | bytes 73736 | tf_op jit(solution)/shard_map/ppermute | solution.py:198
  93.7 2.0 %collective-permute-start.21 = (bf16[4,2,16,1536]{3,2,1,0:T(8,128)(2,1)S(1)}, bf16[4,2,16,1536]{3,2,1,0:T(8,128)(2,1)S(1)}, u32[]{:S(2)}, u32[]{:S(2)}) collective-permute-start(bf16[4,2,16,1536]{3,2,1,0:T(8,128)(2,1)S(1)} %get-tuple-element.37), channel_id=1, source_target_pairs={{0,4},{1,5},{2,0},{3,1},{4,6},{5,7},{6,2},{7,3},{8,12},{9,13},{10,... | collective-permute-start | bytes 1179656 | tf_op jit(solution)/shard_map/ppermute | solution.py:198
  95.7 1.4 collective-permute-start.22
  97.2 1.2 collective-permute-done.37
  98.4 0.6 collective-permute-start.38
  99.0 0.1 slice_reduce_fusion
  99.2 3.1 %collective-permute-done.38 = f32[1,6144]{1,0:T(1,128)S(1)} collective-permute-done((f32[1,6144]{1,0:T(1,128)S(1)}, f32[1,6144]{1,0:T(1,128)S(1)}, u32[]{:S(2)}, u32[]{:S(2)}) %collective-permute-start.38) | collective-permute-done | bytes 24608 | tf_op jit(solution)/shard_map/ppermute | solution.py:204
  102.4 1.6 collective-permute-start.39
  103.9 16.4 %collective-permute-done.23 = bf16[4,2,16,1536]{3,2,1,0:T(8,128)(2,1)S(1)} collective-permute-done((bf16[4,2,16,1536]{3,2,1,0:T(8,128)(2,1)S(1)}, bf16[4,2,16,1536]{3,2,1,0:T(8,128)(2,1)S(1)}, u32[]{:S(2)}, u32[]{:S(2)}) %collective-permute-start.23) | collective-permute-done | bytes 393248 | tf_op jit(solution)/shard_map/ppermute | solution.py:198
  120.3 9.0 %collective-permute-done.22 = bf16[4,2,16,1536]{3,2,1,0:T(8,128)(2,1)S(1)} collective-permute-done((bf16[4,2,16,1536]{3,2,1,0:T(8,128)(2,1)S(1)}, bf16[4,2,16,1536]{3,2,1,0:T(8,128)(2,1)S(1)}, u32[]{:S(2)}, u32[]{:S(2)}) %collective-permute-start.22) | collective-permute-done | bytes 393248 | tf_op jit(solution)/shard_map/ppermute | solution.py:198
  129.3 0.2 maximum_bitcast_fusion.1
  129.6 0.5 collective-permute-start.26
  130.1 0.1 collective-permute-start.27
  130.2 0.4 collective-permute-start.14
  130.6 0.6 add_multiply_fusion
  131.3 0.5 collective-permute-start.28
  131.8 1.5 collective-permute-start.32
  133.4 0.2 maximum_bitcast_fusion.2
  133.6 0.3 maximum_bitcast_fusion
  133.9 0.2 convert_add_fusion
  134.2 0.7 collective-permute-start.16
  134.9 2.8 %collective-permute-start.17 = (bf16[16,6144]{1,0:T(8,128)(2,1)S(1)}, bf16[16,6144]{1,0:T(8,128)(2,1)S(1)}, u32[]{:S(2)}, u32[]{:S(2)}) collective-permute-start(bf16[16,6144]{1,0:T(8,128)(2,1)S(1)} %get-tuple-element.34), channel_id=1, source_target_pairs={{0,4},{1,5},{2,0},{3,1},{4,6},{5,7},{6,2},{7,3},{8,12},{9,13},{10,... | collective-permute-start | bytes 589832 | tf_op jit(solution)/shard_map/ppermute | solution.py:198
  137.8 0.2 fusion.23
  138.0 0.1 copy.10
  138.1 0.1 copy.9
  138.2 7.3 %collective-permute-done.32 = bf16[128,2048]{1,0:T(8,128)(2,1)S(1)} collective-permute-done((bf16[128,2048]{1,0:T(8,128)(2,1)S(1)}, bf16[128,2048]{1,0:T(8,128)(2,1)S(1)}, u32[]{:S(2)}, u32[]{:S(2)}) %collective-permute-start.32) | collective-permute-done | bytes 524320 | tf_op jit(solution)/shard_map/ppermute | solution.py:204
  145.5 1.5 collective-permute-start.31
  147.0 1.5 collective-permute-start.29
  148.5 0.5 collective-permute-start.33
  149.0 3.4 %collective-permute-done.16 = bf16[16,6144]{1,0:T(8,128)(2,1)S(1)} collective-permute-done((bf16[16,6144]{1,0:T(8,128)(2,1)S(1)}, bf16[16,6144]{1,0:T(8,128)(2,1)S(1)}, u32[]{:S(2)}, u32[]{:S(2)}) %collective-permute-start.16) | collective-permute-done | bytes 196640 | tf_op jit(solution)/shard_map/ppermute | solution.py:198
  152.4 1.5 collective-permute-start.30
  153.9 0.3 fusion.21
  154.2 0.8 multiply_convert_fusion.2
  155.0 5.2 %collective-permute-done.31 = bf16[128,2048]{1,0:T(8,128)(2,1)S(1)} collective-permute-done((bf16[128,2048]{1,0:T(8,128)(2,1)S(1)}, bf16[128,2048]{1,0:T(8,128)(2,1)S(1)}, u32[]{:S(2)}, u32[]{:S(2)}) %collective-permute-start.31) | collective-permute-done | bytes 524320 | tf_op jit(solution)/shard_map/ppermute | solution.py:204
  160.3 9.2 %collective-permute-done.33 = bf16[128,2048]{1,0:T(8,128)(2,1)S(1)} collective-permute-done((bf16[128,2048]{1,0:T(8,128)(2,1)S(1)}, bf16[128,2048]{1,0:T(8,128)(2,1)S(1)}, u32[]{:S(2)}, u32[]{:S(2)}) %collective-permute-start.33) | collective-permute-done | bytes 524320 | tf_op jit(solution)/shard_map/ppermute | solution.py:204
  169.5 5.4 %multiply_convert_fusion = bf16[2048,1536]{1,0:T(8,128)(2,1)} fusion(bf16[512,1536]{1,0:T(8,128)(2,1)S(1)} %bitcast.38, bf16[128,2048]{1,0:T(8,128)(2,1)S(1)} %collective-permute-done.33, bf16[128,2048]{1,0:T(8,128)(2,1)S(1)} %collective-permute-done.32, bf16[128,2048]{1,0:T(8,128)(2,1)S(1)} %collective-permute-done.31, bf16[128,2048]{1,0:T(8,128)(2,1)S(1)} %copy-done.14), kind=kOutput, calls=%fused_computation | convolution fusion | flops 3235905536 | bytes 9961472 | tf_op jit(solution)/shard_map/dot_general | solution.py:35
  174.9 5.4 %multiply_convert_fusion.1 = bf16[1536,2048]{1,0:T(8,128)(2,1)} fusion(bf16[512,1536]{1,0:T(8,128)(2,1)S(1)} %bitcast.37, bf16[128,2048]{1,0:T(8,128)(2,1)S(1)} %collective-permute-done.30, bf16[128,2048]{1,0:T(8,128)(2,1)S(1)} %collective-permute-done.29, bf16[128,2048]{1,0:T(8,128)(2,1)S(1)} %collective-permute-done.28, ...), kind=kOutput, calls=%fused_computation.1 | convolution fusion | flops 3235905536 | bytes 9961472 | tf_op jit(solution)/shard_map/dot_general | solution.py:35
  (85 shorter events, 0.9 us)
Async XLA Ops:
  0.6 7.8 %collective-permute-start.7 = (bf16[16,6144]{1,0:T(8,128)(2,1)}, bf16[16,6144]{1,0:T(8,128)(2,1)S(1)}, u32[]{:S(2)}, u32[]{:S(2)}) collective-permute-start(bf16[16,6144]{1,0:T(8,128)(2,1)} %refs_0_.2), channel_id=1, source_target_pairs={{0,4},{1,5},{2,0},{3,1},{4,6},{5,7},{6,2},{7,3},{8,12},{9,13},{10,... | collective-permute-start | bytes 589832 | tf_op jit(solution)/shard_map/ppermute | solution.py:198
  8.4 8.8 %collective-permute-start.8 = (bf16[16,6144]{1,0:T(8,128)(2,1)S(1)}, bf16[16,6144]{1,0:T(8,128)(2,1)S(1)}, u32[]{:S(2)}, u32[]{:S(2)}) collective-permute-start(bf16[16,6144]{1,0:T(8,128)(2,1)S(1)} %collective-permute-done.7.refs_1_), channel_id=1, source_target_pairs={{0,4},{1,5},{2,0},{3,1},{4,6},{5,7},{6,2},{7,3},{8,12},{9,13},{10,... | collective-permute-start | bytes 589832 | tf_op jit(solution)/shard_map/ppermute | solution.py:198
  8.4 32.5 %collective-permute-start.10 = (bf16[16,6144]{1,0:T(8,128)(2,1)}, bf16[16,6144]{1,0:T(8,128)(2,1)S(1)}, u32[]{:S(2)}, u32[]{:S(2)}) collective-permute-start(bf16[16,6144]{1,0:T(8,128)(2,1)} %refs_0_.2), channel_id=1, source_target_pairs={{0,1},{1,0},{2,3},{3,2},{4,5},{5,4},{6,7},{7,6},{8,9},{9,8},{10,11... | collective-permute-start | bytes 589832 | tf_op jit(solution)/shard_map/ppermute | solution.py:201
  8.4 32.6 %collective-permute-start = (bf16[16,6144]{1,0:T(8,128)(2,1)}, bf16[16,6144]{1,0:T(8,128)(2,1)S(1)}, u32[]{:S(2)}, u32[]{:S(2)}) collective-permute-start(bf16[16,6144]{1,0:T(8,128)(2,1)} %refs_0_.3), channel_id=1, source_target_pairs={{0,4},{1,5},{2,0},{3,1},{4,6},{5,7},{6,2},{7,3},{8,12},{9,13},{10,... | collective-permute-start | bytes 589832 | tf_op jit(solution)/shard_map/ppermute | solution.py:198
  17.2 24.3 %collective-permute-start.9 = (bf16[16,6144]{1,0:T(8,128)(2,1)S(1)}, bf16[16,6144]{1,0:T(8,128)(2,1)S(1)}, u32[]{:S(2)}, u32[]{:S(2)}) collective-permute-start(bf16[16,6144]{1,0:T(8,128)(2,1)S(1)} %collective-permute-done.8.refs_2_), channel_id=1, source_target_pairs={{0,4},{1,5},{2,0},{3,1},{4,6},{5,7},{6,2},{7,3},{8,12},{9,13},{10,... | collective-permute-start | bytes 589832 | tf_op jit(solution)/shard_map/ppermute | solution.py:198
  17.2 24.4 %collective-permute-start.1 = (bf16[16,6144]{1,0:T(8,128)(2,1)}, bf16[16,6144]{1,0:T(8,128)(2,1)S(1)}, u32[]{:S(2)}, u32[]{:S(2)}) collective-permute-start(bf16[16,6144]{1,0:T(8,128)(2,1)} %refs_0_.3), channel_id=1, source_target_pairs={{0,6},{1,7},{2,4},{3,5},{4,2},{5,3},{6,0},{7,1},{8,14},{9,15},{10,... | collective-permute-start | bytes 589832 | tf_op jit(solution)/shard_map/ppermute | solution.py:198
  18.6 23.5 %collective-permute-start.2 = (bf16[16,6144]{1,0:T(8,128)(2,1)}, bf16[16,6144]{1,0:T(8,128)(2,1)S(1)}, u32[]{:S(2)}, u32[]{:S(2)}) collective-permute-start(bf16[16,6144]{1,0:T(8,128)(2,1)} %refs_0_.3), channel_id=1, source_target_pairs={{0,2},{1,3},{2,6},{3,7},{4,0},{5,1},{6,4},{7,5},{8,10},{9,11},{10,... | collective-permute-start | bytes 589832 | tf_op jit(solution)/shard_map/ppermute | solution.py:198
  22.4 9.3 %copy-start.6 = (bf16[16,6144]{1,0:T(8,128)(2,1)S(1)}, bf16[16,6144]{1,0:T(8,128)(2,1)}, u32[]{:S(2)}) copy-start(bf16[16,6144]{1,0:T(8,128)(2,1)} %refs_0_.2) | copy-start | bytes 589828
  22.4 9.3 %copy-start.7 = (bf16[16,6144]{1,0:T(8,128)(2,1)S(1)}, bf16[16,6144]{1,0:T(8,128)(2,1)}, u32[]{:S(2)}) copy-start(bf16[16,6144]{1,0:T(8,128)(2,1)} %refs_0_.3) | copy-start | bytes 589828
  22.4 9.3 %copy-start.8 = (f32[6144]{0:T(1024)S(1)}, f32[6144]{0:T(1024)}, u32[]{:S(2)}) copy-start(f32[6144]{0:T(1024)} %param.6) | copy-start | bytes 73732
  27.1 4.6 %copy-start = (bf16[3072,2048]{1,0:T(8,128)(2,1)}, bf16[3072,2048]{1,0:T(8,128)(2,1)S(1)}, u32[]{:S(2)}) copy-start(bf16[3072,2048]{1,0:T(8,128)(2,1)S(1)} %fetch.1.refs_10_.second) | copy-start | bytes 37748740
  36.4 4.6 %copy-start.2 = (bf16[3072,2048]{1,0:T(8,128)(2,1)}, bf16[3072,2048]{1,0:T(8,128)(2,1)S(1)}, u32[]{:S(2)}) copy-start(bf16[3072,2048]{1,0:T(8,128)(2,1)S(1)} %get-tuple-element.15.refs_9_.first) | copy-start | bytes 37748740
  41.0 2.3 %copy-start.9 = (bf16[16,6144]{1,0:T(8,128)(2,1)}, bf16[16,6144]{1,0:T(8,128)(2,1)S(1)}, u32[]{:S(2)}) copy-start(bf16[16,6144]{1,0:T(8,128)(2,1)S(1)} %collective-permute-done.10.refs_4_) | copy-start | bytes 589828
  41.0 1.7 collective-permute-start.11
  41.0 1.7 collective-permute-start.12
  41.5 1.8 copy-start.11
  41.5 1.7 collective-permute-start.13
  41.6 21.6 %collective-permute-start.3 = (bf16[16,6144]{1,0:T(8,128)(2,1)S(1)}, bf16[16,6144]{1,0:T(8,128)(2,1)S(1)}, u32[]{:S(2)}, u32[]{:S(2)}) collective-permute-start(bf16[16,6144]{1,0:T(8,128)(2,1)S(1)} %copy-done.7), channel_id=1, source_target_pairs={{0,1},{1,0},{2,3},{3,2},{4,5},{5,4},{6,7},{7,6},{8,9},{9,8},{10,11... | collective-permute-start | bytes 589832 | tf_op jit(solution)/shard_map/ppermute | solution.py:201
  42.1 47.7 %collective-permute-start.18 = (bf16[2,16,1536]{2,1,0:T(8,128)(2,1)S(1)}, bf16[2,16,1536]{2,1,0:T(8,128)(2,1)S(1)}, u32[]{:S(2)}, u32[]{:S(2)}) collective-permute-start(bf16[2,16,1536]{2,1,0:T(8,128)(2,1)S(1)} %get-tuple-element.41), channel_id=1, source_target_pairs={{0,8},{8,0},{16,24},{24,16},{1,9},{9,1},{17,25},{25,17},{2,10},{10... | collective-permute-start | bytes 294920 | tf_op jit(solution)/shard_map/ppermute | solution.py:204
  42.7 22.1 %collective-permute-start.4 = (bf16[16,6144]{1,0:T(8,128)(2,1)S(1)}, bf16[16,6144]{1,0:T(8,128)(2,1)S(1)}, u32[]{:S(2)}, u32[]{:S(2)}) collective-permute-start(bf16[16,6144]{1,0:T(8,128)(2,1)S(1)} %collective-permute-done.refs_1_), channel_id=1, source_target_pairs={{0,1},{1,0},{2,3},{3,2},{4,5},{5,4},{6,7},{7,6},{8,9},{9,8},{10,11... | collective-permute-start | bytes 589832 | tf_op jit(solution)/shard_map/ppermute | solution.py:201
  42.7 23.5 %collective-permute-start.5 = (bf16[16,6144]{1,0:T(8,128)(2,1)S(1)}, bf16[16,6144]{1,0:T(8,128)(2,1)S(1)}, u32[]{:S(2)}, u32[]{:S(2)}) collective-permute-start(bf16[16,6144]{1,0:T(8,128)(2,1)S(1)} %collective-permute-done.1.refs_2_), channel_id=1, source_target_pairs={{0,1},{1,0},{2,3},{3,2},{4,5},{5,4},{6,7},{7,6},{8,9},{9,8},{10,11... | collective-permute-start | bytes 589832 | tf_op jit(solution)/shard_map/ppermute | solution.py:201
  43.2 23.0 %collective-permute-start.6 = (bf16[16,6144]{1,0:T(8,128)(2,1)S(1)}, bf16[16,6144]{1,0:T(8,128)(2,1)S(1)}, u32[]{:S(2)}, u32[]{:S(2)}) collective-permute-start(bf16[16,6144]{1,0:T(8,128)(2,1)S(1)} %collective-permute-done.2.refs_3_), channel_id=1, source_target_pairs={{0,1},{1,0},{2,3},{3,2},{4,5},{5,4},{6,7},{7,6},{8,9},{9,8},{10,11... | collective-permute-start | bytes 589832 | tf_op jit(solution)/shard_map/ppermute | solution.py:201
  43.3 4.6 %copy-start.1 = (bf16[3072,2048]{1,0:T(8,128)(2,1)S(1)}, bf16[3072,2048]{1,0:T(8,128)(2,1)}, u32[]{:S(2)}) copy-start(bf16[3072,2048]{1,0:T(8,128)(2,1)} %copy-done) | copy-start | bytes 37748740
  47.8 4.6 %copy-start.3 = (bf16[3072,2048]{1,0:T(8,128)(2,1)S(1)}, bf16[3072,2048]{1,0:T(8,128)(2,1)}, u32[]{:S(2)}) copy-start(bf16[3072,2048]{1,0:T(8,128)(2,1)} %copy-done.2) | copy-start | bytes 37748740
  52.4 0.9 copy-start.10
  53.3 0.9 copy-start.12
  54.3 27.0 %slice-start = ((s8[12582912]{0:T(1024)(128)(4,1)}), s8[4194304]{0:T(1024)(128)(4,1)S(1)}, s32[]{:S(2)}) async-start(s8[12582912]{0:T(1024)(128)(4,1)} %bitcast.30), calls=%async_computation | async-start | bytes 8388608
  54.3 27.1 %slice-start.1 = ((s8[12582912]{0:T(1024)(128)(4,1)}), s8[4194304]{0:T(1024)(128)(4,1)S(1)}, s32[]{:S(2)}) async-start(s8[12582912]{0:T(1024)(128)(4,1)} %bitcast.30), calls=%async_computation.1 | async-start | bytes 8388608
  54.3 27.1 %slice-start.3 = ((s8[12582912]{0:T(1024)(128)(4,1)}), s8[4194304]{0:T(1024)(128)(4,1)S(1)}, s32[]{:S(2)}) async-start(s8[12582912]{0:T(1024)(128)(4,1)} %bitcast.32), calls=%async_computation.3 | async-start | bytes 8388608
  54.3 27.1 %slice-start.4 = ((s8[12582912]{0:T(1024)(128)(4,1)}), s8[4194304]{0:T(1024)(128)(4,1)S(1)}, s32[]{:S(2)}) async-start(s8[12582912]{0:T(1024)(128)(4,1)} %bitcast.32), calls=%async_computation.4 | async-start | bytes 8388608
  60.0 3.2 %copy-start.4 = (bf16[512,6144]{1,0:T(8,128)(2,1)}, bf16[512,6144]{1,0:T(8,128)(2,1)S(1)}, u32[]{:S(2)}) copy-start(bf16[512,6144]{1,0:T(8,128)(2,1)S(1)} %get-tuple-element.16.refs_8_) | copy-start | bytes 18874372
  63.2 82.3 %copy-start.13 = (bf16[128,2048]{1,0:T(8,128)(2,1)}, bf16[128,2048]{1,0:T(8,128)(2,1)S(1)}, u32[]{:S(2)}) copy-start(bf16[128,2048]{1,0:T(8,128)(2,1)S(1)} %get-tuple-element.24) | copy-start | bytes 1572868
  63.2 30.3 %collective-permute-start.19 = (bf16[2,16,1536]{2,1,0:T(8,128)(2,1)S(1)}, bf16[2,16,1536]{2,1,0:T(8,128)(2,1)S(1)}, u32[]{:S(2)}, u32[]{:S(2)}) collective-permute-start(bf16[2,16,1536]{2,1,0:T(8,128)(2,1)S(1)} %get-tuple-element.40), channel_id=1, source_target_pairs={{0,16},{8,24},{16,0},{24,8},{1,17},{9,25},{17,1},{25,9},{2,18},{10... | collective-permute-start | bytes 294920 | tf_op jit(solution)/shard_map/ppermute | solution.py:204
  64.7 28.8 %collective-permute-start.20 = (bf16[2,16,1536]{2,1,0:T(8,128)(2,1)S(1)}, bf16[2,16,1536]{2,1,0:T(8,128)(2,1)S(1)}, u32[]{:S(2)}, u32[]{:S(2)}) collective-permute-start(bf16[2,16,1536]{2,1,0:T(8,128)(2,1)S(1)} %get-tuple-element.39), channel_id=1, source_target_pairs={{0,24},{8,16},{16,8},{24,0},{1,25},{9,17},{17,9},{25,1},{2,26},{10... | collective-permute-start | bytes 294920 | tf_op jit(solution)/shard_map/ppermute | solution.py:204
  66.2 2.8 %copy-start.5 = (bf16[512,6144]{1,0:T(8,128)(2,1)S(1)}, bf16[512,6144]{1,0:T(8,128)(2,1)}, u32[]{:S(2)}) copy-start(bf16[512,6144]{1,0:T(8,128)(2,1)} %copy-done.4) | copy-start | bytes 18874372
  69.0 12.4 %slice-start.2 = ((s8[12582912]{0:T(1024)(128)(4,1)}), s8[4194304]{0:T(1024)(128)(4,1)S(1)}, s32[]{:S(2)}) async-start(s8[12582912]{0:T(1024)(128)(4,1)} %bitcast.30), calls=%async_computation.2 | async-start | bytes 8388608
  69.0 12.4 %slice-start.5 = ((s8[12582912]{0:T(1024)(128)(4,1)}), s8[4194304]{0:T(1024)(128)(4,1)S(1)}, s32[]{:S(2)}) async-start(s8[12582912]{0:T(1024)(128)(4,1)} %bitcast.32), calls=%async_computation.5 | async-start | bytes 8388608
  89.0 6.7 %collective-permute-start.34 = (f32[1,6144]{1,0:T(1,128)S(1)}, f32[1,6144]{1,0:T(1,128)S(1)}, u32[]{:S(2)}, u32[]{:S(2)}) collective-permute-start(f32[1,6144]{1,0:T(1,128)S(1)} %get-tuple-element.25), channel_id=1, source_target_pairs={{0,4},{1,5},{2,0},{3,1},{4,6},{5,7},{6,2},{7,3},{8,12},{9,13},{10,... | collective-permute-start | bytes 73736 | tf_op jit(solution)/shard_map/ppermute | solution.py:198
  89.1 8.0 %collective-permute-start.35 = (f32[1,6144]{1,0:T(1,128)S(1)}, f32[1,6144]{1,0:T(1,128)S(1)}, u32[]{:S(2)}, u32[]{:S(2)}) collective-permute-start(f32[1,6144]{1,0:T(1,128)S(1)} %get-tuple-element.25), channel_id=1, source_target_pairs={{0,6},{1,7},{2,4},{3,5},{4,2},{5,3},{6,0},{7,1},{8,14},{9,15},{10,... | collective-permute-start | bytes 73736 | tf_op jit(solution)/shard_map/ppermute | solution.py:198
  89.8 7.3 %collective-permute-start.36 = (f32[1,6144]{1,0:T(1,128)S(1)}, f32[1,6144]{1,0:T(1,128)S(1)}, u32[]{:S(2)}, u32[]{:S(2)}) collective-permute-start(f32[1,6144]{1,0:T(1,128)S(1)} %get-tuple-element.25), channel_id=1, source_target_pairs={{0,2},{1,3},{2,6},{3,7},{4,0},{5,1},{6,4},{7,5},{8,10},{9,11},{10,... | collective-permute-start | bytes 73736 | tf_op jit(solution)/shard_map/ppermute | solution.py:198
  93.6 26.7 %collective-permute-start.23 = (bf16[4,2,16,1536]{3,2,1,0:T(8,128)(2,1)S(1)}, bf16[4,2,16,1536]{3,2,1,0:T(8,128)(2,1)S(1)}, u32[]{:S(2)}, u32[]{:S(2)}) collective-permute-start(bf16[4,2,16,1536]{3,2,1,0:T(8,128)(2,1)S(1)} %get-tuple-element.37), channel_id=1, source_target_pairs={{0,2},{1,3},{2,6},{3,7},{4,0},{5,1},{6,4},{7,5},{8,10},{9,11},{10,... | collective-permute-start | bytes 1179656 | tf_op jit(solution)/shard_map/ppermute | solution.py:198
  93.7 26.6 %collective-permute-start.21 = (bf16[4,2,16,1536]{3,2,1,0:T(8,128)(2,1)S(1)}, bf16[4,2,16,1536]{3,2,1,0:T(8,128)(2,1)S(1)}, u32[]{:S(2)}, u32[]{:S(2)}) collective-permute-start(bf16[4,2,16,1536]{3,2,1,0:T(8,128)(2,1)S(1)} %get-tuple-element.37), channel_id=1, source_target_pairs={{0,4},{1,5},{2,0},{3,1},{4,6},{5,7},{6,2},{7,3},{8,12},{9,13},{10,... | collective-permute-start | bytes 1179656 | tf_op jit(solution)/shard_map/ppermute | solution.py:198
  95.7 33.6 %collective-permute-start.22 = (bf16[4,2,16,1536]{3,2,1,0:T(8,128)(2,1)S(1)}, bf16[4,2,16,1536]{3,2,1,0:T(8,128)(2,1)S(1)}, u32[]{:S(2)}, u32[]{:S(2)}) collective-permute-start(bf16[4,2,16,1536]{3,2,1,0:T(8,128)(2,1)S(1)} %get-tuple-element.37), channel_id=1, source_target_pairs={{0,6},{1,7},{2,4},{3,5},{4,2},{5,3},{6,0},{7,1},{8,14},{9,15},{10,... | collective-permute-start | bytes 1179656 | tf_op jit(solution)/shard_map/ppermute | solution.py:198
  97.1 1.3 collective-permute-start.37
  98.4 3.9 %collective-permute-start.38 = (f32[1,6144]{1,0:T(1,128)S(1)}, f32[1,6144]{1,0:T(1,128)S(1)}, u32[]{:S(2)}, u32[]{:S(2)}) collective-permute-start(f32[1,6144]{1,0:T(1,128)S(1)} %add.54), channel_id=1, source_target_pairs={{0,8},{8,0},{16,24},{24,16},{1,9},{9,1},{17,25},{25,17},{2,10},{10... | collective-permute-start | bytes 73736 | tf_op jit(solution)/shard_map/ppermute | solution.py:204
  99.1 32.1 %collective-permute-start.24 = (bf16[4,2,16,1536]{3,2,1,0:T(8,128)(2,1)S(1)}, bf16[4,2,16,1536]{3,2,1,0:T(8,128)(2,1)S(1)}, u32[]{:S(2)}, u32[]{:S(2)}) collective-permute-start(bf16[4,2,16,1536]{3,2,1,0:T(8,128)(2,1)S(1)} %get-tuple-element.37), channel_id=1, source_target_pairs={{0,1},{1,0},{2,3},{3,2},{4,5},{5,4},{6,7},{7,6},{8,9},{9,8},{10,11... | collective-permute-start | bytes 1179656 | tf_op jit(solution)/shard_map/ppermute | solution.py:201
  102.4 27.8 %collective-permute-start.39 = (f32[1,6144]{1,0:T(1,128)S(1)}, f32[1,6144]{1,0:T(1,128)S(1)}, u32[]{:S(2)}, u32[]{:S(2)}) collective-permute-start(f32[1,6144]{1,0:T(1,128)S(1)} %add.55), channel_id=1, source_target_pairs={{0,16},{8,24},{16,0},{24,8},{1,17},{9,25},{17,1},{25,9},{2,18},{10... | collective-permute-start | bytes 73736 | tf_op jit(solution)/shard_map/ppermute | solution.py:204
  129.5 2.3 %collective-permute-start.25 = (bf16[4,2,16,1536]{3,2,1,0:T(8,128)(2,1)S(1)}, bf16[4,2,16,1536]{3,2,1,0:T(8,128)(2,1)S(1)}, u32[]{:S(2)}, u32[]{:S(2)}) collective-permute-start(bf16[4,2,16,1536]{3,2,1,0:T(8,128)(2,1)S(1)} %collective-permute-done.21), channel_id=1, source_target_pairs={{0,1},{1,0},{2,3},{3,2},{4,5},{5,4},{6,7},{7,6},{8,9},{9,8},{10,11... | collective-permute-start | bytes 1179656 | tf_op jit(solution)/shard_map/ppermute | solution.py:201
  129.6 3.7 %collective-permute-start.26 = (bf16[4,2,16,1536]{3,2,1,0:T(8,128)(2,1)S(1)}, bf16[4,2,16,1536]{3,2,1,0:T(8,128)(2,1)S(1)}, u32[]{:S(2)}, u32[]{:S(2)}) collective-permute-start(bf16[4,2,16,1536]{3,2,1,0:T(8,128)(2,1)S(1)} %collective-permute-done.22), channel_id=1, source_target_pairs={{0,1},{1,0},{2,3},{3,2},{4,5},{5,4},{6,7},{7,6},{8,9},{9,8},{10,11... | collective-permute-start | bytes 1179656 | tf_op jit(solution)/shard_map/ppermute | solution.py:201
  130.1 3.2 %collective-permute-start.27 = (bf16[4,2,16,1536]{3,2,1,0:T(8,128)(2,1)S(1)}, bf16[4,2,16,1536]{3,2,1,0:T(8,128)(2,1)S(1)}, u32[]{:S(2)}, u32[]{:S(2)}) collective-permute-start(bf16[4,2,16,1536]{3,2,1,0:T(8,128)(2,1)S(1)} %collective-permute-done.23), channel_id=1, source_target_pairs={{0,1},{1,0},{2,3},{3,2},{4,5},{5,4},{6,7},{7,6},{8,9},{9,8},{10,11... | collective-permute-start | bytes 1179656 | tf_op jit(solution)/shard_map/ppermute | solution.py:201
  130.2 3.7 %collective-permute-start.14 = (bf16[64,6144]{1,0:T(8,128)(2,1)S(1)}, bf16[64,6144]{1,0:T(8,128)(2,1)S(1)}, u32[]{:S(2)}, u32[]{:S(2)}) collective-permute-start(bf16[64,6144]{1,0:T(8,128)(2,1)S(1)} %get-tuple-element.20), channel_id=1, source_target_pairs={{0,1},{1,0},{2,3},{3,2},{4,5},{5,4},{6,7},{7,6},{8,9},{9,8},{10,11... | collective-permute-start | bytes 2359304 | tf_op jit(solution)/shard_map/ppermute | solution.py:201
  131.3 15.7 %collective-permute-start.28 = (bf16[128,2048]{1,0:T(8,128)(2,1)S(1)}, bf16[128,2048]{1,0:T(8,128)(2,1)S(1)}, u32[]{:S(2)}, u32[]{:S(2)}) collective-permute-start(bf16[128,2048]{1,0:T(8,128)(2,1)S(1)} %shard_map.85.pre), channel_id=1, source_target_pairs={{0,8},{8,0},{16,24},{24,16},{1,9},{9,1},{17,25},{25,17},{2,10},{10... | collective-permute-start | bytes 1572872 | tf_op jit(solution)/shard_map/ppermute | solution.py:204
  131.8 13.6 %collective-permute-start.32 = (bf16[128,2048]{1,0:T(8,128)(2,1)S(1)}, bf16[128,2048]{1,0:T(8,128)(2,1)S(1)}, u32[]{:S(2)}, u32[]{:S(2)}) collective-permute-start(bf16[128,2048]{1,0:T(8,128)(2,1)S(1)} %get-tuple-element.24), channel_id=1, source_target_pairs={{0,16},{8,24},{16,0},{24,8},{1,17},{9,25},{17,1},{25,9},{2,18},{10... | collective-permute-start | bytes 1572872 | tf_op jit(solution)/shard_map/ppermute | solution.py:204
  134.1 14.4 %collective-permute-start.15 = (bf16[16,6144]{1,0:T(8,128)(2,1)S(1)}, bf16[16,6144]{1,0:T(8,128)(2,1)S(1)}, u32[]{:S(2)}, u32[]{:S(2)}) collective-permute-start(bf16[16,6144]{1,0:T(8,128)(2,1)S(1)} %get-tuple-element.33), channel_id=1, source_target_pairs={{0,2},{1,3},{2,6},{3,7},{4,0},{5,1},{6,4},{7,5},{8,10},{9,11},{10,... | collective-permute-start | bytes 589832 | tf_op jit(solution)/shard_map/ppermute | solution.py:198
  134.2 18.2 %collective-permute-start.16 = (bf16[16,6144]{1,0:T(8,128)(2,1)S(1)}, bf16[16,6144]{1,0:T(8,128)(2,1)S(1)}, u32[]{:S(2)}, u32[]{:S(2)}) collective-permute-start(bf16[16,6144]{1,0:T(8,128)(2,1)S(1)} %get-tuple-element.35), channel_id=1, source_target_pairs={{0,6},{1,7},{2,4},{3,5},{4,2},{5,3},{6,0},{7,1},{8,14},{9,15},{10,... | collective-permute-start | bytes 589832 | tf_op jit(solution)/shard_map/ppermute | solution.py:198
  134.9 19.0 %collective-permute-start.17 = (bf16[16,6144]{1,0:T(8,128)(2,1)S(1)}, bf16[16,6144]{1,0:T(8,128)(2,1)S(1)}, u32[]{:S(2)}, u32[]{:S(2)}) collective-permute-start(bf16[16,6144]{1,0:T(8,128)(2,1)S(1)} %get-tuple-element.34), channel_id=1, source_target_pairs={{0,4},{1,5},{2,0},{3,1},{4,6},{5,7},{6,2},{7,3},{8,12},{9,13},{10,... | collective-permute-start | bytes 589832 | tf_op jit(solution)/shard_map/ppermute | solution.py:198
  145.5 14.8 %collective-permute-start.31 = (bf16[128,2048]{1,0:T(8,128)(2,1)S(1)}, bf16[128,2048]{1,0:T(8,128)(2,1)S(1)}, u32[]{:S(2)}, u32[]{:S(2)}) collective-permute-start(bf16[128,2048]{1,0:T(8,128)(2,1)S(1)} %get-tuple-element.24), channel_id=1, source_target_pairs={{0,8},{8,0},{16,24},{24,16},{1,9},{9,1},{17,25},{25,17},{2,10},{10... | collective-permute-start | bytes 1572872 | tf_op jit(solution)/shard_map/ppermute | solution.py:204
  146.9 22.5 %copy-start.14 = (bf16[128,2048]{1,0:T(8,128)(2,1)S(1)}, bf16[128,2048]{1,0:T(8,128)(2,1)}, u32[]{:S(2)}) copy-start(bf16[128,2048]{1,0:T(8,128)(2,1)} %copy-done.13) | copy-start | bytes 1572868
  147.0 27.9 %collective-permute-start.29 = (bf16[128,2048]{1,0:T(8,128)(2,1)S(1)}, bf16[128,2048]{1,0:T(8,128)(2,1)S(1)}, u32[]{:S(2)}, u32[]{:S(2)}) collective-permute-start(bf16[128,2048]{1,0:T(8,128)(2,1)S(1)} %shard_map.85.pre), channel_id=1, source_target_pairs={{0,16},{8,24},{16,0},{24,8},{1,17},{9,25},{17,1},{25,9},{2,18},{10... | collective-permute-start | bytes 1572872 | tf_op jit(solution)/shard_map/ppermute | solution.py:204
  148.5 21.0 %collective-permute-start.33 = (bf16[128,2048]{1,0:T(8,128)(2,1)S(1)}, bf16[128,2048]{1,0:T(8,128)(2,1)S(1)}, u32[]{:S(2)}, u32[]{:S(2)}) collective-permute-start(bf16[128,2048]{1,0:T(8,128)(2,1)S(1)} %collective-permute-done.32), channel_id=1, source_target_pairs={{0,8},{8,0},{16,24},{24,16},{1,9},{9,1},{17,25},{25,17},{2,10},{10... | collective-permute-start | bytes 1572872 | tf_op jit(solution)/shard_map/ppermute | solution.py:204
  152.4 22.5 %collective-permute-start.30 = (bf16[128,2048]{1,0:T(8,128)(2,1)S(1)}, bf16[128,2048]{1,0:T(8,128)(2,1)S(1)}, u32[]{:S(2)}, u32[]{:S(2)}) collective-permute-start(bf16[128,2048]{1,0:T(8,128)(2,1)S(1)} %collective-permute-done.28), channel_id=1, source_target_pairs={{0,16},{8,24},{16,0},{24,8},{1,17},{9,25},{17,1},{25,9},{2,18},{10... | collective-permute-start | bytes 1572872 | tf_op jit(solution)/shard_map/ppermute | solution.py:204

commit v4 on v3

--- a/solution.py
+++ b/solution.py
@@ -86,17 +86,12 @@
         copy.wait()
 
 
-def norm_kernel(parts, tokens, cotan, gain, weight, x_hat, scale, blocks, held, sems):
+def norm_kernel(tokens, gain, weight, x_hat, scale, held, sems):
     copies = fetch_copies(0, weight, held, sems)
     for copy in copies:
         copy.start()
-    normed, x_hat[...], inv_std = normalise(tokens[...], gain[...])
+    _, x_hat[...], inv_std = normalise(tokens[...], gain[...])
     scale[...] = jnp.broadcast_to(inv_std, scale.shape)
-    cols = normed.shape[1] // parts
-    for part in range(parts):
-        span = slice(part * cols, (part + 1) * cols)
-        blocks[part, 0] = normed[:, span]
-        blocks[part, 1] = cotan[:, span]
     for copy in copies:
         copy.wait()
 
@@ -228,20 +223,19 @@
     gain_row = norm_gain.reshape(1, width)
     first = width // 2
     fetch_sems = [pltpu.SemaphoreType.DMA((4,))]
-    x_hat, scale, blocks, up_first = pl.pallas_call(
-        functools.partial(norm_kernel, n_dp),
-        in_specs=[WHOLE] * 3 + [STAYS],
-        out_specs=[WHOLE] * 4,
+    x_hat, scale, up_first = pl.pallas_call(
+        norm_kernel,
+        in_specs=[WHOLE] * 2 + [STAYS],
+        out_specs=[WHOLE] * 3,
         scratch_shapes=fetch_sems,
         compiler_params=pltpu.CompilerParams(vmem_limit_bytes=5 * 2**20),
         out_shape=[
             jax.ShapeDtypeStruct((rows, width), jnp.float32),
             jax.ShapeDtypeStruct((rows, 128), jnp.float32),
-            jax.ShapeDtypeStruct((n_dp, 2, rows, cols), jnp.bfloat16),
             pltpu.VMEM((first, units), jnp.bfloat16),
         ],
         name="ln",
-    )(tokens, out_grad, gain_row, up_weight)
+    )(tokens, gain_row, up_weight)
     inv_std = scale[:, :1]
     up_second = pl.pallas_call(
         functools.partial(fetch_kernel, first),
@@ -253,16 +247,18 @@
         name="fetch",
     )(up_weight)
 
+    def block_of(array, k):
+        return lax.dynamic_slice_in_dim(array, (me ^ k) * cols, cols, axis=1)
+
     def column_shards(k):
-        both = lax.dynamic_index_in_dim(blocks, me ^ k, 0, keepdims=False)
-        return replica(both, k) if k else both
+        block = block_of(out_grad, k)
+        return replica(block, k) if k else block
 
     shard_list = [column_shards(k) for k in range(n_dp)]
     shard = jnp.stack(shard_list)
     shards_mine, shards_other = spread(shard, False)
     columns = jnp.stack([jnp.stack(shards_mine), jnp.stack(shards_other)])
-    columns = columns.transpose(3, 2, 0, 1, 4, 5).reshape(2, -1, cols)
-    normed_cols, cotan_cols = columns[0], columns[1]
+    cotan_cols = columns.transpose(2, 0, 1, 3, 4).reshape(-1, cols)
 
     float_units, half_units = ((group, units), jnp.float32), ((group, units), jnp.bfloat16)
     half_width = ((group, width), jnp.bfloat16)
@@ -303,12 +299,19 @@
     hidden_all = jnp.concatenate(replicas(hidden, True), axis=0)
     pre_all = jnp.concatenate(replicas(pre_grad, False), axis=0)
 
+    half = rows * chips
+    normed_parts = [block_of(normed_all, 0)]
+    for k in range(1, n_dp):
+        block = replica(block_of(normed_all[:half], k), k)
+        normed_parts += [block, across(block)]
+    normed_cols = jnp.concatenate(normed_parts, axis=0)
+
     received = [along_ring(gain_grad, s) for s in range(1, chips)]
     for part in received:
         gain_grad = gain_grad + part
-    gain_grad = gain_grad + across(gain_grad)
     for bit in range((n_dp - 1).bit_length()):
         gain_grad = gain_grad + replica(gain_grad, 1 << bit)
+    gain_grad = gain_grad + across(gain_grad)
     gain_grad = gain_grad.reshape(width) * factor
 
     total = mine.astype(jnp.float32) + across(other).astype(jnp.float32)

time: 182 us -> 166 us (0.912)
  the two profiles are of different devices: /device:TPU:10 before, /device:TPU:0 now
where the time goes in v4:
time: 166 us
  waiting for transfers between devices  78 us (47%)
  starting transfers between devices  38.3 us (23%)
  Pallas kernels  34.4 us (21%)
  matrix products  10.7 us (6%)
  other arithmetic  2.33 us (1%)
    ppermute x15, waiting for transfers between devices, along_ring(): return lax.ppermute(array, 'mp', ring_perm(n_mp, shift))  46.8 us
    ppermute x14, waiting for transfers between devices, replica(): return lax.ppermute(array, 'dp', swap_perm(n_dp, mask))  29.3 us
    pallas_call x3, Pallas kernels, call(): pl.pallas_call(kernel, in_specs=[WHOLE] * (len(operands) - stay) + [STAYS...  25.1 us
    ppermute x15, starting transfers between devices, along_ring(): return lax.ppermute(array, 'mp', ring_perm(n_mp, shift))  21.6 us
    ppermute x14, starting transfers between devices, replica(): return lax.ppermute(array, 'dp', swap_perm(n_dp, mask))  14.1 us
    dot_general x2, matrix products, contract(): lax.dot_general(a, b, (dims, ((), ())), preferred_element_type=jnp.float32)  10.7 us
    pallas_call x1, Pallas kernels, layer(): pl.pallas_call(norm_kernel, in_specs=[WHOLE] * 2 + [STAYS], out_specs=[WH...  4.69 us
    pallas_call x1, Pallas kernels, layer(): pl.pallas_call(functools.partial(fetch_kernel, first), in_specs=[STAYS],...  4.68 us
  transfers between devices with their start and end apart: 46, of which 18 were waited for; matrix products, arithmetic and copies ran while one was open for 5% of the time, Pallas kernels for 21%

profile of v4, /device:TPU:0, one launch (start us, length us, event | category | flops | bytes accessed | tf_op | source)
XLA Modules:
  0.0 166.0 jit_solution(17500093411384071333)
XLA Ops:
  0.6 4.1 %collective-permute-start.7 = (bf16[16,6144]{1,0:T(8,128)(2,1)}, bf16[16,6144]{1,0:T(8,128)(2,1)S(1)}, u32[]{:S(2)}, u32[]{:S(2)}) collective-permute-start(bf16[16,6144]{1,0:T(8,128)(2,1)} %refs_0_.2), channel_id=1, source_target_pairs={{0,4},{1,5},{2,0},{3,1},{4,6},{5,7},{6,2},{7,3},{8,12},{9,13},{10,... | collective-permute-start | bytes 589832 | tf_op jit(solution)/shard_map/ppermute | solution.py:193
  4.7 4.5 %collective-permute-done.7.refs_1_ = bf16[16,6144]{1,0:T(8,128)(2,1)S(1)} collective-permute-done((bf16[16,6144]{1,0:T(8,128)(2,1)}, bf16[16,6144]{1,0:T(8,128)(2,1)S(1)}, u32[]{:S(2)}, u32[]{:S(2)}) %collective-permute-start.7) | collective-permute-done | bytes 196640 | tf_op jit(solution)/shard_map/ppermute | solution.py:193
  9.2 3.3 %collective-permute-start.8 = (bf16[16,6144]{1,0:T(8,128)(2,1)S(1)}, bf16[16,6144]{1,0:T(8,128)(2,1)S(1)}, u32[]{:S(2)}, u32[]{:S(2)}) collective-permute-start(bf16[16,6144]{1,0:T(8,128)(2,1)S(1)} %collective-permute-done.7.refs_1_), channel_id=1, source_target_pairs={{0,4},{1,5},{2,0},{3,1},{4,6},{5,7},{6,2},{7,3},{8,12},{9,13},{10,... | collective-permute-start | bytes 589832 | tf_op jit(solution)/shard_map/ppermute | solution.py:193
  12.5 0.9 dynamic-slice_bitcast_fusion
  13.4 1.6 collective-permute-start.30
  14.9 1.5 collective-permute-start.31
  16.5 0.5 collective-permute-start.32
  16.9 1.0 collective-permute-done.30
  17.9 0.7 collective-permute-start
  18.6 0.7 collective-permute-done.31
  19.4 1.3 collective-permute-start.1
  20.7 0.7 collective-permute-done.32
  21.5 2.9 %collective-permute-start.9 = (bf16[16,6144]{1,0:T(8,128)(2,1)S(1)}, bf16[16,6144]{1,0:T(8,128)(2,1)S(1)}, u32[]{:S(2)}, u32[]{:S(2)}) collective-permute-start(bf16[16,6144]{1,0:T(8,128)(2,1)S(1)} %collective-permute-done.8.refs_2_), channel_id=1, source_target_pairs={{0,4},{1,5},{2,0},{3,1},{4,6},{5,7},{6,2},{7,3},{8,12},{9,13},{10,... | collective-permute-start | bytes 589832 | tf_op jit(solution)/shard_map/ppermute | solution.py:193
  24.4 0.1 collective-permute-start.3
  24.5 5.6 %collective-permute-done.refs_1_ = bf16[16,6144]{1,0:T(8,128)(2,1)S(1)} collective-permute-done((bf16[16,6144]{1,0:T(8,128)(2,1)}, bf16[16,6144]{1,0:T(8,128)(2,1)S(1)}, u32[]{:S(2)}, u32[]{:S(2)}) %collective-permute-start) | collective-permute-done | bytes 196640 | tf_op jit(solution)/shard_map/ppermute | solution.py:193
  30.2 0.1 collective-permute-start.11
  30.2 14.9 %collective-permute-done.2.refs_3_ = bf16[16,6144]{1,0:T(8,128)(2,1)S(1)} collective-permute-done((bf16[16,6144]{1,0:T(8,128)(2,1)}, bf16[16,6144]{1,0:T(8,128)(2,1)S(1)}, u32[]{:S(2)}, u32[]{:S(2)}) %collective-permute-start.2) | collective-permute-done | bytes 196640 | tf_op jit(solution)/shard_map/ppermute | solution.py:193
  45.2 0.5 collective-permute-start.13
  45.7 4.7 %fetch.1.refs_10_.second = bf16[3072,2048]{1,0:T(8,128)(2,1)S(1)} custom-call(bf16[6144,2048]{1,0:T(8,128)(2,1)} %weight.3), custom_call_target="tpu_custom_call" | custom-call | tf_op jit(solution)/shard_map/fetch/pallas_call | solution.py:240
  50.4 4.7 %ln.1 = (f32[16,6144]{1,0:T(8,128)S(1)}, f32[16,128]{1,0:T(8,128)S(1)}, bf16[3072,2048]{1,0:T(8,128)(2,1)S(1)}) custom-call(bf16[16,6144]{1,0:T(8,128)(2,1)S(1)} %copy-done, f32[1,6144]{1,0:T(1,128)S(1)} %bitcast.33, bf16[6144,2048]{1,0:T(8,128)(2,1)} %weight.3), custom_call_target="tpu_custom_call" | custom-call | tf_op jit(solution)/shard_map/ln/pallas_call | solution.py:226
  55.1 0.1 slice_reduce_fusion
  55.2 2.9 %collective-permute-start.34 = (bf16[4,16,1536]{2,1,0:T(8,128)(2,1)S(1)}, bf16[4,16,1536]{2,1,0:T(8,128)(2,1)S(1)}, u32[]{:S(2)}, u32[]{:S(2)}) collective-permute-start(bf16[4,16,1536]{2,1,0:T(8,128)(2,1)S(1)} %get-tuple-element.36), channel_id=1, source_target_pairs={{0,6},{1,7},{2,4},{3,5},{4,2},{5,3},{6,0},{7,1},{8,14},{9,15},{10,... | collective-permute-start | bytes 589832 | tf_op jit(solution)/shard_map/ppermute | solution.py:193
  58.1 0.1 collective-permute-start.4
  58.2 0.5 collective-permute-start.5
  58.7 0.1 collective-permute-start.6
  58.8 5.7 %shard_map.84 = (bf16[128,2048]{1,0:T(8,128)(2,1)S(1)}, f32[128,2048]{1,0:T(8,128)S(1)}, bf16[128,6144]{1,0:T(8,128)(2,1)S(1)}, bf16[512,6144]{1,0:T(8,128)(2,1)S(1)}) custom-call(bf16[16,6144]{1,0:T(8,128)(2,1)S(1)} %copy-done, bf16[16,6144]{1,0:T(8,128)(2,1)S(1)} %collective-permute-done.7.refs_1_, bf16[16,6144]{1,0:T(8,128)(2,1)S(1)} %collective-permute-done.8.refs_2_, ...), custom_call_target="tpu_custom_call" | custom-call | flops 3221225472 | bytes 51929088 | tf_op jit(solution)/shard_map/pallas_call | solution.py:59
  64.5 0.3 collective-permute-done.34
  64.9 0.2 collective-permute-start.36
  65.0 5.1 %collective-permute-done.35 = bf16[4,16,1536]{2,1,0:T(8,128)(2,1)S(1)} collective-permute-done((bf16[4,16,1536]{2,1,0:T(8,128)(2,1)S(1)}, bf16[4,16,1536]{2,1,0:T(8,128)(2,1)S(1)}, u32[]{:S(2)}, u32[]{:S(2)}) %collective-permute-start.35) | collective-permute-done | bytes 196640 | tf_op jit(solution)/shard_map/ppermute | solution.py:193
  70.1 0.5 collective-permute-start.38
  70.7 11.7 %shard_map.85.pre = bf16[128,2048]{1,0:T(8,128)(2,1)S(1)} custom-call(bf16[16,6144]{1,0:T(8,128)(2,1)S(1)} %copy-done.1, bf16[16,6144]{1,0:T(8,128)(2,1)S(1)} %collective-permute-done.refs_1_, bf16[16,6144]{1,0:T(8,128)(2,1)S(1)} %collective-permute-done.1.refs_2_, bf16[16,6144]{1,0:T(8,128)(2,1)S(1)} %collective-permute-done.2.refs_3_, ...), custom_call_target="tpu_custom_call" | custom-call | flops 3221225472 | bytes 34078720 | tf_op jit(solution)/shard_map/pallas_call | solution.py:59
  82.4 7.7 %shard_map.86 = (bf16[64,6144]{1,0:T(8,128)(2,1)S(1)}, bf16[64,6144]{1,0:T(8,128)(2,1)S(1)}, f32[1,6144]{1,0:T(1,128)S(1)}) custom-call(bf16[128,2048]{1,0:T(8,128)(2,1)S(1)} %shard_map.85.pre, bf16[3072,2048]{1,0:T(8,128)(2,1)S(1)} %get-tuple-element.14.refs_9_.first, bf16[3072,2048]{1,0:T(8,128)(2,1)S(1)} %fetch.1.refs_10_.second, ...), custom_call_target="tpu_custom_call" | custom-call | flops 3221225472 | bytes 27287552 | tf_op jit(solution)/shard_map/pallas_call | solution.py:59
  90.1 1.4 collective-permute-start.41
  91.6 0.9 collective-permute-start.42
  92.4 0.1 maximum_bitcast_fusion.1
  92.5 1.4 collective-permute-done.40
  93.9 2.1 %collective-permute-done.41 = f32[1,6144]{1,0:T(1,128)S(1)} collective-permute-done((f32[1,6144]{1,0:T(1,128)S(1)}, f32[1,6144]{1,0:T(1,128)S(1)}, u32[]{:S(2)}, u32[]{:S(2)}) %collective-permute-start.41) | collective-permute-done | bytes 24608 | tf_op jit(solution)/shard_map/ppermute | solution.py:193
  96.0 0.3 collective-permute-done.42
  96.4 1.6 collective-permute-start.43
  97.9 0.1 pad_maximum_fusion
  98.1 2.2 %collective-permute-done.43 = f32[1,6144]{1,0:T(1,128)S(1)} collective-permute-done((f32[1,6144]{1,0:T(1,128)S(1)}, f32[1,6144]{1,0:T(1,128)S(1)}, u32[]{:S(2)}, u32[]{:S(2)}) %collective-permute-start.43) | collective-permute-done | bytes 24608 | tf_op jit(solution)/shard_map/ppermute | solution.py:199
  100.3 1.6 collective-permute-start.44
  102.0 1.5 collective-permute-start.24
  103.5 0.5 collective-permute-start.28
  104.0 0.1 collective-permute-done.44
  104.4 1.8 %collective-permute-start.18 = (bf16[64,1536]{1,0:T(8,128)(2,1)S(1)}, bf16[64,1536]{1,0:T(8,128)(2,1)S(1)}, u32[]{:S(2)}, u32[]{:S(2)}) collective-permute-start(bf16[64,1536]{1,0:T(8,128)(2,1)S(1)} %get-tuple-element.31), channel_id=1, source_target_pairs={{0,8},{8,0},{16,24},{24,16},{1,9},{9,1},{17,25},{25,17},{2,10},{10... | collective-permute-start | bytes 589832 | tf_op jit(solution)/shard_map/ppermute | solution.py:199
  106.2 1.5 collective-permute-start.20
  107.7 0.5 collective-permute-start.22
  108.2 0.6 add_multiply_fusion
  108.8 11.7 %collective-permute-done.18 = bf16[64,1536]{1,0:T(8,128)(2,1)S(1)} collective-permute-done((bf16[64,1536]{1,0:T(8,128)(2,1)S(1)}, bf16[64,1536]{1,0:T(8,128)(2,1)S(1)}, u32[]{:S(2)}, u32[]{:S(2)}) %collective-permute-start.18) | collective-permute-done | bytes 196640 | tf_op jit(solution)/shard_map/ppermute | solution.py:199
  120.6 3.3 %collective-permute-done.20 = bf16[64,1536]{1,0:T(8,128)(2,1)S(1)} collective-permute-done((bf16[64,1536]{1,0:T(8,128)(2,1)S(1)}, bf16[64,1536]{1,0:T(8,128)(2,1)S(1)}, u32[]{:S(2)}, u32[]{:S(2)}) %collective-permute-start.20) | collective-permute-done | bytes 196640 | tf_op jit(solution)/shard_map/ppermute | solution.py:199
  123.9 0.5 collective-permute-start.21
  124.5 1.9 %collective-permute-done.21 = bf16[64,1536]{1,0:T(8,128)(2,1)S(1)} collective-permute-done((bf16[64,1536]{1,0:T(8,128)(2,1)S(1)}, bf16[64,1536]{1,0:T(8,128)(2,1)S(1)}, u32[]{:S(2)}, u32[]{:S(2)}) %collective-permute-start.21) | collective-permute-done | bytes 196640 | tf_op jit(solution)/shard_map/ppermute | solution.py:196
  126.5 0.2 convert_add_fusion
  126.8 1.9 %collective-permute-start.16 = (bf16[16,6144]{1,0:T(8,128)(2,1)S(1)}, bf16[16,6144]{1,0:T(8,128)(2,1)S(1)}, u32[]{:S(2)}, u32[]{:S(2)}) collective-permute-start(bf16[16,6144]{1,0:T(8,128)(2,1)S(1)} %get-tuple-element.34), channel_id=1, source_target_pairs={{0,6},{1,7},{2,4},{3,5},{4,2},{5,3},{6,0},{7,1},{8,14},{9,15},{10,... | collective-permute-start | bytes 589832 | tf_op jit(solution)/shard_map/ppermute | solution.py:193
  128.8 1.9 %collective-permute-start.17 = (bf16[16,6144]{1,0:T(8,128)(2,1)S(1)}, bf16[16,6144]{1,0:T(8,128)(2,1)S(1)}, u32[]{:S(2)}, u32[]{:S(2)}) collective-permute-start(bf16[16,6144]{1,0:T(8,128)(2,1)S(1)} %get-tuple-element.33), channel_id=1, source_target_pairs={{0,4},{1,5},{2,0},{3,1},{4,6},{5,7},{6,2},{7,3},{8,12},{9,13},{10,... | collective-permute-start | bytes 589832 | tf_op jit(solution)/shard_map/ppermute | solution.py:193
  130.8 0.6 collective-permute-start.27
  131.4 12.5 %collective-permute-done.15 = bf16[16,6144]{1,0:T(8,128)(2,1)S(1)} collective-permute-done((bf16[16,6144]{1,0:T(8,128)(2,1)S(1)}, bf16[16,6144]{1,0:T(8,128)(2,1)S(1)}, u32[]{:S(2)}, u32[]{:S(2)}) %collective-permute-start.15) | collective-permute-done | bytes 196640 | tf_op jit(solution)/shard_map/ppermute | solution.py:193
  144.0 0.8 collective-permute-start.29
  144.8 0.3 fusion.21
  145.1 0.8 multiply_convert_fusion.2
  145.9 9.4 %collective-permute-done.29 = bf16[128,2048]{1,0:T(8,128)(2,1)S(1)} collective-permute-done((bf16[128,2048]{1,0:T(8,128)(2,1)S(1)}, bf16[128,2048]{1,0:T(8,128)(2,1)S(1)}, u32[]{:S(2)}, u32[]{:S(2)}) %collective-permute-start.29) | collective-permute-done | bytes 524320 | tf_op jit(solution)/shard_map/ppermute | solution.py:199
  155.3 5.4 %multiply_convert_fusion = bf16[2048,1536]{1,0:T(8,128)(2,1)} fusion(bf16[512,1536]{1,0:T(8,128)(2,1)S(1)} %bitcast.36, bf16[128,2048]{1,0:T(8,128)(2,1)S(1)} %collective-permute-done.29, bf16[128,2048]{1,0:T(8,128)(2,1)S(1)} %collective-permute-done.28, bf16[128,2048]{1,0:T(8,128)(2,1)S(1)} %collective-permute-done.27, ...), kind=kOutput, calls=%fused_computation | convolution fusion | flops 3235905536 | bytes 9961472 | tf_op jit(solution)/shard_map/dot_general | solution.py:35
  160.7 5.4 %multiply_convert_fusion.1 = bf16[1536,2048]{1,0:T(8,128)(2,1)} fusion(bf16[512,1536]{1,0:T(8,128)(2,1)S(1)} %constant_dynamic-update-slice_fusion, bf16[128,2048]{1,0:T(8,128)(2,1)S(1)} %collective-permute-done.26, bf16[128,2048]{1,0:T(8,128)(2,1)S(1)} %collective-permute-done.25, bf16[128,2048]{1,0:T(8,128)(2,1)S(1)} %collective-permute-done.24, ...), kind=kOutput, calls=%fused_computation.1 | convolution fusion | flops 3235905536 | bytes 9961472 | tf_op jit(solution)/shard_map/dot_general | solution.py:35
  (64 shorter events, 0.9 us)
Async XLA Ops:
  0.6 8.6 %collective-permute-start.7 = (bf16[16,6144]{1,0:T(8,128)(2,1)}, bf16[16,6144]{1,0:T(8,128)(2,1)S(1)}, u32[]{:S(2)}, u32[]{:S(2)}) collective-permute-start(bf16[16,6144]{1,0:T(8,128)(2,1)} %refs_0_.2), channel_id=1, source_target_pairs={{0,4},{1,5},{2,0},{3,1},{4,6},{5,7},{6,2},{7,3},{8,12},{9,13},{10,... | collective-permute-start | bytes 589832 | tf_op jit(solution)/shard_map/ppermute | solution.py:193
  9.2 12.2 %collective-permute-start.8 = (bf16[16,6144]{1,0:T(8,128)(2,1)S(1)}, bf16[16,6144]{1,0:T(8,128)(2,1)S(1)}, u32[]{:S(2)}, u32[]{:S(2)}) collective-permute-start(bf16[16,6144]{1,0:T(8,128)(2,1)S(1)} %collective-permute-done.7.refs_1_), channel_id=1, source_target_pairs={{0,4},{1,5},{2,0},{3,1},{4,6},{5,7},{6,2},{7,3},{8,12},{9,13},{10,... | collective-permute-start | bytes 589832 | tf_op jit(solution)/shard_map/ppermute | solution.py:193
  13.4 4.6 %collective-permute-start.30 = (bf16[16,1536]{1,0:T(8,128)(2,1)S(1)}, bf16[16,1536]{1,0:T(8,128)(2,1)S(1)}, u32[]{:S(2)}, u32[]{:S(2)}) collective-permute-start(bf16[16,1536]{1,0:T(8,128)(2,1)S(1)} %get-tuple-element.38), channel_id=1, source_target_pairs={{0,8},{8,0},{16,24},{24,16},{1,9},{9,1},{17,25},{25,17},{2,10},{10... | collective-permute-start | bytes 147464 | tf_op jit(solution)/shard_map/ppermute | solution.py:199
  14.9 4.4 %collective-permute-start.31 = (bf16[16,1536]{1,0:T(8,128)(2,1)S(1)}, bf16[16,1536]{1,0:T(8,128)(2,1)S(1)}, u32[]{:S(2)}, u32[]{:S(2)}) collective-permute-start(bf16[16,1536]{1,0:T(8,128)(2,1)S(1)} %get-tuple-element.40), channel_id=1, source_target_pairs={{0,16},{8,24},{16,0},{24,8},{1,17},{9,25},{17,1},{25,9},{2,18},{10... | collective-permute-start | bytes 147464 | tf_op jit(solution)/shard_map/ppermute | solution.py:199
  16.5 5.0 %collective-permute-start.32 = (bf16[16,1536]{1,0:T(8,128)(2,1)S(1)}, bf16[16,1536]{1,0:T(8,128)(2,1)S(1)}, u32[]{:S(2)}, u32[]{:S(2)}) collective-permute-start(bf16[16,1536]{1,0:T(8,128)(2,1)S(1)} %get-tuple-element.39), channel_id=1, source_target_pairs={{0,24},{8,16},{16,8},{24,0},{1,25},{9,17},{17,9},{25,1},{2,26},{10... | collective-permute-start | bytes 147464 | tf_op jit(solution)/shard_map/ppermute | solution.py:199
  16.9 7.5 %collective-permute-start.10 = (bf16[16,6144]{1,0:T(8,128)(2,1)}, bf16[16,6144]{1,0:T(8,128)(2,1)S(1)}, u32[]{:S(2)}, u32[]{:S(2)}) collective-permute-start(bf16[16,6144]{1,0:T(8,128)(2,1)} %refs_0_.2), channel_id=1, source_target_pairs={{0,1},{1,0},{2,3},{3,2},{4,5},{5,4},{6,7},{7,6},{8,9},{9,8},{10,11... | collective-permute-start | bytes 589832 | tf_op jit(solution)/shard_map/ppermute | solution.py:196
  17.9 12.2 %collective-permute-start = (bf16[16,6144]{1,0:T(8,128)(2,1)}, bf16[16,6144]{1,0:T(8,128)(2,1)S(1)}, u32[]{:S(2)}, u32[]{:S(2)}) collective-permute-start(bf16[16,6144]{1,0:T(8,128)(2,1)} %refs_0_.3), channel_id=1, source_target_pairs={{0,4},{1,5},{2,0},{3,1},{4,6},{5,7},{6,2},{7,3},{8,12},{9,13},{10,... | collective-permute-start | bytes 589832 | tf_op jit(solution)/shard_map/ppermute | solution.py:193
  19.4 10.8 %collective-permute-start.1 = (bf16[16,6144]{1,0:T(8,128)(2,1)}, bf16[16,6144]{1,0:T(8,128)(2,1)S(1)}, u32[]{:S(2)}, u32[]{:S(2)}) collective-permute-start(bf16[16,6144]{1,0:T(8,128)(2,1)} %refs_0_.3), channel_id=1, source_target_pairs={{0,6},{1,7},{2,4},{3,5},{4,2},{5,3},{6,0},{7,1},{8,14},{9,15},{10,... | collective-permute-start | bytes 589832 | tf_op jit(solution)/shard_map/ppermute | solution.py:193
  21.5 23.7 %collective-permute-start.2 = (bf16[16,6144]{1,0:T(8,128)(2,1)}, bf16[16,6144]{1,0:T(8,128)(2,1)S(1)}, u32[]{:S(2)}, u32[]{:S(2)}) collective-permute-start(bf16[16,6144]{1,0:T(8,128)(2,1)} %refs_0_.3), channel_id=1, source_target_pairs={{0,2},{1,3},{2,6},{3,7},{4,0},{5,1},{6,4},{7,5},{8,10},{9,11},{10,... | collective-permute-start | bytes 589832 | tf_op jit(solution)/shard_map/ppermute | solution.py:193
  21.5 23.7 %collective-permute-start.9 = (bf16[16,6144]{1,0:T(8,128)(2,1)S(1)}, bf16[16,6144]{1,0:T(8,128)(2,1)S(1)}, u32[]{:S(2)}, u32[]{:S(2)}) collective-permute-start(bf16[16,6144]{1,0:T(8,128)(2,1)S(1)} %collective-permute-done.8.refs_2_), channel_id=1, source_target_pairs={{0,4},{1,5},{2,0},{3,1},{4,6},{5,7},{6,2},{7,3},{8,12},{9,13},{10,... | collective-permute-start | bytes 589832 | tf_op jit(solution)/shard_map/ppermute | solution.py:193
  24.4 30.8 %collective-permute-start.3 = (bf16[16,6144]{1,0:T(8,128)(2,1)}, bf16[16,6144]{1,0:T(8,128)(2,1)S(1)}, u32[]{:S(2)}, u32[]{:S(2)}) collective-permute-start(bf16[16,6144]{1,0:T(8,128)(2,1)} %refs_0_.3), channel_id=1, source_target_pairs={{0,1},{1,0},{2,3},{3,2},{4,5},{5,4},{6,7},{7,6},{8,9},{9,8},{10,11... | collective-permute-start | bytes 589832 | tf_op jit(solution)/shard_map/ppermute | solution.py:196
  30.1 20.2 %copy-start = (bf16[16,6144]{1,0:T(8,128)(2,1)S(1)}, bf16[16,6144]{1,0:T(8,128)(2,1)}, u32[]{:S(2)}) copy-start(bf16[16,6144]{1,0:T(8,128)(2,1)} %refs_0_.2) | copy-start | bytes 589828
  30.1 20.2 %copy-start.2 = (f32[6144]{0:T(1024)S(1)}, f32[6144]{0:T(1024)}, u32[]{:S(2)}) copy-start(f32[6144]{0:T(1024)} %param.6) | copy-start | bytes 73732
  30.1 28.0 %collective-permute-start.33 = (bf16[4,16,1536]{2,1,0:T(8,128)(2,1)S(1)}, bf16[4,16,1536]{2,1,0:T(8,128)(2,1)S(1)}, u32[]{:S(2)}, u32[]{:S(2)}) collective-permute-start(bf16[4,16,1536]{2,1,0:T(8,128)(2,1)S(1)} %get-tuple-element.36), channel_id=1, source_target_pairs={{0,4},{1,5},{2,0},{3,1},{4,6},{5,7},{6,2},{7,3},{8,12},{9,13},{10,... | collective-permute-start | bytes 589832 | tf_op jit(solution)/shard_map/ppermute | solution.py:193
  30.2 28.0 %collective-permute-start.11 = (bf16[16,6144]{1,0:T(8,128)(2,1)S(1)}, bf16[16,6144]{1,0:T(8,128)(2,1)S(1)}, u32[]{:S(2)}, u32[]{:S(2)}) collective-permute-start(bf16[16,6144]{1,0:T(8,128)(2,1)S(1)} %collective-permute-done.7.refs_1_), channel_id=1, source_target_pairs={{0,1},{1,0},{2,3},{3,2},{4,5},{5,4},{6,7},{7,6},{8,9},{9,8},{10,11... | collective-permute-start | bytes 589832 | tf_op jit(solution)/shard_map/ppermute | solution.py:196
  45.1 13.1 %collective-permute-start.12 = (bf16[16,6144]{1,0:T(8,128)(2,1)S(1)}, bf16[16,6144]{1,0:T(8,128)(2,1)S(1)}, u32[]{:S(2)}, u32[]{:S(2)}) collective-permute-start(bf16[16,6144]{1,0:T(8,128)(2,1)S(1)} %collective-permute-done.8.refs_2_), channel_id=1, source_target_pairs={{0,1},{1,0},{2,3},{3,2},{4,5},{5,4},{6,7},{7,6},{8,9},{9,8},{10,11... | collective-permute-start | bytes 589832 | tf_op jit(solution)/shard_map/ppermute | solution.py:196
  45.2 13.6 %collective-permute-start.13 = (bf16[16,6144]{1,0:T(8,128)(2,1)S(1)}, bf16[16,6144]{1,0:T(8,128)(2,1)S(1)}, u32[]{:S(2)}, u32[]{:S(2)}) collective-permute-start(bf16[16,6144]{1,0:T(8,128)(2,1)S(1)} %collective-permute-done.9.refs_3_), channel_id=1, source_target_pairs={{0,1},{1,0},{2,3},{3,2},{4,5},{5,4},{6,7},{7,6},{8,9},{9,8},{10,11... | collective-permute-start | bytes 589832 | tf_op jit(solution)/shard_map/ppermute | solution.py:196
  55.2 9.7 %collective-permute-start.34 = (bf16[4,16,1536]{2,1,0:T(8,128)(2,1)S(1)}, bf16[4,16,1536]{2,1,0:T(8,128)(2,1)S(1)}, u32[]{:S(2)}, u32[]{:S(2)}) collective-permute-start(bf16[4,16,1536]{2,1,0:T(8,128)(2,1)S(1)} %get-tuple-element.36), channel_id=1, source_target_pairs={{0,6},{1,7},{2,4},{3,5},{4,2},{5,3},{6,0},{7,1},{8,14},{9,15},{10,... | collective-permute-start | bytes 589832 | tf_op jit(solution)/shard_map/ppermute | solution.py:193
  58.1 12.0 %collective-permute-start.35 = (bf16[4,16,1536]{2,1,0:T(8,128)(2,1)S(1)}, bf16[4,16,1536]{2,1,0:T(8,128)(2,1)S(1)}, u32[]{:S(2)}, u32[]{:S(2)}) collective-permute-start(bf16[4,16,1536]{2,1,0:T(8,128)(2,1)S(1)} %get-tuple-element.36), channel_id=1, source_target_pairs={{0,2},{1,3},{2,6},{3,7},{4,0},{5,1},{6,4},{7,5},{8,10},{9,11},{10,... | collective-permute-start | bytes 589832 | tf_op jit(solution)/shard_map/ppermute | solution.py:193
  58.1 12.0 %collective-permute-start.4 = (bf16[16,6144]{1,0:T(8,128)(2,1)S(1)}, bf16[16,6144]{1,0:T(8,128)(2,1)S(1)}, u32[]{:S(2)}, u32[]{:S(2)}) collective-permute-start(bf16[16,6144]{1,0:T(8,128)(2,1)S(1)} %collective-permute-done.refs_1_), channel_id=1, source_target_pairs={{0,1},{1,0},{2,3},{3,2},{4,5},{5,4},{6,7},{7,6},{8,9},{9,8},{10,11... | collective-permute-start | bytes 589832 | tf_op jit(solution)/shard_map/ppermute | solution.py:196
  58.2 12.4 %collective-permute-start.5 = (bf16[16,6144]{1,0:T(8,128)(2,1)S(1)}, bf16[16,6144]{1,0:T(8,128)(2,1)S(1)}, u32[]{:S(2)}, u32[]{:S(2)}) collective-permute-start(bf16[16,6144]{1,0:T(8,128)(2,1)S(1)} %collective-permute-done.1.refs_2_), channel_id=1, source_target_pairs={{0,1},{1,0},{2,3},{3,2},{4,5},{5,4},{6,7},{7,6},{8,9},{9,8},{10,11... | collective-permute-start | bytes 589832 | tf_op jit(solution)/shard_map/ppermute | solution.py:196
  58.7 12.0 %collective-permute-start.6 = (bf16[16,6144]{1,0:T(8,128)(2,1)S(1)}, bf16[16,6144]{1,0:T(8,128)(2,1)S(1)}, u32[]{:S(2)}, u32[]{:S(2)}) collective-permute-start(bf16[16,6144]{1,0:T(8,128)(2,1)S(1)} %collective-permute-done.2.refs_3_), channel_id=1, source_target_pairs={{0,1},{1,0},{2,3},{3,2},{4,5},{5,4},{6,7},{7,6},{8,9},{9,8},{10,11... | collective-permute-start | bytes 589832 | tf_op jit(solution)/shard_map/ppermute | solution.py:196
  58.8 11.9 %copy-start.1 = (bf16[16,6144]{1,0:T(8,128)(2,1)S(1)}, bf16[16,6144]{1,0:T(8,128)(2,1)}, u32[]{:S(2)}) copy-start(bf16[16,6144]{1,0:T(8,128)(2,1)} %refs_0_.3) | copy-start | bytes 589828
  64.9 25.2 %collective-permute-start.36 = (bf16[4,16,1536]{2,1,0:T(8,128)(2,1)S(1)}, bf16[4,16,1536]{2,1,0:T(8,128)(2,1)S(1)}, u32[]{:S(2)}, u32[]{:S(2)}) collective-permute-start(bf16[4,16,1536]{2,1,0:T(8,128)(2,1)S(1)} %get-tuple-element.36), channel_id=1, source_target_pairs={{0,1},{1,0},{2,3},{3,2},{4,5},{5,4},{6,7},{7,6},{8,9},{9,8},{10,11... | collective-permute-start | bytes 589832 | tf_op jit(solution)/shard_map/ppermute | solution.py:196
  70.1 21.5 %collective-permute-start.37 = (bf16[4,16,1536]{2,1,0:T(8,128)(2,1)S(1)}, bf16[4,16,1536]{2,1,0:T(8,128)(2,1)S(1)}, u32[]{:S(2)}, u32[]{:S(2)}) collective-permute-start(bf16[4,16,1536]{2,1,0:T(8,128)(2,1)S(1)} %collective-permute-done.33), channel_id=1, source_target_pairs={{0,1},{1,0},{2,3},{3,2},{4,5},{5,4},{6,7},{7,6},{8,9},{9,8},{10,11... | collective-permute-start | bytes 589832 | tf_op jit(solution)/shard_map/ppermute | solution.py:196
  70.1 22.3 %collective-permute-start.38 = (bf16[4,16,1536]{2,1,0:T(8,128)(2,1)S(1)}, bf16[4,16,1536]{2,1,0:T(8,128)(2,1)S(1)}, u32[]{:S(2)}, u32[]{:S(2)}) collective-permute-start(bf16[4,16,1536]{2,1,0:T(8,128)(2,1)S(1)} %collective-permute-done.34), channel_id=1, source_target_pairs={{0,1},{1,0},{2,3},{3,2},{4,5},{5,4},{6,7},{7,6},{8,9},{9,8},{10,11... | collective-permute-start | bytes 589832 | tf_op jit(solution)/shard_map/ppermute | solution.py:196
  70.6 21.8 %collective-permute-start.39 = (bf16[4,16,1536]{2,1,0:T(8,128)(2,1)S(1)}, bf16[4,16,1536]{2,1,0:T(8,128)(2,1)S(1)}, u32[]{:S(2)}, u32[]{:S(2)}) collective-permute-start(bf16[4,16,1536]{2,1,0:T(8,128)(2,1)S(1)} %collective-permute-done.35), channel_id=1, source_target_pairs={{0,1},{1,0},{2,3},{3,2},{4,5},{5,4},{6,7},{7,6},{8,9},{9,8},{10,11... | collective-permute-start | bytes 589832 | tf_op jit(solution)/shard_map/ppermute | solution.py:196
  90.0 3.9 %collective-permute-start.40 = (f32[1,6144]{1,0:T(1,128)S(1)}, f32[1,6144]{1,0:T(1,128)S(1)}, u32[]{:S(2)}, u32[]{:S(2)}) collective-permute-start(f32[1,6144]{1,0:T(1,128)S(1)} %get-tuple-element.23), channel_id=1, source_target_pairs={{0,4},{1,5},{2,0},{3,1},{4,6},{5,7},{6,2},{7,3},{8,12},{9,13},{10,... | collective-permute-start | bytes 73736 | tf_op jit(solution)/shard_map/ppermute | solution.py:193
  90.1 5.9 %collective-permute-start.41 = (f32[1,6144]{1,0:T(1,128)S(1)}, f32[1,6144]{1,0:T(1,128)S(1)}, u32[]{:S(2)}, u32[]{:S(2)}) collective-permute-start(f32[1,6144]{1,0:T(1,128)S(1)} %get-tuple-element.23), channel_id=1, source_target_pairs={{0,6},{1,7},{2,4},{3,5},{4,2},{5,3},{6,0},{7,1},{8,14},{9,15},{10,... | collective-permute-start | bytes 73736 | tf_op jit(solution)/shard_map/ppermute | solution.py:193
  91.6 4.8 %collective-permute-start.42 = (f32[1,6144]{1,0:T(1,128)S(1)}, f32[1,6144]{1,0:T(1,128)S(1)}, u32[]{:S(2)}, u32[]{:S(2)}) collective-permute-start(f32[1,6144]{1,0:T(1,128)S(1)} %get-tuple-element.23), channel_id=1, source_target_pairs={{0,2},{1,3},{2,6},{3,7},{4,0},{5,1},{6,4},{7,5},{8,10},{9,11},{10,... | collective-permute-start | bytes 73736 | tf_op jit(solution)/shard_map/ppermute | solution.py:193
  96.4 3.9 %collective-permute-start.43 = (f32[1,6144]{1,0:T(1,128)S(1)}, f32[1,6144]{1,0:T(1,128)S(1)}, u32[]{:S(2)}, u32[]{:S(2)}) collective-permute-start(f32[1,6144]{1,0:T(1,128)S(1)} %add_add_fusion), channel_id=1, source_target_pairs={{0,8},{8,0},{16,24},{24,16},{1,9},{9,1},{17,25},{25,17},{2,10},{10... | collective-permute-start | bytes 73736 | tf_op jit(solution)/shard_map/ppermute | solution.py:199
  100.3 3.9 %collective-permute-start.44 = (f32[1,6144]{1,0:T(1,128)S(1)}, f32[1,6144]{1,0:T(1,128)S(1)}, u32[]{:S(2)}, u32[]{:S(2)}) collective-permute-start(f32[1,6144]{1,0:T(1,128)S(1)} %add.57), channel_id=1, source_target_pairs={{0,16},{8,24},{16,0},{24,8},{1,17},{9,25},{17,1},{25,9},{2,18},{10... | collective-permute-start | bytes 73736 | tf_op jit(solution)/shard_map/ppermute | solution.py:199
  102.0 29.4 %collective-permute-start.24 = (bf16[128,2048]{1,0:T(8,128)(2,1)S(1)}, bf16[128,2048]{1,0:T(8,128)(2,1)S(1)}, u32[]{:S(2)}, u32[]{:S(2)}) collective-permute-start(bf16[128,2048]{1,0:T(8,128)(2,1)S(1)} %shard_map.85.pre), channel_id=1, source_target_pairs={{0,8},{8,0},{16,24},{24,16},{1,9},{9,1},{17,25},{25,17},{2,10},{10... | collective-permute-start | bytes 1572872 | tf_op jit(solution)/shard_map/ppermute | solution.py:199
  103.5 27.2 %collective-permute-start.28 = (bf16[128,2048]{1,0:T(8,128)(2,1)S(1)}, bf16[128,2048]{1,0:T(8,128)(2,1)S(1)}, u32[]{:S(2)}, u32[]{:S(2)}) collective-permute-start(bf16[128,2048]{1,0:T(8,128)(2,1)S(1)} %get-tuple-element.22), channel_id=1, source_target_pairs={{0,16},{8,24},{16,0},{24,8},{1,17},{9,25},{17,1},{25,9},{2,18},{10... | collective-permute-start | bytes 1572872 | tf_op jit(solution)/shard_map/ppermute | solution.py:199
  104.2 3.5 %collective-permute-start.45 = (f32[1,6144]{1,0:T(1,128)S(1)}, f32[1,6144]{1,0:T(1,128)S(1)}, u32[]{:S(2)}, u32[]{:S(2)}) collective-permute-start(f32[1,6144]{1,0:T(1,128)S(1)} %add.58), channel_id=1, source_target_pairs={{0,1},{1,0},{2,3},{3,2},{4,5},{5,4},{6,7},{7,6},{8,9},{9,8},{10,11... | collective-permute-start | bytes 73736 | tf_op jit(solution)/shard_map/ppermute | solution.py:196
  104.4 16.2 %collective-permute-start.18 = (bf16[64,1536]{1,0:T(8,128)(2,1)S(1)}, bf16[64,1536]{1,0:T(8,128)(2,1)S(1)}, u32[]{:S(2)}, u32[]{:S(2)}) collective-permute-start(bf16[64,1536]{1,0:T(8,128)(2,1)S(1)} %get-tuple-element.31), channel_id=1, source_target_pairs={{0,8},{8,0},{16,24},{24,16},{1,9},{9,1},{17,25},{25,17},{2,10},{10... | collective-permute-start | bytes 589832 | tf_op jit(solution)/shard_map/ppermute | solution.py:199
  106.2 17.7 %collective-permute-start.20 = (bf16[64,1536]{1,0:T(8,128)(2,1)S(1)}, bf16[64,1536]{1,0:T(8,128)(2,1)S(1)}, u32[]{:S(2)}, u32[]{:S(2)}) collective-permute-start(bf16[64,1536]{1,0:T(8,128)(2,1)S(1)} %get-tuple-element.30), channel_id=1, source_target_pairs={{0,16},{8,24},{16,0},{24,8},{1,17},{9,25},{17,1},{25,9},{2,18},{10... | collective-permute-start | bytes 589832 | tf_op jit(solution)/shard_map/ppermute | solution.py:199
  107.7 16.2 %collective-permute-start.22 = (bf16[64,1536]{1,0:T(8,128)(2,1)S(1)}, bf16[64,1536]{1,0:T(8,128)(2,1)S(1)}, u32[]{:S(2)}, u32[]{:S(2)}) collective-permute-start(bf16[64,1536]{1,0:T(8,128)(2,1)S(1)} %get-tuple-element.29), channel_id=1, source_target_pairs={{0,24},{8,16},{16,8},{24,0},{1,25},{9,17},{17,9},{25,1},{2,26},{10... | collective-permute-start | bytes 589832 | tf_op jit(solution)/shard_map/ppermute | solution.py:199
  120.6 3.8 %collective-permute-start.19 = (bf16[64,1536]{1,0:T(8,128)(2,1)S(1)}, bf16[64,1536]{1,0:T(8,128)(2,1)S(1)}, u32[]{:S(2)}, u32[]{:S(2)}) collective-permute-start(bf16[64,1536]{1,0:T(8,128)(2,1)S(1)} %collective-permute-done.18), channel_id=1, source_target_pairs={{0,1},{1,0},{2,3},{3,2},{4,5},{5,4},{6,7},{7,6},{8,9},{9,8},{10,11... | collective-permute-start | bytes 589832 | tf_op jit(solution)/shard_map/ppermute | solution.py:196
  123.9 2.6 %collective-permute-start.14 = (bf16[64,6144]{1,0:T(8,128)(2,1)S(1)}, bf16[64,6144]{1,0:T(8,128)(2,1)S(1)}, u32[]{:S(2)}, u32[]{:S(2)}) collective-permute-start(bf16[64,6144]{1,0:T(8,128)(2,1)S(1)} %get-tuple-element.19), channel_id=1, source_target_pairs={{0,1},{1,0},{2,3},{3,2},{4,5},{5,4},{6,7},{7,6},{8,9},{9,8},{10,11... | collective-permute-start | bytes 2359304 | tf_op jit(solution)/shard_map/ppermute | solution.py:196
  123.9 2.6 %collective-permute-start.21 = (bf16[64,1536]{1,0:T(8,128)(2,1)S(1)}, bf16[64,1536]{1,0:T(8,128)(2,1)S(1)}, u32[]{:S(2)}, u32[]{:S(2)}) collective-permute-start(bf16[64,1536]{1,0:T(8,128)(2,1)S(1)} %collective-permute-done.20), channel_id=1, source_target_pairs={{0,1},{1,0},{2,3},{3,2},{4,5},{5,4},{6,7},{7,6},{8,9},{9,8},{10,11... | collective-permute-start | bytes 589832 | tf_op jit(solution)/shard_map/ppermute | solution.py:196
  124.4 4.4 %collective-permute-start.23 = (bf16[64,1536]{1,0:T(8,128)(2,1)S(1)}, bf16[64,1536]{1,0:T(8,128)(2,1)S(1)}, u32[]{:S(2)}, u32[]{:S(2)}) collective-permute-start(bf16[64,1536]{1,0:T(8,128)(2,1)S(1)} %collective-permute-done.22), channel_id=1, source_target_pairs={{0,1},{1,0},{2,3},{3,2},{4,5},{5,4},{6,7},{7,6},{8,9},{9,8},{10,11... | collective-permute-start | bytes 589832 | tf_op jit(solution)/shard_map/ppermute | solution.py:196
  126.8 17.2 %collective-permute-start.15 = (bf16[16,6144]{1,0:T(8,128)(2,1)S(1)}, bf16[16,6144]{1,0:T(8,128)(2,1)S(1)}, u32[]{:S(2)}, u32[]{:S(2)}) collective-permute-start(bf16[16,6144]{1,0:T(8,128)(2,1)S(1)} %get-tuple-element.32), channel_id=1, source_target_pairs={{0,2},{1,3},{2,6},{3,7},{4,0},{5,1},{6,4},{7,5},{8,10},{9,11},{10,... | collective-permute-start | bytes 589832 | tf_op jit(solution)/shard_map/ppermute | solution.py:193
  126.8 17.9 %collective-permute-start.16 = (bf16[16,6144]{1,0:T(8,128)(2,1)S(1)}, bf16[16,6144]{1,0:T(8,128)(2,1)S(1)}, u32[]{:S(2)}, u32[]{:S(2)}) collective-permute-start(bf16[16,6144]{1,0:T(8,128)(2,1)S(1)} %get-tuple-element.34), channel_id=1, source_target_pairs={{0,6},{1,7},{2,4},{3,5},{4,2},{5,3},{6,0},{7,1},{8,14},{9,15},{10,... | collective-permute-start | bytes 589832 | tf_op jit(solution)/shard_map/ppermute | solution.py:193
  128.8 16.0 %collective-permute-start.17 = (bf16[16,6144]{1,0:T(8,128)(2,1)S(1)}, bf16[16,6144]{1,0:T(8,128)(2,1)S(1)}, u32[]{:S(2)}, u32[]{:S(2)}) collective-permute-start(bf16[16,6144]{1,0:T(8,128)(2,1)S(1)} %get-tuple-element.33), channel_id=1, source_target_pairs={{0,4},{1,5},{2,0},{3,1},{4,6},{5,7},{6,2},{7,3},{8,12},{9,13},{10,... | collective-permute-start | bytes 589832 | tf_op jit(solution)/shard_map/ppermute | solution.py:193
  130.8 15.2 %collective-permute-start.27 = (bf16[128,2048]{1,0:T(8,128)(2,1)S(1)}, bf16[128,2048]{1,0:T(8,128)(2,1)S(1)}, u32[]{:S(2)}, u32[]{:S(2)}) collective-permute-start(bf16[128,2048]{1,0:T(8,128)(2,1)S(1)} %get-tuple-element.22), channel_id=1, source_target_pairs={{0,8},{8,0},{16,24},{24,16},{1,9},{9,1},{17,25},{25,17},{2,10},{10... | collective-permute-start | bytes 1572872 | tf_op jit(solution)/shard_map/ppermute | solution.py:199
  131.4 29.3 %collective-permute-start.25 = (bf16[128,2048]{1,0:T(8,128)(2,1)S(1)}, bf16[128,2048]{1,0:T(8,128)(2,1)S(1)}, u32[]{:S(2)}, u32[]{:S(2)}) collective-permute-start(bf16[128,2048]{1,0:T(8,128)(2,1)S(1)} %shard_map.85.pre), channel_id=1, source_target_pairs={{0,16},{8,24},{16,0},{24,8},{1,17},{9,25},{17,1},{25,9},{2,18},{10... | collective-permute-start | bytes 1572872 | tf_op jit(solution)/shard_map/ppermute | solution.py:199
  144.0 11.3 %collective-permute-start.29 = (bf16[128,2048]{1,0:T(8,128)(2,1)S(1)}, bf16[128,2048]{1,0:T(8,128)(2,1)S(1)}, u32[]{:S(2)}, u32[]{:S(2)}) collective-permute-start(bf16[128,2048]{1,0:T(8,128)(2,1)S(1)} %collective-permute-done.28), channel_id=1, source_target_pairs={{0,8},{8,0},{16,24},{24,16},{1,9},{9,1},{17,25},{25,17},{2,10},{10... | collective-permute-start | bytes 1572872 | tf_op jit(solution)/shard_map/ppermute | solution.py:199
  144.8 15.9 %collective-permute-start.26 = (bf16[128,2048]{1,0:T(8,128)(2,1)S(1)}, bf16[128,2048]{1,0:T(8,128)(2,1)S(1)}, u32[]{:S(2)}, u32[]{:S(2)}) collective-permute-start(bf16[128,2048]{1,0:T(8,128)(2,1)S(1)} %collective-permute-done.24), channel_id=1, source_target_pairs={{0,16},{8,24},{16,0},{24,8},{1,17},{9,25},{17,1},{25,9},{2,18},{10... | collective-permute-start | bytes 1572872 | tf_op jit(solution)/shard_map/ppermute | solution.py:199

commit v5 on v4

--- a/solution.py
+++ b/solution.py
@@ -86,11 +86,17 @@
         copy.wait()
 
 
-def norm_kernel(tokens, gain, weight, x_hat, scale, held, sems):
+def norm_kernel(tokens, gain, weight, x_hat, scale, held, sems, rows, row, row_sems):
     copies = fetch_copies(0, weight, held, sems)
-    for copy in copies:
+    small = [
+        pltpu.make_async_copy(tokens, rows, row_sems.at[0]),
+        pltpu.make_async_copy(gain, row, row_sems.at[1]),
+    ]
+    for copy in small + copies:
         copy.start()
-    _, x_hat[...], inv_std = normalise(tokens[...], gain[...])
+    for copy in small:
+        copy.wait()
+    _, x_hat[...], inv_std = normalise(rows[...], row[...])
     scale[...] = jnp.broadcast_to(inv_std, scale.shape)
     for copy in copies:
         copy.wait()
@@ -225,9 +231,14 @@
     fetch_sems = [pltpu.SemaphoreType.DMA((4,))]
     x_hat, scale, up_first = pl.pallas_call(
         norm_kernel,
-        in_specs=[WHOLE] * 2 + [STAYS],
+        in_specs=[STAYS] * 3,
         out_specs=[WHOLE] * 3,
-        scratch_shapes=fetch_sems,
+        scratch_shapes=[
+            *fetch_sems,
+            pltpu.VMEM(tokens.shape, jnp.bfloat16),
+            pltpu.VMEM(gain_row.shape, jnp.float32),
+            pltpu.SemaphoreType.DMA((2,)),
+        ],
         compiler_params=pltpu.CompilerParams(vmem_limit_bytes=5 * 2**20),
         out_shape=[
             jax.ShapeDtypeStruct((rows, width), jnp.float32),
@@ -235,7 +246,7 @@
             pltpu.VMEM((first, units), jnp.bfloat16),
         ],
         name="ln",
-    )(tokens, gain_row, up_weight)
+    )(*(pltpu.with_memory_space_constraint(a, pltpu.HBM) for a in (tokens, gain_row)), up_weight)
     inv_std = scale[:, :1]
     up_second = pl.pallas_call(
         functools.partial(fetch_kernel, first),
@@ -266,7 +277,7 @@
     flops = 2 * group * width * units
     part_rows = chunk(units, 512, 128)
     hidden, slope, normed_all, down_first = call(
-        functools.partial(preact_kernel, chunk(units, 512, 128), len(token_pieces)),
+        functools.partial(preact_kernel, chunk(units, 1024, 128), len(token_pieces)),
         (*token_pieces, gain_row, up_first, up_second, down_weight),
         (half_units, float_units, half_width, pltpu.VMEM((part_rows, width), jnp.bfloat16)),
         5,
@@ -289,7 +300,7 @@
         1,
     )
     mine, other, gain_grad = call(
-        functools.partial(normgrad_kernel, chunk(first, 1536, 128)),
+        functools.partial(normgrad_kernel, chunk(first, 3072, 128)),
         (pre_grad, up_first, up_second, normed_all, gain_row),
         (core_width, core_width, ((1, width), jnp.float32)),
         5,
@@ -310,7 +321,8 @@
     for part in received:
         gain_grad = gain_grad + part
     for bit in range((n_dp - 1).bit_length()):
-        gain_grad = gain_grad + replica(gain_grad, 1 << bit)
+        part = replica(gain_grad, 1 << bit)
+        gain_grad = gain_grad + part
     gain_grad = gain_grad + across(gain_grad)
     gain_grad = gain_grad.reshape(width) * factor
 

time: 166 us -> 166 us (level)
  transfers between devices with their start and end apart: 46 -> 46, of which waited for: 18 -> 18; matrix products, arithmetic and copies ran while one was open for 5% -> 5% of each run, Pallas kernels for 21% -> 20%
where the time goes in v5:
time: 166 us; the launch traced here: 165 us
  waiting for transfers between devices  78.1 us (47%)
  starting transfers between devices  38.3 us (23%)
  Pallas kernels  33.8 us (20%)
  matrix products  10.7 us (6%)
  other arithmetic  2.33 us (1%)
    ppermute x15, waiting for transfers between devices, along_ring(): return lax.ppermute(array, 'mp', ring_perm(n_mp, shift))  46.8 us
    ppermute x14, waiting for transfers between devices, replica(): return lax.ppermute(array, 'dp', swap_perm(n_dp, mask))  29.3 us
    pallas_call x3, Pallas kernels, call(): pl.pallas_call(kernel, in_specs=[WHOLE] * (len(operands) - stay) + [STAYS...  24.4 us
    ppermute x15, starting transfers between devices, along_ring(): return lax.ppermute(array, 'mp', ring_perm(n_mp, shift))  21.6 us
    ppermute x14, starting transfers between devices, replica(): return lax.ppermute(array, 'dp', swap_perm(n_dp, mask))  14 us
    dot_general x2, matrix products, contract(): lax.dot_general(a, b, (dims, ((), ())), preferred_element_type=jnp.float32)  10.7 us
    pallas_call x1, Pallas kernels, layer(): pl.pallas_call(norm_kernel, in_specs=[STAYS] * 3, out_specs=[WHOLE] * 3,...  4.81 us
    pallas_call x1, Pallas kernels, layer(): pl.pallas_call(functools.partial(fetch_kernel, first), in_specs=[STAYS],...  4.68 us
  transfers between devices with their start and end apart: 46, of which 18 were waited for; matrix products, arithmetic and copies ran while one was open for 5% of the time, Pallas kernels for 20%

profile of v5, /device:TPU:0, one launch (start us, length us, event | category | flops | bytes accessed | tf_op | source)
XLA Modules:
  0.0 165.5 jit_solution(18339761426350923531)
XLA Ops:
  0.6 4.1 %collective-permute-start.7 = (bf16[16,6144]{1,0:T(8,128)(2,1)}, bf16[16,6144]{1,0:T(8,128)(2,1)S(1)}, u32[]{:S(2)}, u32[]{:S(2)}) collective-permute-start(bf16[16,6144]{1,0:T(8,128)(2,1)} %refs_0_.2), channel_id=1, source_target_pairs={{0,4},{1,5},{2,0},{3,1},{4,6},{5,7},{6,2},{7,3},{8,12},{9,13},{10,... | collective-permute-start | bytes 589832 | tf_op jit(solution)/shard_map/ppermute | solution.py:199
  4.7 4.5 %collective-permute-done.7.refs_1_ = bf16[16,6144]{1,0:T(8,128)(2,1)S(1)} collective-permute-done((bf16[16,6144]{1,0:T(8,128)(2,1)}, bf16[16,6144]{1,0:T(8,128)(2,1)S(1)}, u32[]{:S(2)}, u32[]{:S(2)}) %collective-permute-start.7) | collective-permute-done | bytes 196640 | tf_op jit(solution)/shard_map/ppermute | solution.py:199
  9.2 3.3 %collective-permute-start.8 = (bf16[16,6144]{1,0:T(8,128)(2,1)S(1)}, bf16[16,6144]{1,0:T(8,128)(2,1)S(1)}, u32[]{:S(2)}, u32[]{:S(2)}) collective-permute-start(bf16[16,6144]{1,0:T(8,128)(2,1)S(1)} %collective-permute-done.7.refs_1_), channel_id=1, source_target_pairs={{0,4},{1,5},{2,0},{3,1},{4,6},{5,7},{6,2},{7,3},{8,12},{9,13},{10,... | collective-permute-start | bytes 589832 | tf_op jit(solution)/shard_map/ppermute | solution.py:199
  12.5 0.9 dynamic-slice_bitcast_fusion
  13.4 1.6 collective-permute-start.30
  14.9 1.5 collective-permute-start.31
  16.5 0.5 collective-permute-start.32
  16.9 1.0 collective-permute-done.30
  17.9 0.7 collective-permute-start
  18.6 0.7 collective-permute-done.31
  19.4 1.3 collective-permute-start.1
  20.7 0.7 collective-permute-done.32
  21.5 2.9 %collective-permute-start.9 = (bf16[16,6144]{1,0:T(8,128)(2,1)S(1)}, bf16[16,6144]{1,0:T(8,128)(2,1)S(1)}, u32[]{:S(2)}, u32[]{:S(2)}) collective-permute-start(bf16[16,6144]{1,0:T(8,128)(2,1)S(1)} %collective-permute-done.8.refs_2_), channel_id=1, source_target_pairs={{0,4},{1,5},{2,0},{3,1},{4,6},{5,7},{6,2},{7,3},{8,12},{9,13},{10,... | collective-permute-start | bytes 589832 | tf_op jit(solution)/shard_map/ppermute | solution.py:199
  24.4 0.1 collective-permute-start.3
  24.5 5.6 %collective-permute-done.refs_1_ = bf16[16,6144]{1,0:T(8,128)(2,1)S(1)} collective-permute-done((bf16[16,6144]{1,0:T(8,128)(2,1)}, bf16[16,6144]{1,0:T(8,128)(2,1)S(1)}, u32[]{:S(2)}, u32[]{:S(2)}) %collective-permute-start) | collective-permute-done | bytes 196640 | tf_op jit(solution)/shard_map/ppermute | solution.py:199
  30.2 15.0 %collective-permute-done.2.refs_3_ = bf16[16,6144]{1,0:T(8,128)(2,1)S(1)} collective-permute-done((bf16[16,6144]{1,0:T(8,128)(2,1)}, bf16[16,6144]{1,0:T(8,128)(2,1)S(1)}, u32[]{:S(2)}, u32[]{:S(2)}) %collective-permute-start.2) | collective-permute-done | bytes 196640 | tf_op jit(solution)/shard_map/ppermute | solution.py:199
  45.2 0.5 collective-permute-start.13
  45.7 4.7 %fetch.1.refs_10_.second = bf16[3072,2048]{1,0:T(8,128)(2,1)S(1)} custom-call(bf16[6144,2048]{1,0:T(8,128)(2,1)} %weight.3), custom_call_target="tpu_custom_call" | custom-call | tf_op jit(solution)/shard_map/fetch/pallas_call | solution.py:251
  50.4 4.8 %ln.1 = (f32[16,6144]{1,0:T(8,128)S(1)}, f32[16,128]{1,0:T(8,128)S(1)}, bf16[3072,2048]{1,0:T(8,128)(2,1)S(1)}) custom-call(bf16[16,6144]{1,0:T(8,128)(2,1)} %refs_0_.2, f32[1,6144]{1,0:T(1,128)} %bitcast.33, bf16[6144,2048]{1,0:T(8,128)(2,1)} %weight.3), custom_call_target="tpu_custom_call" | custom-call | tf_op jit(solution)/shard_map/ln/pallas_call | solution.py:232
  55.2 0.1 slice_reduce_fusion
  55.3 2.9 %collective-permute-start.34 = (bf16[4,16,1536]{2,1,0:T(8,128)(2,1)S(1)}, bf16[4,16,1536]{2,1,0:T(8,128)(2,1)S(1)}, u32[]{:S(2)}, u32[]{:S(2)}) collective-permute-start(bf16[4,16,1536]{2,1,0:T(8,128)(2,1)S(1)} %get-tuple-element.36), channel_id=1, source_target_pairs={{0,6},{1,7},{2,4},{3,5},{4,2},{5,3},{6,0},{7,1},{8,14},{9,15},{10,... | collective-permute-start | bytes 589832 | tf_op jit(solution)/shard_map/ppermute | solution.py:199
  58.3 0.1 collective-permute-start.4
  58.3 0.5 collective-permute-start.5
  58.8 0.1 collective-permute-start.6
  58.9 5.7 %shard_map.84 = (bf16[128,2048]{1,0:T(8,128)(2,1)S(1)}, f32[128,2048]{1,0:T(8,128)S(1)}, bf16[128,6144]{1,0:T(8,128)(2,1)S(1)}, bf16[512,6144]{1,0:T(8,128)(2,1)S(1)}) custom-call(bf16[16,6144]{1,0:T(8,128)(2,1)S(1)} %copy-done, bf16[16,6144]{1,0:T(8,128)(2,1)S(1)} %collective-permute-done.7.refs_1_, bf16[16,6144]{1,0:T(8,128)(2,1)S(1)} %collective-permute-done.8.refs_2_, ...), custom_call_target="tpu_custom_call" | custom-call | flops 3221225472 | bytes 51929088 | tf_op jit(solution)/shard_map/pallas_call | solution.py:59
  64.7 0.3 collective-permute-done.34
  65.0 0.2 collective-permute-start.36
  65.2 5.0 %collective-permute-done.35 = bf16[4,16,1536]{2,1,0:T(8,128)(2,1)S(1)} collective-permute-done((bf16[4,16,1536]{2,1,0:T(8,128)(2,1)S(1)}, bf16[4,16,1536]{2,1,0:T(8,128)(2,1)S(1)}, u32[]{:S(2)}, u32[]{:S(2)}) %collective-permute-start.35) | collective-permute-done | bytes 196640 | tf_op jit(solution)/shard_map/ppermute | solution.py:199
  70.2 0.5 collective-permute-start.38
  70.8 11.7 %shard_map.85.pre = bf16[128,2048]{1,0:T(8,128)(2,1)S(1)} custom-call(bf16[16,6144]{1,0:T(8,128)(2,1)S(1)} %copy-done.1, bf16[16,6144]{1,0:T(8,128)(2,1)S(1)} %collective-permute-done.refs_1_, bf16[16,6144]{1,0:T(8,128)(2,1)S(1)} %collective-permute-done.1.refs_2_, bf16[16,6144]{1,0:T(8,128)(2,1)S(1)} %collective-permute-done.2.refs_3_, ...), custom_call_target="tpu_custom_call" | custom-call | flops 3221225472 | bytes 34078720 | tf_op jit(solution)/shard_map/pallas_call | solution.py:59
  82.5 6.9 %shard_map.86 = (bf16[64,6144]{1,0:T(8,128)(2,1)S(1)}, bf16[64,6144]{1,0:T(8,128)(2,1)S(1)}, f32[1,6144]{1,0:T(1,128)S(1)}) custom-call(bf16[128,2048]{1,0:T(8,128)(2,1)S(1)} %shard_map.85.pre, bf16[3072,2048]{1,0:T(8,128)(2,1)S(1)} %get-tuple-element.14.refs_9_.first, bf16[3072,2048]{1,0:T(8,128)(2,1)S(1)} %fetch.1.refs_10_.second, ...), custom_call_target="tpu_custom_call" | custom-call | flops 3221225472 | bytes 27287552 | tf_op jit(solution)/shard_map/pallas_call | solution.py:59
  89.5 1.5 collective-permute-start.41
  91.0 0.8 collective-permute-start.42
  91.8 0.1 maximum_bitcast_fusion.1
  91.9 1.4 collective-permute-done.40
  93.3 2.1 %collective-permute-done.41 = f32[1,6144]{1,0:T(1,128)S(1)} collective-permute-done((f32[1,6144]{1,0:T(1,128)S(1)}, f32[1,6144]{1,0:T(1,128)S(1)}, u32[]{:S(2)}, u32[]{:S(2)}) %collective-permute-start.41) | collective-permute-done | bytes 24608 | tf_op jit(solution)/shard_map/ppermute | solution.py:199
  95.4 0.3 collective-permute-done.42
  95.8 1.6 collective-permute-start.43
  97.3 0.1 pad_maximum_fusion
  97.5 2.2 %collective-permute-done.43 = f32[1,6144]{1,0:T(1,128)S(1)} collective-permute-done((f32[1,6144]{1,0:T(1,128)S(1)}, f32[1,6144]{1,0:T(1,128)S(1)}, u32[]{:S(2)}, u32[]{:S(2)}) %collective-permute-start.43) | collective-permute-done | bytes 24608 | tf_op jit(solution)/shard_map/ppermute | solution.py:205
  99.7 1.6 collective-permute-start.44
  101.4 1.6 collective-permute-start.24
  102.9 0.5 collective-permute-start.28
  103.5 0.2 collective-permute-done.44
  103.6 0.1 collective-permute-start.45
  103.8 1.8 %collective-permute-start.18 = (bf16[64,1536]{1,0:T(8,128)(2,1)S(1)}, bf16[64,1536]{1,0:T(8,128)(2,1)S(1)}, u32[]{:S(2)}, u32[]{:S(2)}) collective-permute-start(bf16[64,1536]{1,0:T(8,128)(2,1)S(1)} %get-tuple-element.31), channel_id=1, source_target_pairs={{0,8},{8,0},{16,24},{24,16},{1,9},{9,1},{17,25},{25,17},{2,10},{10... | collective-permute-start | bytes 589832 | tf_op jit(solution)/shard_map/ppermute | solution.py:205
  105.6 1.5 collective-permute-start.20
  107.1 0.5 collective-permute-start.22
  107.6 0.6 add_multiply_fusion
  108.3 11.7 %collective-permute-done.18 = bf16[64,1536]{1,0:T(8,128)(2,1)S(1)} collective-permute-done((bf16[64,1536]{1,0:T(8,128)(2,1)S(1)}, bf16[64,1536]{1,0:T(8,128)(2,1)S(1)}, u32[]{:S(2)}, u32[]{:S(2)}) %collective-permute-start.18) | collective-permute-done | bytes 196640 | tf_op jit(solution)/shard_map/ppermute | solution.py:205
  120.0 3.3 %collective-permute-done.20 = bf16[64,1536]{1,0:T(8,128)(2,1)S(1)} collective-permute-done((bf16[64,1536]{1,0:T(8,128)(2,1)S(1)}, bf16[64,1536]{1,0:T(8,128)(2,1)S(1)}, u32[]{:S(2)}, u32[]{:S(2)}) %collective-permute-start.20) | collective-permute-done | bytes 196640 | tf_op jit(solution)/shard_map/ppermute | solution.py:205
  123.3 0.5 collective-permute-start.21
  123.9 1.9 %collective-permute-done.21 = bf16[64,1536]{1,0:T(8,128)(2,1)S(1)} collective-permute-done((bf16[64,1536]{1,0:T(8,128)(2,1)S(1)}, bf16[64,1536]{1,0:T(8,128)(2,1)S(1)}, u32[]{:S(2)}, u32[]{:S(2)}) %collective-permute-start.21) | collective-permute-done | bytes 196640 | tf_op jit(solution)/shard_map/ppermute | solution.py:202
  125.9 0.2 convert_add_fusion
  126.3 1.9 %collective-permute-start.16 = (bf16[16,6144]{1,0:T(8,128)(2,1)S(1)}, bf16[16,6144]{1,0:T(8,128)(2,1)S(1)}, u32[]{:S(2)}, u32[]{:S(2)}) collective-permute-start(bf16[16,6144]{1,0:T(8,128)(2,1)S(1)} %get-tuple-element.34), channel_id=1, source_target_pairs={{0,6},{1,7},{2,4},{3,5},{4,2},{5,3},{6,0},{7,1},{8,14},{9,15},{10,... | collective-permute-start | bytes 589832 | tf_op jit(solution)/shard_map/ppermute | solution.py:199
  128.2 1.9 %collective-permute-start.17 = (bf16[16,6144]{1,0:T(8,128)(2,1)S(1)}, bf16[16,6144]{1,0:T(8,128)(2,1)S(1)}, u32[]{:S(2)}, u32[]{:S(2)}) collective-permute-start(bf16[16,6144]{1,0:T(8,128)(2,1)S(1)} %get-tuple-element.33), channel_id=1, source_target_pairs={{0,4},{1,5},{2,0},{3,1},{4,6},{5,7},{6,2},{7,3},{8,12},{9,13},{10,... | collective-permute-start | bytes 589832 | tf_op jit(solution)/shard_map/ppermute | solution.py:199
  130.2 0.6 collective-permute-start.27
  130.8 12.6 %collective-permute-done.15 = bf16[16,6144]{1,0:T(8,128)(2,1)S(1)} collective-permute-done((bf16[16,6144]{1,0:T(8,128)(2,1)S(1)}, bf16[16,6144]{1,0:T(8,128)(2,1)S(1)}, u32[]{:S(2)}, u32[]{:S(2)}) %collective-permute-start.15) | collective-permute-done | bytes 196640 | tf_op jit(solution)/shard_map/ppermute | solution.py:199
  143.4 0.8 collective-permute-start.29
  144.2 0.3 fusion.21
  144.5 0.8 multiply_convert_fusion.2
  145.3 9.4 %collective-permute-done.29 = bf16[128,2048]{1,0:T(8,128)(2,1)S(1)} collective-permute-done((bf16[128,2048]{1,0:T(8,128)(2,1)S(1)}, bf16[128,2048]{1,0:T(8,128)(2,1)S(1)}, u32[]{:S(2)}, u32[]{:S(2)}) %collective-permute-start.29) | collective-permute-done | bytes 524320 | tf_op jit(solution)/shard_map/ppermute | solution.py:205
  154.7 5.4 %multiply_convert_fusion = bf16[2048,1536]{1,0:T(8,128)(2,1)} fusion(bf16[512,1536]{1,0:T(8,128)(2,1)S(1)} %bitcast.36, bf16[128,2048]{1,0:T(8,128)(2,1)S(1)} %collective-permute-done.29, bf16[128,2048]{1,0:T(8,128)(2,1)S(1)} %collective-permute-done.28, bf16[128,2048]{1,0:T(8,128)(2,1)S(1)} %collective-permute-done.27, ...), kind=kOutput, calls=%fused_computation | convolution fusion | flops 3235905536 | bytes 9961472 | tf_op jit(solution)/shard_map/dot_general | solution.py:35
  160.1 5.4 %multiply_convert_fusion.1 = bf16[1536,2048]{1,0:T(8,128)(2,1)} fusion(bf16[512,1536]{1,0:T(8,128)(2,1)S(1)} %constant_dynamic-update-slice_fusion, bf16[128,2048]{1,0:T(8,128)(2,1)S(1)} %collective-permute-done.26, bf16[128,2048]{1,0:T(8,128)(2,1)S(1)} %collective-permute-done.25, bf16[128,2048]{1,0:T(8,128)(2,1)S(1)} %collective-permute-done.24, ...), kind=kOutput, calls=%fused_computation.1 | convolution fusion | flops 3235905536 | bytes 9961472 | tf_op jit(solution)/shard_map/dot_general | solution.py:35
  (64 shorter events, 0.8 us)
Async XLA Ops:
  0.6 8.6 %collective-permute-start.7 = (bf16[16,6144]{1,0:T(8,128)(2,1)}, bf16[16,6144]{1,0:T(8,128)(2,1)S(1)}, u32[]{:S(2)}, u32[]{:S(2)}) collective-permute-start(bf16[16,6144]{1,0:T(8,128)(2,1)} %refs_0_.2), channel_id=1, source_target_pairs={{0,4},{1,5},{2,0},{3,1},{4,6},{5,7},{6,2},{7,3},{8,12},{9,13},{10,... | collective-permute-start | bytes 589832 | tf_op jit(solution)/shard_map/ppermute | solution.py:199
  9.2 12.2 %collective-permute-start.8 = (bf16[16,6144]{1,0:T(8,128)(2,1)S(1)}, bf16[16,6144]{1,0:T(8,128)(2,1)S(1)}, u32[]{:S(2)}, u32[]{:S(2)}) collective-permute-start(bf16[16,6144]{1,0:T(8,128)(2,1)S(1)} %collective-permute-done.7.refs_1_), channel_id=1, source_target_pairs={{0,4},{1,5},{2,0},{3,1},{4,6},{5,7},{6,2},{7,3},{8,12},{9,13},{10,... | collective-permute-start | bytes 589832 | tf_op jit(solution)/shard_map/ppermute | solution.py:199
  13.4 4.6 %collective-permute-start.30 = (bf16[16,1536]{1,0:T(8,128)(2,1)S(1)}, bf16[16,1536]{1,0:T(8,128)(2,1)S(1)}, u32[]{:S(2)}, u32[]{:S(2)}) collective-permute-start(bf16[16,1536]{1,0:T(8,128)(2,1)S(1)} %get-tuple-element.38), channel_id=1, source_target_pairs={{0,8},{8,0},{16,24},{24,16},{1,9},{9,1},{17,25},{25,17},{2,10},{10... | collective-permute-start | bytes 147464 | tf_op jit(solution)/shard_map/ppermute | solution.py:205
  14.9 4.4 %collective-permute-start.31 = (bf16[16,1536]{1,0:T(8,128)(2,1)S(1)}, bf16[16,1536]{1,0:T(8,128)(2,1)S(1)}, u32[]{:S(2)}, u32[]{:S(2)}) collective-permute-start(bf16[16,1536]{1,0:T(8,128)(2,1)S(1)} %get-tuple-element.40), channel_id=1, source_target_pairs={{0,16},{8,24},{16,0},{24,8},{1,17},{9,25},{17,1},{25,9},{2,18},{10... | collective-permute-start | bytes 147464 | tf_op jit(solution)/shard_map/ppermute | solution.py:205
  16.5 5.0 %collective-permute-start.32 = (bf16[16,1536]{1,0:T(8,128)(2,1)S(1)}, bf16[16,1536]{1,0:T(8,128)(2,1)S(1)}, u32[]{:S(2)}, u32[]{:S(2)}) collective-permute-start(bf16[16,1536]{1,0:T(8,128)(2,1)S(1)} %get-tuple-element.39), channel_id=1, source_target_pairs={{0,24},{8,16},{16,8},{24,0},{1,25},{9,17},{17,9},{25,1},{2,26},{10... | collective-permute-start | bytes 147464 | tf_op jit(solution)/shard_map/ppermute | solution.py:205
  16.9 7.5 %collective-permute-start.10 = (bf16[16,6144]{1,0:T(8,128)(2,1)}, bf16[16,6144]{1,0:T(8,128)(2,1)S(1)}, u32[]{:S(2)}, u32[]{:S(2)}) collective-permute-start(bf16[16,6144]{1,0:T(8,128)(2,1)} %refs_0_.2), channel_id=1, source_target_pairs={{0,1},{1,0},{2,3},{3,2},{4,5},{5,4},{6,7},{7,6},{8,9},{9,8},{10,11... | collective-permute-start | bytes 589832 | tf_op jit(solution)/shard_map/ppermute | solution.py:202
  17.9 12.2 %collective-permute-start = (bf16[16,6144]{1,0:T(8,128)(2,1)}, bf16[16,6144]{1,0:T(8,128)(2,1)S(1)}, u32[]{:S(2)}, u32[]{:S(2)}) collective-permute-start(bf16[16,6144]{1,0:T(8,128)(2,1)} %refs_0_.3), channel_id=1, source_target_pairs={{0,4},{1,5},{2,0},{3,1},{4,6},{5,7},{6,2},{7,3},{8,12},{9,13},{10,... | collective-permute-start | bytes 589832 | tf_op jit(solution)/shard_map/ppermute | solution.py:199
  19.4 10.8 %collective-permute-start.1 = (bf16[16,6144]{1,0:T(8,128)(2,1)}, bf16[16,6144]{1,0:T(8,128)(2,1)S(1)}, u32[]{:S(2)}, u32[]{:S(2)}) collective-permute-start(bf16[16,6144]{1,0:T(8,128)(2,1)} %refs_0_.3), channel_id=1, source_target_pairs={{0,6},{1,7},{2,4},{3,5},{4,2},{5,3},{6,0},{7,1},{8,14},{9,15},{10,... | collective-permute-start | bytes 589832 | tf_op jit(solution)/shard_map/ppermute | solution.py:199
  21.5 23.7 %collective-permute-start.2 = (bf16[16,6144]{1,0:T(8,128)(2,1)}, bf16[16,6144]{1,0:T(8,128)(2,1)S(1)}, u32[]{:S(2)}, u32[]{:S(2)}) collective-permute-start(bf16[16,6144]{1,0:T(8,128)(2,1)} %refs_0_.3), channel_id=1, source_target_pairs={{0,2},{1,3},{2,6},{3,7},{4,0},{5,1},{6,4},{7,5},{8,10},{9,11},{10,... | collective-permute-start | bytes 589832 | tf_op jit(solution)/shard_map/ppermute | solution.py:199
  21.5 23.7 %collective-permute-start.9 = (bf16[16,6144]{1,0:T(8,128)(2,1)S(1)}, bf16[16,6144]{1,0:T(8,128)(2,1)S(1)}, u32[]{:S(2)}, u32[]{:S(2)}) collective-permute-start(bf16[16,6144]{1,0:T(8,128)(2,1)S(1)} %collective-permute-done.8.refs_2_), channel_id=1, source_target_pairs={{0,4},{1,5},{2,0},{3,1},{4,6},{5,7},{6,2},{7,3},{8,12},{9,13},{10,... | collective-permute-start | bytes 589832 | tf_op jit(solution)/shard_map/ppermute | solution.py:199
  24.4 30.9 %collective-permute-start.3 = (bf16[16,6144]{1,0:T(8,128)(2,1)}, bf16[16,6144]{1,0:T(8,128)(2,1)S(1)}, u32[]{:S(2)}, u32[]{:S(2)}) collective-permute-start(bf16[16,6144]{1,0:T(8,128)(2,1)} %refs_0_.3), channel_id=1, source_target_pairs={{0,1},{1,0},{2,3},{3,2},{4,5},{5,4},{6,7},{7,6},{8,9},{9,8},{10,11... | collective-permute-start | bytes 589832 | tf_op jit(solution)/shard_map/ppermute | solution.py:202
  30.1 28.1 %collective-permute-start.33 = (bf16[4,16,1536]{2,1,0:T(8,128)(2,1)S(1)}, bf16[4,16,1536]{2,1,0:T(8,128)(2,1)S(1)}, u32[]{:S(2)}, u32[]{:S(2)}) collective-permute-start(bf16[4,16,1536]{2,1,0:T(8,128)(2,1)S(1)} %get-tuple-element.36), channel_id=1, source_target_pairs={{0,4},{1,5},{2,0},{3,1},{4,6},{5,7},{6,2},{7,3},{8,12},{9,13},{10,... | collective-permute-start | bytes 589832 | tf_op jit(solution)/shard_map/ppermute | solution.py:199
  30.1 28.1 %collective-permute-start.11 = (bf16[16,6144]{1,0:T(8,128)(2,1)S(1)}, bf16[16,6144]{1,0:T(8,128)(2,1)S(1)}, u32[]{:S(2)}, u32[]{:S(2)}) collective-permute-start(bf16[16,6144]{1,0:T(8,128)(2,1)S(1)} %collective-permute-done.7.refs_1_), channel_id=1, source_target_pairs={{0,1},{1,0},{2,3},{3,2},{4,5},{5,4},{6,7},{7,6},{8,9},{9,8},{10,11... | collective-permute-start | bytes 589832 | tf_op jit(solution)/shard_map/ppermute | solution.py:202
  45.1 13.2 %collective-permute-start.12 = (bf16[16,6144]{1,0:T(8,128)(2,1)S(1)}, bf16[16,6144]{1,0:T(8,128)(2,1)S(1)}, u32[]{:S(2)}, u32[]{:S(2)}) collective-permute-start(bf16[16,6144]{1,0:T(8,128)(2,1)S(1)} %collective-permute-done.8.refs_2_), channel_id=1, source_target_pairs={{0,1},{1,0},{2,3},{3,2},{4,5},{5,4},{6,7},{7,6},{8,9},{9,8},{10,11... | collective-permute-start | bytes 589832 | tf_op jit(solution)/shard_map/ppermute | solution.py:202
  45.2 13.7 %collective-permute-start.13 = (bf16[16,6144]{1,0:T(8,128)(2,1)S(1)}, bf16[16,6144]{1,0:T(8,128)(2,1)S(1)}, u32[]{:S(2)}, u32[]{:S(2)}) collective-permute-start(bf16[16,6144]{1,0:T(8,128)(2,1)S(1)} %collective-permute-done.9.refs_3_), channel_id=1, source_target_pairs={{0,1},{1,0},{2,3},{3,2},{4,5},{5,4},{6,7},{7,6},{8,9},{9,8},{10,11... | collective-permute-start | bytes 589832 | tf_op jit(solution)/shard_map/ppermute | solution.py:202
  50.4 8.6 %copy-start = (bf16[16,6144]{1,0:T(8,128)(2,1)S(1)}, bf16[16,6144]{1,0:T(8,128)(2,1)}, u32[]{:S(2)}) copy-start(bf16[16,6144]{1,0:T(8,128)(2,1)} %refs_0_.2) | copy-start | bytes 589828
  50.4 8.6 %copy-start.2 = (f32[6144]{0:T(1024)S(1)}, f32[6144]{0:T(1024)}, u32[]{:S(2)}) copy-start(f32[6144]{0:T(1024)} %param.6) | copy-start | bytes 73732
  55.3 9.7 %collective-permute-start.34 = (bf16[4,16,1536]{2,1,0:T(8,128)(2,1)S(1)}, bf16[4,16,1536]{2,1,0:T(8,128)(2,1)S(1)}, u32[]{:S(2)}, u32[]{:S(2)}) collective-permute-start(bf16[4,16,1536]{2,1,0:T(8,128)(2,1)S(1)} %get-tuple-element.36), channel_id=1, source_target_pairs={{0,6},{1,7},{2,4},{3,5},{4,2},{5,3},{6,0},{7,1},{8,14},{9,15},{10,... | collective-permute-start | bytes 589832 | tf_op jit(solution)/shard_map/ppermute | solution.py:199
  58.2 12.0 %collective-permute-start.35 = (bf16[4,16,1536]{2,1,0:T(8,128)(2,1)S(1)}, bf16[4,16,1536]{2,1,0:T(8,128)(2,1)S(1)}, u32[]{:S(2)}, u32[]{:S(2)}) collective-permute-start(bf16[4,16,1536]{2,1,0:T(8,128)(2,1)S(1)} %get-tuple-element.36), channel_id=1, source_target_pairs={{0,2},{1,3},{2,6},{3,7},{4,0},{5,1},{6,4},{7,5},{8,10},{9,11},{10,... | collective-permute-start | bytes 589832 | tf_op jit(solution)/shard_map/ppermute | solution.py:199
  58.3 12.0 %collective-permute-start.4 = (bf16[16,6144]{1,0:T(8,128)(2,1)S(1)}, bf16[16,6144]{1,0:T(8,128)(2,1)S(1)}, u32[]{:S(2)}, u32[]{:S(2)}) collective-permute-start(bf16[16,6144]{1,0:T(8,128)(2,1)S(1)} %collective-permute-done.refs_1_), channel_id=1, source_target_pairs={{0,1},{1,0},{2,3},{3,2},{4,5},{5,4},{6,7},{7,6},{8,9},{9,8},{10,11... | collective-permute-start | bytes 589832 | tf_op jit(solution)/shard_map/ppermute | solution.py:202
  58.3 12.4 %collective-permute-start.5 = (bf16[16,6144]{1,0:T(8,128)(2,1)S(1)}, bf16[16,6144]{1,0:T(8,128)(2,1)S(1)}, u32[]{:S(2)}, u32[]{:S(2)}) collective-permute-start(bf16[16,6144]{1,0:T(8,128)(2,1)S(1)} %collective-permute-done.1.refs_2_), channel_id=1, source_target_pairs={{0,1},{1,0},{2,3},{3,2},{4,5},{5,4},{6,7},{7,6},{8,9},{9,8},{10,11... | collective-permute-start | bytes 589832 | tf_op jit(solution)/shard_map/ppermute | solution.py:202
  58.8 12.0 %collective-permute-start.6 = (bf16[16,6144]{1,0:T(8,128)(2,1)S(1)}, bf16[16,6144]{1,0:T(8,128)(2,1)S(1)}, u32[]{:S(2)}, u32[]{:S(2)}) collective-permute-start(bf16[16,6144]{1,0:T(8,128)(2,1)S(1)} %collective-permute-done.2.refs_3_), channel_id=1, source_target_pairs={{0,1},{1,0},{2,3},{3,2},{4,5},{5,4},{6,7},{7,6},{8,9},{9,8},{10,11... | collective-permute-start | bytes 589832 | tf_op jit(solution)/shard_map/ppermute | solution.py:202
  58.9 11.9 %copy-start.1 = (bf16[16,6144]{1,0:T(8,128)(2,1)S(1)}, bf16[16,6144]{1,0:T(8,128)(2,1)}, u32[]{:S(2)}) copy-start(bf16[16,6144]{1,0:T(8,128)(2,1)} %refs_0_.3) | copy-start | bytes 589828
  65.0 24.5 %collective-permute-start.36 = (bf16[4,16,1536]{2,1,0:T(8,128)(2,1)S(1)}, bf16[4,16,1536]{2,1,0:T(8,128)(2,1)S(1)}, u32[]{:S(2)}, u32[]{:S(2)}) collective-permute-start(bf16[4,16,1536]{2,1,0:T(8,128)(2,1)S(1)} %get-tuple-element.36), channel_id=1, source_target_pairs={{0,1},{1,0},{2,3},{3,2},{4,5},{5,4},{6,7},{7,6},{8,9},{9,8},{10,11... | collective-permute-start | bytes 589832 | tf_op jit(solution)/shard_map/ppermute | solution.py:202
  70.2 20.8 %collective-permute-start.37 = (bf16[4,16,1536]{2,1,0:T(8,128)(2,1)S(1)}, bf16[4,16,1536]{2,1,0:T(8,128)(2,1)S(1)}, u32[]{:S(2)}, u32[]{:S(2)}) collective-permute-start(bf16[4,16,1536]{2,1,0:T(8,128)(2,1)S(1)} %collective-permute-done.33), channel_id=1, source_target_pairs={{0,1},{1,0},{2,3},{3,2},{4,5},{5,4},{6,7},{7,6},{8,9},{9,8},{10,11... | collective-permute-start | bytes 589832 | tf_op jit(solution)/shard_map/ppermute | solution.py:202
  70.2 21.6 %collective-permute-start.38 = (bf16[4,16,1536]{2,1,0:T(8,128)(2,1)S(1)}, bf16[4,16,1536]{2,1,0:T(8,128)(2,1)S(1)}, u32[]{:S(2)}, u32[]{:S(2)}) collective-permute-start(bf16[4,16,1536]{2,1,0:T(8,128)(2,1)S(1)} %collective-permute-done.34), channel_id=1, source_target_pairs={{0,1},{1,0},{2,3},{3,2},{4,5},{5,4},{6,7},{7,6},{8,9},{9,8},{10,11... | collective-permute-start | bytes 589832 | tf_op jit(solution)/shard_map/ppermute | solution.py:202
  70.7 21.1 %collective-permute-start.39 = (bf16[4,16,1536]{2,1,0:T(8,128)(2,1)S(1)}, bf16[4,16,1536]{2,1,0:T(8,128)(2,1)S(1)}, u32[]{:S(2)}, u32[]{:S(2)}) collective-permute-start(bf16[4,16,1536]{2,1,0:T(8,128)(2,1)S(1)} %collective-permute-done.35), channel_id=1, source_target_pairs={{0,1},{1,0},{2,3},{3,2},{4,5},{5,4},{6,7},{7,6},{8,9},{9,8},{10,11... | collective-permute-start | bytes 589832 | tf_op jit(solution)/shard_map/ppermute | solution.py:202
  89.5 3.9 %collective-permute-start.40 = (f32[1,6144]{1,0:T(1,128)S(1)}, f32[1,6144]{1,0:T(1,128)S(1)}, u32[]{:S(2)}, u32[]{:S(2)}) collective-permute-start(f32[1,6144]{1,0:T(1,128)S(1)} %get-tuple-element.23), channel_id=1, source_target_pairs={{0,4},{1,5},{2,0},{3,1},{4,6},{5,7},{6,2},{7,3},{8,12},{9,13},{10,... | collective-permute-start | bytes 73736 | tf_op jit(solution)/shard_map/ppermute | solution.py:199
  89.5 5.9 %collective-permute-start.41 = (f32[1,6144]{1,0:T(1,128)S(1)}, f32[1,6144]{1,0:T(1,128)S(1)}, u32[]{:S(2)}, u32[]{:S(2)}) collective-permute-start(f32[1,6144]{1,0:T(1,128)S(1)} %get-tuple-element.23), channel_id=1, source_target_pairs={{0,6},{1,7},{2,4},{3,5},{4,2},{5,3},{6,0},{7,1},{8,14},{9,15},{10,... | collective-permute-start | bytes 73736 | tf_op jit(solution)/shard_map/ppermute | solution.py:199
  91.0 4.8 %collective-permute-start.42 = (f32[1,6144]{1,0:T(1,128)S(1)}, f32[1,6144]{1,0:T(1,128)S(1)}, u32[]{:S(2)}, u32[]{:S(2)}) collective-permute-start(f32[1,6144]{1,0:T(1,128)S(1)} %get-tuple-element.23), channel_id=1, source_target_pairs={{0,2},{1,3},{2,6},{3,7},{4,0},{5,1},{6,4},{7,5},{8,10},{9,11},{10,... | collective-permute-start | bytes 73736 | tf_op jit(solution)/shard_map/ppermute | solution.py:199
  95.8 3.9 %collective-permute-start.43 = (f32[1,6144]{1,0:T(1,128)S(1)}, f32[1,6144]{1,0:T(1,128)S(1)}, u32[]{:S(2)}, u32[]{:S(2)}) collective-permute-start(f32[1,6144]{1,0:T(1,128)S(1)} %add_add_fusion), channel_id=1, source_target_pairs={{0,8},{8,0},{16,24},{24,16},{1,9},{9,1},{17,25},{25,17},{2,10},{10... | collective-permute-start | bytes 73736 | tf_op jit(solution)/shard_map/ppermute | solution.py:205
  99.7 3.9 %collective-permute-start.44 = (f32[1,6144]{1,0:T(1,128)S(1)}, f32[1,6144]{1,0:T(1,128)S(1)}, u32[]{:S(2)}, u32[]{:S(2)}) collective-permute-start(f32[1,6144]{1,0:T(1,128)S(1)} %add.57), channel_id=1, source_target_pairs={{0,16},{8,24},{16,0},{24,8},{1,17},{9,25},{17,1},{25,9},{2,18},{10... | collective-permute-start | bytes 73736 | tf_op jit(solution)/shard_map/ppermute | solution.py:205
  101.4 29.4 %collective-permute-start.24 = (bf16[128,2048]{1,0:T(8,128)(2,1)S(1)}, bf16[128,2048]{1,0:T(8,128)(2,1)S(1)}, u32[]{:S(2)}, u32[]{:S(2)}) collective-permute-start(bf16[128,2048]{1,0:T(8,128)(2,1)S(1)} %shard_map.85.pre), channel_id=1, source_target_pairs={{0,8},{8,0},{16,24},{24,16},{1,9},{9,1},{17,25},{25,17},{2,10},{10... | collective-permute-start | bytes 1572872 | tf_op jit(solution)/shard_map/ppermute | solution.py:205
  102.9 27.2 %collective-permute-start.28 = (bf16[128,2048]{1,0:T(8,128)(2,1)S(1)}, bf16[128,2048]{1,0:T(8,128)(2,1)S(1)}, u32[]{:S(2)}, u32[]{:S(2)}) collective-permute-start(bf16[128,2048]{1,0:T(8,128)(2,1)S(1)} %get-tuple-element.22), channel_id=1, source_target_pairs={{0,16},{8,24},{16,0},{24,8},{1,17},{9,25},{17,1},{25,9},{2,18},{10... | collective-permute-start | bytes 1572872 | tf_op jit(solution)/shard_map/ppermute | solution.py:205
  103.6 3.5 %collective-permute-start.45 = (f32[1,6144]{1,0:T(1,128)S(1)}, f32[1,6144]{1,0:T(1,128)S(1)}, u32[]{:S(2)}, u32[]{:S(2)}) collective-permute-start(f32[1,6144]{1,0:T(1,128)S(1)} %add.58), channel_id=1, source_target_pairs={{0,1},{1,0},{2,3},{3,2},{4,5},{5,4},{6,7},{7,6},{8,9},{9,8},{10,11... | collective-permute-start | bytes 73736 | tf_op jit(solution)/shard_map/ppermute | solution.py:202
  103.8 16.2 %collective-permute-start.18 = (bf16[64,1536]{1,0:T(8,128)(2,1)S(1)}, bf16[64,1536]{1,0:T(8,128)(2,1)S(1)}, u32[]{:S(2)}, u32[]{:S(2)}) collective-permute-start(bf16[64,1536]{1,0:T(8,128)(2,1)S(1)} %get-tuple-element.31), channel_id=1, source_target_pairs={{0,8},{8,0},{16,24},{24,16},{1,9},{9,1},{17,25},{25,17},{2,10},{10... | collective-permute-start | bytes 589832 | tf_op jit(solution)/shard_map/ppermute | solution.py:205
  105.6 17.7 %collective-permute-start.20 = (bf16[64,1536]{1,0:T(8,128)(2,1)S(1)}, bf16[64,1536]{1,0:T(8,128)(2,1)S(1)}, u32[]{:S(2)}, u32[]{:S(2)}) collective-permute-start(bf16[64,1536]{1,0:T(8,128)(2,1)S(1)} %get-tuple-element.30), channel_id=1, source_target_pairs={{0,16},{8,24},{16,0},{24,8},{1,17},{9,25},{17,1},{25,9},{2,18},{10... | collective-permute-start | bytes 589832 | tf_op jit(solution)/shard_map/ppermute | solution.py:205
  107.1 16.2 %collective-permute-start.22 = (bf16[64,1536]{1,0:T(8,128)(2,1)S(1)}, bf16[64,1536]{1,0:T(8,128)(2,1)S(1)}, u32[]{:S(2)}, u32[]{:S(2)}) collective-permute-start(bf16[64,1536]{1,0:T(8,128)(2,1)S(1)} %get-tuple-element.29), channel_id=1, source_target_pairs={{0,24},{8,16},{16,8},{24,0},{1,25},{9,17},{17,9},{25,1},{2,26},{10... | collective-permute-start | bytes 589832 | tf_op jit(solution)/shard_map/ppermute | solution.py:205
  120.0 3.8 %collective-permute-start.19 = (bf16[64,1536]{1,0:T(8,128)(2,1)S(1)}, bf16[64,1536]{1,0:T(8,128)(2,1)S(1)}, u32[]{:S(2)}, u32[]{:S(2)}) collective-permute-start(bf16[64,1536]{1,0:T(8,128)(2,1)S(1)} %collective-permute-done.18), channel_id=1, source_target_pairs={{0,1},{1,0},{2,3},{3,2},{4,5},{5,4},{6,7},{7,6},{8,9},{9,8},{10,11... | collective-permute-start | bytes 589832 | tf_op jit(solution)/shard_map/ppermute | solution.py:202
  123.3 2.6 %collective-permute-start.14 = (bf16[64,6144]{1,0:T(8,128)(2,1)S(1)}, bf16[64,6144]{1,0:T(8,128)(2,1)S(1)}, u32[]{:S(2)}, u32[]{:S(2)}) collective-permute-start(bf16[64,6144]{1,0:T(8,128)(2,1)S(1)} %get-tuple-element.19), channel_id=1, source_target_pairs={{0,1},{1,0},{2,3},{3,2},{4,5},{5,4},{6,7},{7,6},{8,9},{9,8},{10,11... | collective-permute-start | bytes 2359304 | tf_op jit(solution)/shard_map/ppermute | solution.py:202
  123.3 2.6 %collective-permute-start.21 = (bf16[64,1536]{1,0:T(8,128)(2,1)S(1)}, bf16[64,1536]{1,0:T(8,128)(2,1)S(1)}, u32[]{:S(2)}, u32[]{:S(2)}) collective-permute-start(bf16[64,1536]{1,0:T(8,128)(2,1)S(1)} %collective-permute-done.20), channel_id=1, source_target_pairs={{0,1},{1,0},{2,3},{3,2},{4,5},{5,4},{6,7},{7,6},{8,9},{9,8},{10,11... | collective-permute-start | bytes 589832 | tf_op jit(solution)/shard_map/ppermute | solution.py:202
  123.8 4.4 %collective-permute-start.23 = (bf16[64,1536]{1,0:T(8,128)(2,1)S(1)}, bf16[64,1536]{1,0:T(8,128)(2,1)S(1)}, u32[]{:S(2)}, u32[]{:S(2)}) collective-permute-start(bf16[64,1536]{1,0:T(8,128)(2,1)S(1)} %collective-permute-done.22), channel_id=1, source_target_pairs={{0,1},{1,0},{2,3},{3,2},{4,5},{5,4},{6,7},{7,6},{8,9},{9,8},{10,11... | collective-permute-start | bytes 589832 | tf_op jit(solution)/shard_map/ppermute | solution.py:202
  126.2 17.2 %collective-permute-start.15 = (bf16[16,6144]{1,0:T(8,128)(2,1)S(1)}, bf16[16,6144]{1,0:T(8,128)(2,1)S(1)}, u32[]{:S(2)}, u32[]{:S(2)}) collective-permute-start(bf16[16,6144]{1,0:T(8,128)(2,1)S(1)} %get-tuple-element.32), channel_id=1, source_target_pairs={{0,2},{1,3},{2,6},{3,7},{4,0},{5,1},{6,4},{7,5},{8,10},{9,11},{10,... | collective-permute-start | bytes 589832 | tf_op jit(solution)/shard_map/ppermute | solution.py:199
  126.3 17.9 %collective-permute-start.16 = (bf16[16,6144]{1,0:T(8,128)(2,1)S(1)}, bf16[16,6144]{1,0:T(8,128)(2,1)S(1)}, u32[]{:S(2)}, u32[]{:S(2)}) collective-permute-start(bf16[16,6144]{1,0:T(8,128)(2,1)S(1)} %get-tuple-element.34), channel_id=1, source_target_pairs={{0,6},{1,7},{2,4},{3,5},{4,2},{5,3},{6,0},{7,1},{8,14},{9,15},{10,... | collective-permute-start | bytes 589832 | tf_op jit(solution)/shard_map/ppermute | solution.py:199
  128.2 16.0 %collective-permute-start.17 = (bf16[16,6144]{1,0:T(8,128)(2,1)S(1)}, bf16[16,6144]{1,0:T(8,128)(2,1)S(1)}, u32[]{:S(2)}, u32[]{:S(2)}) collective-permute-start(bf16[16,6144]{1,0:T(8,128)(2,1)S(1)} %get-tuple-element.33), channel_id=1, source_target_pairs={{0,4},{1,5},{2,0},{3,1},{4,6},{5,7},{6,2},{7,3},{8,12},{9,13},{10,... | collective-permute-start | bytes 589832 | tf_op jit(solution)/shard_map/ppermute | solution.py:199
  130.2 15.2 %collective-permute-start.27 = (bf16[128,2048]{1,0:T(8,128)(2,1)S(1)}, bf16[128,2048]{1,0:T(8,128)(2,1)S(1)}, u32[]{:S(2)}, u32[]{:S(2)}) collective-permute-start(bf16[128,2048]{1,0:T(8,128)(2,1)S(1)} %get-tuple-element.22), channel_id=1, source_target_pairs={{0,8},{8,0},{16,24},{24,16},{1,9},{9,1},{17,25},{25,17},{2,10},{10... | collective-permute-start | bytes 1572872 | tf_op jit(solution)/shard_map/ppermute | solution.py:205
  130.8 29.3 %collective-permute-start.25 = (bf16[128,2048]{1,0:T(8,128)(2,1)S(1)}, bf16[128,2048]{1,0:T(8,128)(2,1)S(1)}, u32[]{:S(2)}, u32[]{:S(2)}) collective-permute-start(bf16[128,2048]{1,0:T(8,128)(2,1)S(1)} %shard_map.85.pre), channel_id=1, source_target_pairs={{0,16},{8,24},{16,0},{24,8},{1,17},{9,25},{17,1},{25,9},{2,18},{10... | collective-permute-start | bytes 1572872 | tf_op jit(solution)/shard_map/ppermute | solution.py:205
  143.4 11.3 %collective-permute-start.29 = (bf16[128,2048]{1,0:T(8,128)(2,1)S(1)}, bf16[128,2048]{1,0:T(8,128)(2,1)S(1)}, u32[]{:S(2)}, u32[]{:S(2)}) collective-permute-start(bf16[128,2048]{1,0:T(8,128)(2,1)S(1)} %collective-permute-done.28), channel_id=1, source_target_pairs={{0,8},{8,0},{16,24},{24,16},{1,9},{9,1},{17,25},{25,17},{2,10},{10... | collective-permute-start | bytes 1572872 | tf_op jit(solution)/shard_map/ppermute | solution.py:205
  144.2 15.9 %collective-permute-start.26 = (bf16[128,2048]{1,0:T(8,128)(2,1)S(1)}, bf16[128,2048]{1,0:T(8,128)(2,1)S(1)}, u32[]{:S(2)}, u32[]{:S(2)}) collective-permute-start(bf16[128,2048]{1,0:T(8,128)(2,1)S(1)} %collective-permute-done.24), channel_id=1, source_target_pairs={{0,16},{8,24},{16,0},{24,8},{1,17},{9,25},{17,1},{25,9},{2,18},{10... | collective-permute-start | bytes 1572872 | tf_op jit(solution)/shard_map/ppermute | solution.py:205
